TPU v7x, 256 devices: a whole 4x4x8 slice. The times are simulated.
256 devices in a mesh: dp: 64 (over x, z, core), rep: 4 (over y).
Axes of the slice: x: 4, y: 4, z: 8, core: 2. Of those that a mesh axis runs over, the one named last changes fastest.
Arguments:
- tokens: bfloat16 [524288, 1280], P(('dp', 'rep')), may hold values from -24 to 24
- sketch_map: bfloat16 [524288, 128], P(('dp', 'rep')), may hold values from -0.125 to 0.125
- test_matrix: bfloat16 [4, 8192, 128], P('rep'), may hold values from -0.03125 to 0.03125
Outputs:
- basis: float32 [1280, 128], P('dp')
- factor: float32 [128, 128], replicated
All inputs are finite; a program needn't handle non-finite values.
Results may differ from a plain program's by a relative error of at most 0.0051.
Values may be sent and summed in bfloat16 or wider, within the bound.
No kernel may reach another device: no remote copies, remote signals or barrier semaphores. Data moves between devices by JAX's collectives and lax.ppermute only.
A program may use at most 64 MiB of HBM per device.

v0:
```python
import jax
import jax.numpy as jnp
from jax import lax
from jax.sharding import Mesh
from jax.sharding import PartitionSpec as P

ITERS = 2
DP = ("dp_0", "dp_1", "dp_2")
DP_REP = ("dp_0", "dp_1", "dp_2", "rep")


def sent_to_all(shard, axis):
    copies = jnp.broadcast_to(shard, (lax.axis_size(axis), *shard.shape))
    return lax.all_to_all(copies, axis, split_axis=0, concat_axis=0, tiled=True)


def over_copies(shard, axis):
    everything = sent_to_all(shard, axis)
    return jnp.sum(everything, axis=0)


def joined_along(tiles, dim):
    tiles = jnp.moveaxis(tiles, 0, dim)
    shape = tiles.shape
    return tiles.reshape(*shape[:dim], shape[dim] * shape[dim + 1], *shape[dim + 2 :])


def collect(shard, axis, dim):
    return joined_along(sent_to_all(shard, axis), dim)


def padded_to(lines, length):
    spare = -lines.shape[0] % length
    if not spare:
        return lines
    return jnp.concatenate([lines, jnp.zeros((spare, *lines.shape[1:]), lines.dtype)])


def gathered_by_axis(shard, axes, dim):
    far, near = axes
    tiles = sent_to_all(sent_to_all(shard, far), near)
    return joined_along(tiles.swapaxes(0, 1).reshape(-1, *shard.shape), dim)


def in_blocks(shard, dim, length):
    shape = shard.shape
    tiles = shard.reshape(*shape[:dim], length, shape[dim] // length, *shape[dim + 1 :])
    return jnp.moveaxis(tiles, dim, 0)


def sent_and_summed(shard, axis, dim):
    length = lax.axis_size(axis)
    tiles = lax.all_to_all(in_blocks(shard, dim, length), axis, 0, 0, tiled=True)
    return jnp.sum(tiles, axis=0)


def sum_by_axis(shard, axes, dim):
    far, near = axes
    tiles = in_blocks(shard, dim, lax.axis_size(far))
    nearer = sent_and_summed(tiles, near, dim + 1)
    arrived = lax.all_to_all(nearer, far, split_axis=0, concat_axis=0, tiled=True)
    return arrived.sum(axis=0)


def sum_by_parts(shard, axes):
    lines = shard.reshape(-1, shard.shape[-1])
    padded = padded_to(lines, lax.axis_size(axes[0]) * lax.axis_size(axes[1]))
    whole = gathered_by_axis(sum_by_axis(padded, axes, 0), axes, 0)
    return lax.slice_in_dim(whole, 0, len(lines)).reshape(shard.shape)


def whole_factor(matrix):
    gram = jnp.dot(
        matrix.T, matrix, precision=lax.Precision.HIGHEST, preferred_element_type=jnp.float32
    )
    lower = jnp.linalg.cholesky(gram)
    return (jax.scipy.linalg.solve_triangular(lower, matrix.T, lower=True).T, lower.T)


def body(tokens, sketch_map, test_matrix):
    width = tokens.shape[1]
    strip = width // lax.axis_size(DP)
    total_tokens = tokens.shape[0] * lax.axis_size(DP) * lax.axis_size("rep")
    sketch = lax.dot_general(
        sketch_map, tokens, (((0,), (0,)), ((), ())), preferred_element_type=jnp.float32
    ).astype(jnp.bfloat16)
    merged = lax.all_to_all(sketch, DP, split_axis=1, concat_axis=0, tiled=True)
    local_start = lax.dot_general(
        merged, test_matrix[0], (((0,), (0,)), ((), ())), preferred_element_type=jnp.float32
    )
    start = over_copies(local_start, "rep")
    gathered = collect(start, DP, 0)
    current, factor = whole_factor(gathered)
    for step in range(ITERS):
        rounded = current.astype(jnp.bfloat16)
        projected = jnp.dot(tokens, rounded, preferred_element_type=jnp.float32).astype(
            jnp.bfloat16
        )
        local_sum = lax.dot_general(
            tokens, projected, (((0,), (0,)), ((), ())), preferred_element_type=jnp.float32
        )
        summed = sum_by_parts(local_sum, (("dp_0", "dp_1"), ("dp_2", "rep")))
        current, factor = whole_factor(summed / total_tokens)
    owned = lax.dynamic_slice_in_dim(current, lax.axis_index(DP) * strip, strip, 0)
    return (owned, factor)


def solution(mesh):
    finer = Mesh(mesh.devices.reshape(4, 8, 2, mesh.shape["rep"]), ("dp_0", "dp_1", "dp_2", "rep"))
    return jax.shard_map(
        body,
        mesh=finer,
        in_specs=(P(DP_REP, None), P(DP_REP, None), P("rep", None, None)),
        out_specs=(P(DP, None), P()),
        check_vma=False,
    )
```

profile of v0, /device:TPU:1, one launch (start us, length us, event | category | flops | bytes accessed | tf_op | source)
XLA Modules:
  0.0 289.9 jit_solution(1632559802495850959)
XLA Ops:
  0.6 0.0 copy-start
  0.6 3.7 %convolution_convert_fusion.4 = bf16[128,1280]{1,0:T(8,128)(2,1)S(1)} fusion(bf16[2048,128]{1,0:T(8,128)(2,1)} %param.7, bf16[2048,1280]{1,0:T(8,128)(2,1)} %param.6), kind=kOutput, calls=%fused_computation.6 | convolution fusion | flops 671252480 | bytes 6094848 | tf_op jit(solution)/shard_map/dot_general | solution.py:84
  4.3 0.2 copy.88
  4.5 0.1 all_to_all.44
  4.6 27.4 %all_to_all.69 = bf16[128,64,20]{0,2,1:T(8,128)(2,1)S(1)} all-to-all(bf16[128,64,20]{0,2,1:T(8,128)(2,1)S(1)} %all_to_all.44), channel_id=1, replica_groups=mesh['dp_0'=4,'dp_1'=8,'dp_2'=2,'rep'=4] {'dp_0','dp_1','dp_2'}, dimensions={1} | all-to-all | bytes 655360 | tf_op jit(solution)/shard_map/all_to_all | solution.py:87
  32.0 0.1 copy.114
  32.1 0.3 copy.110
  32.4 0.0 copy-done
  32.4 0.5 fusion
  32.9 8.4 %all_to_all.70 = f32[4,20,128]{2,1,0:T(8,128)S(1)} all-to-all(f32[4,20,128]{2,1,0:T(8,128)S(1)} %broadcast_in_dim.19), channel_id=1, replica_groups=mesh['dp_0'=4,'dp_1'=8,'dp_2'=2,'rep'=4] {'rep'}, dimensions={0} | all-to-all | bytes 81920 | tf_op jit(solution)/shard_map/all_to_all | solution.py:14
  41.3 0.1 broadcast_in_dim.20
  41.3 30.9 %all_to_all.71 = f32[64,20,128]{2,1,0:T(8,128)S(1)} all-to-all(f32[64,20,128]{2,1,0:T(8,128)S(1)} %broadcast_in_dim.20), channel_id=1, replica_groups=mesh['dp_0'=4,'dp_1'=8,'dp_2'=2,'rep'=4] {'dp_0','dp_1','dp_2'}, dimensions={0} | all-to-all | bytes 1310720 | tf_op jit(solution)/shard_map/all_to_all | solution.py:14
  72.2 1.3 convolution_bitcast_fusion.4
  73.5 0.1 copy.93
  73.6 11.7 %cholesky.59 = f32[128,128]{1,0:T(8,128)S(1)} custom-call(f32[128,128]{1,0:T(8,128)S(1)} %fusion.14), custom_call_target="Cholesky" | custom-call | tf_op jit(solution)/shard_map/jit(cholesky)/cholesky | solution.py:76
  85.3 0.6 compare_reduce_fusion.2
  86.0 0.7 fusion.7
  86.6 10.4 %custom-call.7 = f32[1,128,128]{1,2,0:T(8,128)} custom-call(f32[1,128,128]{2,1,0:T(8,128)S(1)} %fusion.7), custom_call_target="InvertDiagBlocksLowerTriangular" | custom-call | tf_op jit(solution)/shard_map/jit(_solve_triangular)/triangular_solve | solution.py:77
  97.1 0.1 reshape.26
  97.1 2.3 convolution_convert_fusion.3
  99.4 6.7 %convolution_bitcast_fusion.1 = f32[1280,128]{0,1:T(8,128)S(1)} fusion(bf16[2048,1280]{1,0:T(8,128)(2,1)} %param.6, bf16[128,1280]{1,0:T(8,128)(2,1)} %convolution_convert_fusion.3), kind=kOutput, calls=%fused_computation.1 | convolution fusion | flops 1342439424 | bytes 6225920 | tf_op jit(solution)/shard_map/dot_general | solution.py:99
  106.2 1.1 copy.94
  107.3 1.2 reshape_reshape.8
  108.5 0.4 copy.95
  108.9 13.6 %all_to_all.72 = f32[8,32,5,128]{3,1,2,0:T(8,128)S(1)} all-to-all(f32[8,32,5,128]{3,1,2,0:T(8,128)S(1)} %copy.95), channel_id=1, replica_groups=mesh['dp_0'=4,'dp_1'=8,'dp_2'=2,'rep'=4] {'dp_2','rep'}, dimensions={0} | all-to-all | bytes 1310720 | tf_op jit(solution)/shard_map/all_to_all | solution.py:53
  122.5 0.1 copy.96
  122.5 14.3 %all_to_all.73 = f32[32,5,128]{2,1,0:T(8,128)S(1)} all-to-all(f32[32,5,128]{2,1,0:T(8,128)S(1)} %copy.96), channel_id=1, replica_groups=mesh['dp_0'=4,'dp_1'=8,'dp_2'=2,'rep'=4] {'dp_0','dp_1'}, dimensions={0} | all-to-all | bytes 163840 | tf_op jit(solution)/shard_map/all_to_all | solution.py:61
  136.9 13.3 %all_to_all.74 = f32[32,5,128]{2,1,0:T(8,128)S(1)} all-to-all(f32[32,5,128]{2,1,0:T(8,128)S(1)} %broadcast_in_dim.21), channel_id=1, replica_groups=mesh['dp_0'=4,'dp_1'=8,'dp_2'=2,'rep'=4] {'dp_0','dp_1'}, dimensions={0} | all-to-all | bytes 163840 | tf_op jit(solution)/shard_map/all_to_all | solution.py:14
  150.2 0.1 broadcast_in_dim.22
  150.3 16.2 %all_to_all.75 = f32[8,32,5,128]{3,1,2,0:T(8,128)S(1)} all-to-all(f32[8,32,5,128]{3,1,2,0:T(8,128)S(1)} %broadcast_in_dim.22), channel_id=1, replica_groups=mesh['dp_0'=4,'dp_1'=8,'dp_2'=2,'rep'=4] {'dp_2','rep'}, dimensions={0} | all-to-all | bytes 1310720 | tf_op jit(solution)/shard_map/all_to_all | solution.py:14
  166.5 1.2 convolution_bitcast_fusion.3
  167.8 0.1 copy.98
  167.9 11.7 %cholesky.70 = f32[128,128]{1,0:T(8,128)S(1)} custom-call(f32[128,128]{1,0:T(8,128)S(1)} %fusion.12), custom_call_target="Cholesky" | custom-call | tf_op jit(solution)/shard_map/jit(cholesky)/cholesky | solution.py:76
  179.6 0.6 compare_reduce_fusion.1
  180.3 0.7 fusion.8
  181.0 9.8 %custom-call.8 = f32[1,128,128]{1,2,0:T(8,128)S(1)} custom-call(f32[1,128,128]{2,1,0:T(8,128)S(1)} %fusion.8), custom_call_target="InvertDiagBlocksLowerTriangular" | custom-call | tf_op jit(solution)/shard_map/jit(_solve_triangular)/triangular_solve | solution.py:77
  190.8 0.1 multiply_bitcast_fusion.1
  190.8 0.4 copy.99
  191.2 0.9 div.22
  192.2 1.8 convolution_convert_fusion.1
  194.0 6.7 %convolution_bitcast_fusion = f32[1280,128]{0,1:T(8,128)S(1)} fusion(bf16[2048,1280]{1,0:T(8,128)(2,1)} %param.6, bf16[128,1280]{1,0:T(8,128)(2,1)S(1)} %convolution_convert_fusion.1), kind=kOutput, calls=%fused_computation | convolution fusion | flops 1342439424 | bytes 6225920 | tf_op jit(solution)/shard_map/dot_general | solution.py:99
  200.7 1.1 copy.100
  201.7 1.2 reshape_reshape.9
  202.9 0.4 copy.101
  203.3 14.0 %all_to_all.76 = f32[8,32,5,128]{3,1,2,0:T(8,128)S(1)} all-to-all(f32[8,32,5,128]{3,1,2,0:T(8,128)S(1)} %copy.101), channel_id=1, replica_groups=mesh['dp_0'=4,'dp_1'=8,'dp_2'=2,'rep'=4] {'dp_2','rep'}, dimensions={0} | all-to-all | bytes 1310720 | tf_op jit(solution)/shard_map/all_to_all | solution.py:53
  217.3 0.1 copy.102
  217.4 12.3 %all_to_all.77 = f32[32,5,128]{2,1,0:T(8,128)S(1)} all-to-all(f32[32,5,128]{2,1,0:T(8,128)S(1)} %copy.102), channel_id=1, replica_groups=mesh['dp_0'=4,'dp_1'=8,'dp_2'=2,'rep'=4] {'dp_0','dp_1'}, dimensions={0} | all-to-all | bytes 163840 | tf_op jit(solution)/shard_map/all_to_all | solution.py:61
  229.8 13.3 %all_to_all.78 = f32[32,5,128]{2,1,0:T(8,128)S(1)} all-to-all(f32[32,5,128]{2,1,0:T(8,128)S(1)} %broadcast_in_dim.23), channel_id=1, replica_groups=mesh['dp_0'=4,'dp_1'=8,'dp_2'=2,'rep'=4] {'dp_0','dp_1'}, dimensions={0} | all-to-all | bytes 163840 | tf_op jit(solution)/shard_map/all_to_all | solution.py:14
  243.1 0.9 broadcast_in_dim.24
  244.0 6.2 %all-to-all-start.10 = ((f32[8,32,5,128]{3,1,2,0:T(8,128)}), f32[8,32,5,128]{3,1,2,0:T(8,128)S(1)}, u32[]{:S(2)}, u32[]{:S(2)}) async-start(f32[8,32,5,128]{3,1,2,0:T(8,128)} %broadcast_in_dim.24), calls=%async_computation.10 | async-start | bytes 1310720 | tf_op jit(solution)/shard_map/all_to_all | solution.py:14
  250.2 10.8 %all-to-all-done.10 = f32[8,32,5,128]{3,1,2,0:T(8,128)S(1)} async-done(((f32[8,32,5,128]{3,1,2,0:T(8,128)}), f32[8,32,5,128]{3,1,2,0:T(8,128)S(1)}, u32[]{:S(2)}, u32[]{:S(2)}) %all-to-all-start.10) | async-done | bytes 655392 | tf_op jit(solution)/shard_map/all_to_all | solution.py:14
  261.0 1.2 convolution_bitcast_fusion.2
  262.2 0.1 copy.104
  262.3 11.7 %cholesky.81 = f32[128,128]{1,0:T(8,128)S(1)} custom-call(f32[128,128]{1,0:T(8,128)S(1)} %fusion.10), custom_call_target="Cholesky" | custom-call | tf_op jit(solution)/shard_map/jit(cholesky)/cholesky | solution.py:76
  274.1 0.6 compare_reduce_fusion
  274.7 0.7 fusion.20
  275.4 9.8 %custom-call.9 = f32[1,128,128]{1,2,0:T(8,128)S(1)} custom-call(f32[1,128,128]{2,1,0:T(8,128)S(1)} %get-tuple-element.19), custom_call_target="InvertDiagBlocksLowerTriangular" | custom-call | tf_op jit(solution)/shard_map/jit(_solve_triangular)/triangular_solve | solution.py:77
  285.2 0.1 multiply_bitcast_fusion
  285.3 0.4 copy.105
  285.7 0.9 div.25
  286.6 0.7 copy.106
  287.3 1.8 fusion.2
  289.1 0.6 dynamic-slice_bitcast_fusion
  (17 shorter events, 0.4 us)
Async XLA Ops:
  0.6 31.8 %copy-start = (bf16[1,8192,128]{2,1,0:T(8,128)(2,1)S(1)}, bf16[1,8192,128]{2,1,0:T(8,128)(2,1)}, u32[]{:S(2)}) copy-start(bf16[1,8192,128]{2,1,0:T(8,128)(2,1)} %param.8) | copy-start | bytes 6291460
  244.0 16.9 %all-to-all-start.10 = ((f32[8,32,5,128]{3,1,2,0:T(8,128)}), f32[8,32,5,128]{3,1,2,0:T(8,128)S(1)}, u32[]{:S(2)}, u32[]{:S(2)}) async-start(f32[8,32,5,128]{3,1,2,0:T(8,128)} %broadcast_in_dim.24), calls=%async_computation.10 | async-start | bytes 1310720 | tf_op jit(solution)/shard_map/all_to_all | solution.py:14
where the time goes:
time: 294 us; the launch traced here: 290 us
  blocking collectives  164 us (56%)
  other arithmetic  69.5 us (24%)
  matrix products  27.2 us (9%)
  local copies, waits for them, and re-layouts  11.5 us (4%)
  waiting for transfers between devices  10.8 us (4%)
  starting transfers between devices  6.17 us (2%)
    all_to_all x5, blocking collectives, sent_to_all(): return lax.all_to_all(copies, axis, split_axis=0, concat_axis=0, tiled=True)  82.2 us
    another operation x9, other arithmetic, whole_factor(): lower = jnp.linalg.cholesky(gram)  37.2 us
    another operation x5, other arithmetic, whole_factor(): jax.scipy.linalg.solve_triangular(lower, matrix.T, lower=True)  31.4 us
    all_to_all x2, blocking collectives, sent_and_summed(): lax.all_to_all(in_blocks(shard, dim, length), axis, 0, 0, tiled=True)  27.5 us
    all_to_all x1, blocking collectives, body(): merged = lax.all_to_all(sketch, DP, split_axis=1, concat_axis=0, tiled=True)  27.4 us
    all_to_all x2, blocking collectives, sum_by_axis(): lax.all_to_all(nearer, far, split_axis=0, concat_axis=0, tiled=True)  26.6 us
    dot_general x2, matrix products, body(): lax.dot_general(tokens, projected, (((0,), (0,)), ((), ())), preferred_el...  13.4 us
    all_to_all x1, waiting for transfers between devices, sent_to_all(): return lax.all_to_all(copies, axis, split_axis=0, concat_axis=0, tiled=True)  10.8 us
  transfers between devices with their start and end apart: 1, of which 1 were waited for; matrix products, arithmetic and copies ran while one was open for 0% of the time, Pallas kernels for 0%

commit v1 on v0

v1 whole, which is shorter than its diff:
```python
import jax
import jax.numpy as jnp
from jax import lax
from jax.experimental import pallas as pl
from jax.experimental.pallas import tpu as pltpu
from jax.sharding import Mesh
from jax.sharding import PartitionSpec as P

ITERS = 2
ALL = ("x", "z", "c", "y")
LANES = 128
SUB = 8
VMEM_LIMIT = 60 * 1024 * 1024
F32 = jnp.float32
BF16 = jnp.bfloat16
HI = lax.Precision.HIGHEST
NN = (((1,), (0,)), ((), ()))
NT = (((1,), (1,)), ((), ()))


def layout(width):
    n = width // LANES
    index = {}
    for i in range(n):
        for j in range(i, n):
            index[i, j] = n + len(index)
    used = n + len(index)
    total = used + used % 2
    return n, index, used, total


def local_products(width, tokens_dev):
    n, index, used, total = layout(width)
    wide = 2 * LANES
    rows = total * LANES // 2

    def kernel(core, tok, smap, test, keep, send, xt, acc, sem):
        for i in range(n):
            cols = slice(i * LANES, (i + 1) * LANES)
            xt[cols, :] = tok[:, cols].T
        sketch = jnp.dot(smap[...].T, tok[...], preferred_element_type=F32).astype(BF16)
        start = jnp.dot(test[...].T, sketch, preferred_element_type=F32)
        for i in range(n):
            acc[i * LANES : (i + 1) * LANES, :] = start[:, i * LANES : (i + 1) * LANES]
        for b in range(used, total):
            acc[b * LANES : (b + 1) * LANES, :] = jnp.zeros((LANES, LANES), F32)
        for big in range(n // 2):
            high = (big + 1) * wide
            out = jnp.dot(
                xt[:high, :], tok[:, big * wide : high], preferred_element_type=F32
            )
            for j in range(2):
                col = 2 * big + j
                for i in range(col + 1):
                    at = index[i, col] * LANES
                    acc[at : at + LANES, :] = out[
                        i * LANES : (i + 1) * LANES, j * LANES : (j + 1) * LANES
                    ]
        c = core[0]
        first = pltpu.make_async_copy(acc.at[pl.ds((1 - c) * rows, rows)], send, sem.at[0])
        second = pltpu.make_async_copy(acc.at[pl.ds(c * rows, rows)], keep, sem.at[1])
        first.start()
        second.start()
        first.wait()
        second.wait()

    half = jax.ShapeDtypeStruct((rows, LANES), F32)
    return pl.pallas_call(
        kernel,
        out_shape=(half, half),
        in_specs=[
            pl.BlockSpec(memory_space=pltpu.SMEM),
            pl.BlockSpec(memory_space=pltpu.VMEM),
            pl.BlockSpec(memory_space=pltpu.VMEM),
            pl.BlockSpec(memory_space=pltpu.VMEM),
        ],
        out_specs=[pl.BlockSpec(memory_space=pl.ANY), pl.BlockSpec(memory_space=pl.ANY)],
        scratch_shapes=[
            pltpu.VMEM((width, tokens_dev), BF16),
            pltpu.VMEM((total * LANES, LANES), F32),
            pltpu.SemaphoreType.DMA((2,)),
        ],
        compiler_params=pltpu.CompilerParams(vmem_limit_bytes=VMEM_LIMIT),
        name="local_products",
    )


def eliminate(gram):
    k = gram.shape[0]
    blocks = k // SUB
    lane = lax.broadcasted_iota(jnp.int32, (SUB, k), 1)
    row = lax.broadcasted_iota(jnp.int32, (SUB, k), 0)
    work = []
    for b in range(blocks):
        eye = jnp.where(lane == row + b * SUB, 1.0, 0.0).astype(F32)
        work.append((gram[b * SUB : (b + 1) * SUB, :], eye))
    factor, inverse = [], []
    for b in range(blocks):
        a, e = work[b]
        at = b * SUB
        d = {}
        for p in range(SUB):
            for q in range(p, SUB):
                d[p, q] = jnp.broadcast_to(a[p : p + 1, at + q : at + q + 1], (1, k))
        ra = [a[p : p + 1, :] for p in range(SUB)]
        re = [e[p : p + 1, :] for p in range(SUB)]
        for p in range(SUB):
            pivot = d[p, p]
            y = lax.rsqrt(pivot)
            y = y * (1.5 - 0.5 * pivot * y * y)
            for q in range(p + 1, SUB):
                d[p, q] = d[p, q] * y
            ra[p] = ra[p] * y
            re[p] = re[p] * y
            for q in range(p + 1, SUB):
                for s in range(q, SUB):
                    d[q, s] = d[q, s] - d[p, q] * d[p, s]
                ra[q] = ra[q] - d[p, q] * ra[p]
                re[q] = re[q] - d[p, q] * re[p]
        fa = jnp.concatenate(ra, axis=0)
        fe = jnp.concatenate(re, axis=0)
        factor.append(jnp.where(lane >= row + at, fa, 0.0))
        inverse.append(fe)
        if b + 1 < blocks:
            turned = fa.T
            for o in range(b + 1, blocks):
                wa, we = work[o]
                cols = turned[o * SUB : (o + 1) * SUB, :]
                for p in range(SUB):
                    coef = jnp.broadcast_to(cols[:, p : p + 1], (SUB, k))
                    wa = wa - coef * ra[p]
                    we = we - coef * re[p]
                work[o] = (wa, we)
    return jnp.concatenate(factor, axis=0), jnp.concatenate(inverse, axis=0)


def refine(width, k, strip, total_tokens):
    n, index, used, total = layout(width)
    rows = total * LANES // 2

    def orthonormal(pt):
        gram = lax.dot_general(pt, pt, NT, precision=HI, preferred_element_type=F32)
        factor, inverse = eliminate(gram)
        return jnp.dot(inverse, pt, precision=HI, preferred_element_type=F32), factor

    def kernel(where, mine, other, basis, factor_out, acc, parts, zt, turned, sem):
        c = where[0]
        first = pltpu.make_async_copy(mine, acc.at[pl.ds(c * rows, rows)], sem.at[0])
        second = pltpu.make_async_copy(other, acc.at[pl.ds((1 - c) * rows, rows)], sem.at[1])
        first.start()
        second.start()
        first.wait()
        second.wait()
        for (i, j), b in index.items():
            v = acc[b * LANES : (b + 1) * LANES, :]
            hi = v.astype(BF16)
            rest = v - hi.astype(F32)
            mid = rest.astype(BF16)
            low = (rest - mid.astype(F32)).astype(BF16)
            ri = slice(i * LANES, (i + 1) * LANES)
            rj = slice(j * LANES, (j + 1) * LANES)
            parts[0, ri, rj] = hi
            parts[1, ri, rj] = mid
            parts[2, ri, rj] = low
        pt = jnp.concatenate([acc[i * LANES : (i + 1) * LANES, :] for i in range(n)], axis=1)
        vt, factor = orthonormal(pt)
        for _ in range(ITERS):
            vb = vt.astype(BF16)
            for j in range(n):
                high = (j + 1) * LANES
                rj = slice(j * LANES, high)
                z = jnp.zeros((k, LANES), F32)
                for s in (2, 1, 0):
                    z = z + lax.dot_general(
                        vb[:, :high], parts[s, :high, rj], NN, preferred_element_type=F32
                    )
                    if j + 1 < n:
                        z = z + lax.dot_general(
                            vb[:, high:], parts[s, rj, high:], NT, preferred_element_type=F32
                        )
                zt[:, rj] = z * (1.0 / total_tokens)
            vt, factor = orthonormal(zt[...])
        factor_out[...] = factor
        for i in range(n):
            cols = slice(i * LANES, (i + 1) * LANES)
            turned[cols, :] = vt[:, cols].T
        basis[...] = turned[pl.ds(where[1] * strip, strip), :]

    return pl.pallas_call(
        kernel,
        out_shape=(
            jax.ShapeDtypeStruct((strip, k), F32),
            jax.ShapeDtypeStruct((k, k), F32),
        ),
        in_specs=[
            pl.BlockSpec(memory_space=pltpu.SMEM),
            pl.BlockSpec(memory_space=pl.ANY),
            pl.BlockSpec(memory_space=pl.ANY),
        ],
        out_specs=[
            pl.BlockSpec(memory_space=pltpu.VMEM),
            pl.BlockSpec(memory_space=pltpu.VMEM),
        ],
        scratch_shapes=[
            pltpu.VMEM((total * LANES, LANES), F32),
            pltpu.VMEM((3, width, width), BF16),
            pltpu.VMEM((k, width), F32),
            pltpu.VMEM((width, k), F32),
            pltpu.SemaphoreType.DMA((2,)),
        ],
        compiler_params=pltpu.CompilerParams(vmem_limit_bytes=VMEM_LIMIT),
        name="refine",
    )


def body(tokens, sketch_map, test_matrix):
    tokens_dev, width = tokens.shape
    k = sketch_map.shape[1]
    strip = width // lax.axis_size(("x", "z", "c"))
    total_tokens = tokens_dev * lax.axis_size(ALL)
    core = lax.axis_index("c")
    slab = lax.axis_index(("x", "z", "c"))
    test = lax.dynamic_slice_in_dim(test_matrix[0], slab * k, k, 0)
    with jax.named_scope("products"):
        keep, send = local_products(width, tokens_dev)(
            core.reshape(1), tokens, sketch_map, test
        )
    rows = keep.shape[0]
    swap = [(0, 1), (1, 0)]
    with jax.named_scope("over_core"):
        half = keep + lax.ppermute(send, "c", swap)
    with jax.named_scope("over_xy"):
        plane = lax.axis_size(("x", "y"))
        tiles = half.reshape(plane, rows // plane, LANES)
        piece = jnp.sum(lax.all_to_all(tiles, ("x", "y"), 0, 0, tiled=True), axis=0)
    with jax.named_scope("over_z"):
        copies = jnp.broadcast_to(piece, (lax.axis_size("z"), *piece.shape))
        piece = jnp.sum(lax.all_to_all(copies, "z", 0, 0, tiled=True), axis=0)
    with jax.named_scope("back_xy"):
        copies = jnp.broadcast_to(piece, (plane, *piece.shape))
        half = lax.all_to_all(copies, ("x", "y"), 0, 0, tiled=True).reshape(rows, LANES)
    with jax.named_scope("back_core"):
        other = lax.ppermute(half, "c", swap)
    with jax.named_scope("refine"):
        where = jnp.stack([core, slab])
        return refine(width, k, strip, total_tokens)(where, half, other)


def solution(mesh):
    finer = Mesh(mesh.devices.reshape(4, 8, 2, mesh.shape["rep"]), ALL)
    return jax.shard_map(
        body,
        mesh=finer,
        in_specs=(P(ALL, None), P(ALL, None), P("y", None, None)),
        out_specs=(P(("x", "z", "c"), None), P()),
        check_vma=False,
    )
```

time: 294 us -> 164 us (0.56); the launches traced: 290 us -> 163 us
  blocking collectives: 164 us -> 95.6 us
  other arithmetic: 69.5 us -> 4.3 us
  Pallas kernels: 0 us -> 42.7 us
  matrix products: 27.2 us -> 0 us
  local copies, waits for them, and re-layouts: 11.5 us -> 3.76 us
  waiting for transfers between devices: 10.8 us -> 7.51 us
    all_to_all x10 -> x3, blocking collectives: 164 us -> 95.6 us  [the longest x1 34.2 us: body(): piece = jnp.sum(lax.all_to_all(copies, 'z', 0, 0, tiled=True), axis=0)]
    another operation x14 -> x1, other arithmetic: 68.5 us -> 0.59 us  [body(): where = jnp.stack([core, slab])]
    pallas_call x0 -> x2, Pallas kernels: none -> 42.7 us  [the longest x1 32.8 us: body(): return refine(width, k, strip, total_tokens)(where, half, other)]
    dot_general x7 -> x0, matrix products: 21.3 us -> none  [the longest x2 13.4 us: body(): lax.dot_general(tokens, projected, (((0,), (0,)), ((), ())), preferred_el...]
    all_to_all x1 -> x0, waiting for transfers between devices: 10.8 us -> none  [sent_to_all(): return lax.all_to_all(copies, axis, split_axis=0, concat_axis=0, tiled=True)]
    ppermute x0 -> x2, starting transfers between devices: none -> 8.68 us  [the longest x1 5.36 us: body(): other = lax.ppermute(half, 'c', swap)]
    ppermute x0 -> x2, waiting for transfers between devices: none -> 7.51 us  [the longest x1 4.09 us: body(): half = keep + lax.ppermute(send, 'c', swap)]
    all_to_all x1 -> x0, starting transfers between devices: 6.17 us -> none  [sent_to_all(): return lax.all_to_all(copies, axis, split_axis=0, concat_axis=0, tiled=True)]
  transfers between devices with their start and end apart: 1 -> 2, of which waited for: 1 -> 2; matrix products, arithmetic and copies ran while one was open for 0% -> 0% of each run, Pallas kernels for 0% -> 0%
where the time goes in v1:
time: 164 us; the launch traced here: 163 us
  blocking collectives  95.6 us (58%)
  Pallas kernels  42.7 us (26%)
  starting transfers between devices  8.68 us (5%)
  waiting for transfers between devices  7.51 us (5%)
  other arithmetic  4.3 us (3%)
  local copies, waits for them, and re-layouts  3.76 us (2%)
    all_to_all x1, blocking collectives, body(): piece = jnp.sum(lax.all_to_all(copies, 'z', 0, 0, tiled=True), axis=0)  34.2 us
    all_to_all x1, blocking collectives, body(): piece = jnp.sum(lax.all_to_all(tiles, ('x', 'y'), 0, 0, tiled=True), axis=0)  33.3 us
    pallas_call x1, Pallas kernels, body(): return refine(width, k, strip, total_tokens)(where, half, other)  32.8 us
    all_to_all x1, blocking collectives, body(): lax.all_to_all(copies, ('x', 'y'), 0, 0, tiled=True).reshape(rows, LANES)  28.1 us
    pallas_call x1, Pallas kernels, body(): local_products(width, tokens_dev)(core.reshape(1), tokens, sketch_map, test)  9.98 us
    ppermute x1, starting transfers between devices, body(): other = lax.ppermute(half, 'c', swap)  5.36 us
    ppermute x1, waiting for transfers between devices, body(): half = keep + lax.ppermute(send, 'c', swap)  4.09 us
    ppermute x1, waiting for transfers between devices, body(): other = lax.ppermute(half, 'c', swap)  3.42 us
  transfers between devices with their start and end apart: 2, of which 2 were waited for; matrix products, arithmetic and copies ran while one was open for 0% of the time, Pallas kernels for 0%

profile of v1, /device:TPU:1, one launch (start us, length us, event | category | flops | bytes accessed | tf_op | source)
XLA Modules:
  0.0 163.4 jit_solution(3586166517440827703)
XLA Ops:
  0.6 0.0 copy-start
  0.7 1.6 copy-done
  2.2 0.6 dynamic-slice_bitcast_fusion.test
  2.8 10.0 %local_products.1 = (f32[4224,128]{1,0:T(8,128)}, f32[4224,128]{1,0:T(8,128)}) custom-call(s32[1]{0:T(128)} %bitcast.core, bf16[2048,1280]{1,0:T(8,128)(2,1)} %tok.1, bf16[2048,128]{1,0:T(8,128)(2,1)} %smap.1, bf16[128,128]{1,0:T(8,128)(2,1)} %dynamic-slice_bitcast_fusion.test), custom_call_target="tpu_custom_call" | custom-call | tf_op jit(solution)/shard_map/products/local_products/pallas_call | solution.py:225
  12.8 3.3 %collective-permute-start = (f32[4224,128]{1,0:T(8,128)}, f32[4224,128]{1,0:T(8,128)S(1)}, u32[]{:S(2)}, u32[]{:S(2)}) collective-permute-start(f32[4224,128]{1,0:T(8,128)} %get-tuple-element.5), channel_id=1, source_target_pairs={{0,4},{4,0},{1,5},{5,1},{2,6},{6,2},{3,7},{7,3},{8,12},{12,8},{9,1... | collective-permute-start | bytes 6488072 | tf_op jit(solution)/shard_map/over_core/ppermute | solution.py:231
  16.1 4.1 %collective-permute-done = f32[4224,128]{1,0:T(8,128)S(1)} collective-permute-done((f32[4224,128]{1,0:T(8,128)}, f32[4224,128]{1,0:T(8,128)S(1)}, u32[]{:S(2)}, u32[]{:S(2)}) %collective-permute-start) | collective-permute-done | bytes 2162720 | tf_op jit(solution)/shard_map/over_core/ppermute | solution.py:231
  20.2 1.9 %add.15 = f32[4224,128]{1,0:T(8,128)S(1)} add(f32[4224,128]{1,0:T(8,128)} %get-tuple-element.4, f32[4224,128]{1,0:T(8,128)S(1)} %collective-permute-done) | non-fusion elementwise | flops 540672 | bytes 6488064 | tf_op jit(solution)/shard_map/over_core/add | solution.py:231
  22.2 33.3 %all_to_all.15 = f32[16,264,128]{2,1,0:T(8,128)} all-to-all(f32[16,264,128]{2,1,0:T(8,128)S(1)} %bitcast.6), channel_id=1, replica_groups=mesh['x'=4,'z'=8,'c'=2,'y'=4] {'x','y'}, dimensions={0} | all-to-all | bytes 4325376 | tf_op jit(solution)/shard_map/over_xy/all_to_all | solution.py:235
  55.4 1.7 %reduce_sum.18 = f32[264,128]{1,0:T(8,128)S(1)} reduce(f32[16,264,128]{2,1,0:T(8,128)} %all_to_all.15, f32[]{:T(128)} %constant.27.clone.1), dimensions={0}, to_apply=%region_0.0 | reduce | flops 506880 | bytes 2297860 | tf_op jit(solution)/shard_map/over_xy/reduce_sum | solution.py:235
  57.2 0.1 broadcast_in_dim.6
  57.2 34.2 %all_to_all.16 = f32[8,264,128]{2,1,0:T(8,128)S(1)} all-to-all(f32[8,264,128]{2,1,0:T(8,128)S(1)} %broadcast_in_dim.6), channel_id=1, replica_groups=mesh['x'=4,'z'=8,'c'=2,'y'=4] {'z'}, dimensions={0} | all-to-all | bytes 2162688 | tf_op jit(solution)/shard_map/over_z/all_to_all | solution.py:238
  91.5 0.1 reduce_sum.19
  91.6 0.1 broadcast_in_dim.7
  91.7 28.1 %all_to_all.17 = f32[16,264,128]{2,1,0:T(8,128)S(1)} all-to-all(f32[16,264,128]{2,1,0:T(8,128)S(1)} %broadcast_in_dim.7), channel_id=1, replica_groups=mesh['x'=4,'z'=8,'c'=2,'y'=4] {'x','y'}, dimensions={0} | all-to-all | bytes 4325376 | tf_op jit(solution)/shard_map/back_xy/all_to_all | solution.py:241
  119.8 0.0 copy-start.1
  119.8 1.3 copy-done.1
  121.1 5.4 %collective-permute-start.1 = (f32[4224,128]{1,0:T(8,128)S(1)}, f32[4224,128]{1,0:T(8,128)}, u32[]{:S(2)}, u32[]{:S(2)}) collective-permute-start(f32[4224,128]{1,0:T(8,128)S(1)} %bitcast.7), channel_id=1, source_target_pairs={{0,4},{4,0},{1,5},{5,1},{2,6},{6,2},{3,7},{7,3},{8,12},{12,8},{9,1... | collective-permute-start | bytes 6488072 | tf_op jit(solution)/shard_map/back_core/ppermute | solution.py:243
  126.5 0.6 pad_add_fusion.where
  127.1 3.4 %collective-permute-done.1.other = f32[4224,128]{1,0:T(8,128)} collective-permute-done((f32[4224,128]{1,0:T(8,128)S(1)}, f32[4224,128]{1,0:T(8,128)}, u32[]{:S(2)}, u32[]{:S(2)}) %collective-permute-start.1) | collective-permute-done | bytes 2162720 | tf_op jit(solution)/shard_map/back_core/ppermute | solution.py:243
  130.5 32.8 %refine.1 = (f32[20,128]{1,0:T(8,128)}, f32[128,128]{1,0:T(8,128)}) custom-call(s32[2]{0:T(128)} %pad_add_fusion.where, f32[4224,128]{1,0:T(8,128)} %bitcast.8, f32[4224,128]{1,0:T(8,128)} %collective-permute-done.1.other), custom_call_target="tpu_custom_call" | custom-call | tf_op jit(solution)/shard_map/refine/refine/pallas_call | solution.py:246
Async XLA Ops:
  0.6 1.6 copy-start
  12.8 7.4 %collective-permute-start = (f32[4224,128]{1,0:T(8,128)}, f32[4224,128]{1,0:T(8,128)S(1)}, u32[]{:S(2)}, u32[]{:S(2)}) collective-permute-start(f32[4224,128]{1,0:T(8,128)} %get-tuple-element.5), channel_id=1, source_target_pairs={{0,4},{4,0},{1,5},{5,1},{2,6},{6,2},{3,7},{7,3},{8,12},{12,8},{9,1... | collective-permute-start | bytes 6488072 | tf_op jit(solution)/shard_map/over_core/ppermute | solution.py:231
  119.8 1.4 copy-start.1
  121.1 9.4 %collective-permute-start.1 = (f32[4224,128]{1,0:T(8,128)S(1)}, f32[4224,128]{1,0:T(8,128)}, u32[]{:S(2)}, u32[]{:S(2)}) collective-permute-start(f32[4224,128]{1,0:T(8,128)S(1)} %bitcast.7), channel_id=1, source_target_pairs={{0,4},{4,0},{1,5},{5,1},{2,6},{6,2},{3,7},{7,3},{8,12},{12,8},{9,1... | collective-permute-start | bytes 6488072 | tf_op jit(solution)/shard_map/back_core/ppermute | solution.py:243

commit v2 on v1

v2 whole, which is shorter than its diff:
```python
import jax
import jax.numpy as jnp
from jax import lax
from jax.experimental import pallas as pl
from jax.experimental.pallas import tpu as pltpu
from jax.sharding import Mesh
from jax.sharding import PartitionSpec as P

ITERS = 2
ALL = ("x", "z", "c", "y")
LANES = 128
SUB = 8
MIB = 1024 * 1024
F32 = jnp.float32
BF16 = jnp.bfloat16
HI = lax.Precision.HIGHEST
NN = (((1,), (0,)), ((), ()))
NT = (((1,), (1,)), ((), ()))
TN = (((0,), (0,)), ((), ()))


class Packing:
    def __init__(self, width, pieces):
        self.n = width // LANES
        self.pairs = self.n // 2
        self.diagonals = 0
        start_at = -(-self.pairs // SUB) * SUB
        covariance = self.pairs * (2 * self.pairs - 1) + self.pairs
        bare = start_at + (self.n + covariance) * LANES
        self.rows = -(-bare // (pieces * SUB)) * (pieces * SUB)
        at = self.rows - (self.n + covariance) * LANES
        self.start = at
        at += self.n * LANES
        self.start_end = at
        self.offset = {}
        self.group = {}
        for pair in reversed(range(self.pairs)):
            begin = at
            left, right = 2 * pair, 2 * pair + 1
            for j in (left, right):
                for i in range(j):
                    self.offset[i, j] = at
                    at += LANES
            self.offset[left, left] = at
            at += LANES
            self.group[pair] = (begin, at)
        self.half = self.rows // 2

    def runs(self, begin, end):
        cuts = [begin] + ([self.half] if begin < self.half < end else []) + [end]
        return list(zip(cuts[:-1], cuts[1:]))


def local_products(pack, width, tokens_dev, k):
    chunks = 2
    part = tokens_dev // chunks
    runs = pack.runs(0, pack.start_end)
    for pair in reversed(range(pack.pairs)):
        runs += pack.runs(*pack.group[pair])

    def kernel(tok_hbm, smap_hbm, test_hbm, keep, send, tok, smap, test, acc, sem, out_sem):
        core = lax.axis_index("c")
        slab = lax.axis_index(("x", "z", "c"))
        loads = []
        for s in range(chunks):
            rows = pl.ds(s * part, part)
            loads.append(pltpu.make_async_copy(tok_hbm.at[rows], tok.at[rows], sem.at[s]))
        load_map = pltpu.make_async_copy(smap_hbm, smap, sem.at[chunks])
        load_test = pltpu.make_async_copy(
            test_hbm.at[0, pl.ds(pl.multiple_of(slab * k, k), k)], test, sem.at[chunks + 1]
        )
        load_map.start()
        for load in loads:
            load.start()
        load_test.start()

        def copies(home, first, last):
            made = []
            for r, (begin, end) in enumerate(runs):
                if begin < first or end > last:
                    continue
                side = begin // pack.half
                to = keep if side == home else send
                made.append(
                    pltpu.make_async_copy(
                        acc.at[begin:end],
                        to.at[begin - side * pack.half : end - side * pack.half],
                        out_sem.at[r],
                    )
                )
            return made

        def store(begin, end):
            for home in range(2):

                @pl.when(core == home)
                def _():
                    for copy in copies(home, begin, end):
                        copy.start()

        load_map.wait()
        sketch = jnp.zeros((k, width), F32)
        for s in range(chunks):
            loads[s].wait()
            rows = slice(s * part, (s + 1) * part)
            sketch = sketch + lax.dot_general(
                smap[rows, :], tok[rows, :], TN, preferred_element_type=F32
            )
        load_test.wait()
        start = lax.dot_general(test[...], sketch.astype(BF16), TN, preferred_element_type=F32)
        acc[: pack.start, :] = jnp.zeros((pack.start, LANES), F32)
        for i in range(pack.n):
            at = pack.start + i * LANES
            acc[at : at + LANES, :] = start[:, i * LANES : (i + 1) * LANES]
        row = lax.broadcasted_iota(jnp.int32, (LANES, LANES), 0)
        col = lax.broadcasted_iota(jnp.int32, (LANES, LANES), 1)
        for pair in reversed(range(pack.pairs)):
            base = 2 * pair * LANES
            high = base + 2 * LANES
            out = lax.dot_general(
                tok[:, :high], tok[:, base:high], TN, preferred_element_type=F32
            )
            for j in range(2):
                for i in range(2 * pair + j):
                    at = pack.offset[i, 2 * pair + j]
                    acc[at : at + LANES, :] = out[
                        i * LANES : (i + 1) * LANES, j * LANES : (j + 1) * LANES
                    ]
            upper = out[base : base + LANES, :LANES]
            lower = out[base + LANES : high, LANES:]
            at = pack.offset[2 * pair, 2 * pair]
            acc[at : at + LANES, :] = jnp.where(row <= col, upper, lower)
            acc[pair : pair + 1, :] = jnp.sum(jnp.where(row == col, lower, 0.0), axis=0)[None, :]
            store(*pack.group[pair])
        store(0, pack.start_end)
        for home in range(2):

            @pl.when(core == home)
            def _():
                for copy in copies(home, 0, pack.rows):
                    copy.wait()

    half = jax.ShapeDtypeStruct((pack.half, LANES), F32)
    return pl.pallas_call(
        kernel,
        out_shape=(half, half),
        in_specs=[pl.BlockSpec(memory_space=pl.ANY)] * 3,
        out_specs=[pl.BlockSpec(memory_space=pl.ANY)] * 2,
        scratch_shapes=[
            pltpu.VMEM((tokens_dev, width), BF16),
            pltpu.VMEM((tokens_dev, k), BF16),
            pltpu.VMEM((k, k), BF16),
            pltpu.VMEM((pack.rows, LANES), F32),
            pltpu.SemaphoreType.DMA((chunks + 2,)),
            pltpu.SemaphoreType.DMA((len(runs),)),
        ],
        compiler_params=pltpu.CompilerParams(vmem_limit_bytes=24 * MIB),
        name="local_products",
    )


def eliminate(gram):
    k = gram.shape[0]
    blocks = k // SUB
    lane = lax.broadcasted_iota(jnp.int32, (SUB, k), 1)
    row = lax.broadcasted_iota(jnp.int32, (SUB, k), 0)
    work, trace = [], []
    for b in range(blocks):
        work.append(gram[b * SUB : (b + 1) * SUB, :])
        trace.append(jnp.where(lane == row + b * SUB, 1.0, 0.0).astype(F32))
    factor, inverse = [], []
    for b in range(blocks):
        at = b * SUB
        spread = {}
        for o in range(b, blocks):
            for q in range(SUB):
                spread[o, q] = jnp.broadcast_to(work[o][:, at + q : at + q + 1], (SUB, k))
        d = {(p, q): spread[b, q][p : p + 1, :] for p in range(SUB) for q in range(p, SUB)}
        scale = []
        for p in range(SUB):
            scale.append(lax.rsqrt(d[p, p]))
            for q in range(p + 1, SUB):
                d[p, q] = d[p, q] * scale[p]
            for q in range(p + 1, SUB):
                for s in range(q, SUB):
                    d[q, s] = d[q, s] - d[p, q] * d[p, s]
        ra = [work[b][p : p + 1, :] for p in range(SUB)]
        re = [trace[b][p : p + 1, :] for p in range(SUB)]
        for p in range(SUB):
            ra[p] = ra[p] * scale[p]
            re[p] = re[p] * scale[p]
            for q in range(p + 1, SUB):
                ra[q] = ra[q] - d[p, q] * ra[p]
                re[q] = re[q] - d[p, q] * re[p]
        for o in range(b + 1, blocks):
            column = [spread[o, q] for q in range(SUB)]
            for p in range(SUB):
                column[p] = column[p] * scale[p]
                for q in range(p + 1, SUB):
                    column[q] = column[q] - d[p, q] * column[p]
                work[o] = work[o] - column[p] * ra[p]
                trace[o] = trace[o] - column[p] * re[p]
        factor.append(jnp.where(lane >= row + at, jnp.concatenate(ra, axis=0), 0.0))
        inverse.append(jnp.concatenate(re, axis=0))
    return jnp.concatenate(factor, axis=0), jnp.concatenate(inverse, axis=0)


def refine(pack, width, k, strip, total_tokens):
    n = pack.n

    def orthonormal(pt):
        gram = lax.dot_general(pt, pt, NT, precision=HI, preferred_element_type=F32)
        factor, inverse = eliminate(gram)
        return jnp.dot(inverse, pt, precision=HI, preferred_element_type=F32), factor

    def kernel(mine, other, basis, factor_out, acc, parts, zt, turned, sem):
        core = lax.axis_index("c")
        slab = lax.axis_index(("x", "z", "c"))
        cut = pack.start_end

        def load(home, run):
            sides = (mine, other) if home == 0 else (other, mine)
            side, begin, end = ((0, 0, cut), (0, cut, pack.half), (1, 0, pack.half))[run]
            at = side * pack.half
            return pltpu.make_async_copy(
                sides[side].at[begin:end], acc.at[at + begin : at + end], sem.at[run]
            )

        def each_home(action):
            for home in range(2):

                @pl.when(core == home)
                def _():
                    action(home)

        each_home(lambda home: [load(home, run).start() for run in range(3)])
        each_home(lambda home: load(home, 0).wait())
        pt = jnp.concatenate(
            [acc[pack.start + i * LANES : pack.start + (i + 1) * LANES, :] for i in range(n)],
            axis=1,
        )
        vt, factor = orthonormal(pt)
        each_home(lambda home: [load(home, run).wait() for run in (1, 2)])

        def put(i, j, v):
            hi = v.astype(BF16)
            rest = v - hi.astype(F32)
            mid = rest.astype(BF16)
            low = (rest - mid.astype(F32)).astype(BF16)
            ri = slice(i * LANES, (i + 1) * LANES)
            rj = slice(j * LANES, (j + 1) * LANES)
            parts[0, ri, rj] = hi
            parts[1, ri, rj] = mid
            parts[2, ri, rj] = low

        row = lax.broadcasted_iota(jnp.int32, (LANES, LANES), 0)
        col = lax.broadcasted_iota(jnp.int32, (LANES, LANES), 1)
        for (i, j), at in pack.offset.items():
            v = acc[at : at + LANES, :]
            if i < j:
                put(i, j, v)
            else:
                flipped = v.T
                put(i, i, jnp.where(row <= col, v, flipped))
                pair = i // 2
                whole = jnp.where(row > col, v, flipped)
                put(i + 1, i + 1, jnp.where(row == col, acc[pair : pair + 1, :], whole))
        for _ in range(ITERS):
            vb = vt.astype(BF16)
            for j in range(n):
                high = (j + 1) * LANES
                rj = slice(j * LANES, high)
                z = jnp.zeros((k, LANES), F32)
                for s in (2, 1, 0):
                    z = z + lax.dot_general(
                        vb[:, :high], parts[s, :high, rj], NN, preferred_element_type=F32
                    )
                    if j + 1 < n:
                        z = z + lax.dot_general(
                            vb[:, high:], parts[s, rj, high:], NT, preferred_element_type=F32
                        )
                zt[:, rj] = z * (1.0 / total_tokens)
            vt, factor = orthonormal(zt[...])
        factor_out[...] = factor
        for i in range(n):
            cols = slice(i * LANES, (i + 1) * LANES)
            turned[cols, :] = vt[:, cols].T
        basis[...] = turned[pl.ds(slab * strip, strip), :]

    return pl.pallas_call(
        kernel,
        out_shape=(
            jax.ShapeDtypeStruct((strip, k), F32),
            jax.ShapeDtypeStruct((k, k), F32),
        ),
        in_specs=[pl.BlockSpec(memory_space=pl.ANY)] * 2,
        out_specs=[pl.BlockSpec(memory_space=pltpu.VMEM)] * 2,
        scratch_shapes=[
            pltpu.VMEM((pack.rows, LANES), F32),
            pltpu.VMEM((3, width, width), BF16),
            pltpu.VMEM((k, width), F32),
            pltpu.VMEM((width, k), F32),
            pltpu.SemaphoreType.DMA((3,)),
        ],
        compiler_params=pltpu.CompilerParams(vmem_limit_bytes=28 * MIB),
        name="refine",
    )


def body(tokens, sketch_map, test_matrix):
    tokens_dev, width = tokens.shape
    k = sketch_map.shape[1]
    strip = width // lax.axis_size(("x", "z", "c"))
    total_tokens = tokens_dev * lax.axis_size(ALL)
    plane = lax.axis_size(("x", "y"))
    pack = Packing(width, 2 * plane)
    with jax.named_scope("products"):
        held = [
            pltpu.with_memory_space_constraint(array, pltpu.HBM)
            for array in (tokens, sketch_map, test_matrix)
        ]
        keep, send = local_products(pack, width, tokens_dev, k)(*held)
    swap = [(0, 1), (1, 0)]
    with jax.named_scope("over_core"):
        half = keep + lax.ppermute(send, "c", swap)
    with jax.named_scope("over_xy"):
        tiles = half.reshape(plane, pack.half // plane, LANES)
        piece = jnp.sum(lax.all_to_all(tiles, ("x", "y"), 0, 0, tiled=True), axis=0)
    with jax.named_scope("over_z"):
        copies = jnp.broadcast_to(piece, (lax.axis_size("z"), *piece.shape))
        piece = jnp.sum(lax.all_to_all(copies, "z", 0, 0, tiled=True), axis=0)
    with jax.named_scope("back_xy"):
        copies = jnp.broadcast_to(piece, (plane, *piece.shape))
        half = lax.all_to_all(copies, ("x", "y"), 0, 0, tiled=True).reshape(pack.half, LANES)
    with jax.named_scope("back_core"):
        other = lax.ppermute(half, "c", swap)
    with jax.named_scope("refine"):
        return refine(pack, width, k, strip, total_tokens)(half, other)


def solution(mesh):
    finer = Mesh(mesh.devices.reshape(4, 8, 2, mesh.shape["rep"]), ALL)
    return jax.shard_map(
        body,
        mesh=finer,
        in_specs=(P(ALL, None), P(ALL, None), P("y", None, None)),
        out_specs=(P(("x", "z", "c"), None), P()),
        check_vma=False,
    )
```

time: 164 us -> 148 us (0.902)
  other arithmetic: 4.3 us -> 0.36 us
  blocking collectives: 95.6 us -> 91.7 us
  local copies, waits for them, and re-layouts: 3.76 us -> 0.2 us
  Pallas kernels: 42.7 us -> 39.2 us
    pallas_call x2, Pallas kernels: 42.7 us -> 39.2 us  [the longest x1 25.3 us: body(): return refine(pack, width, k, strip, total_tokens)(half, other)]
    unnamed x4 -> x0, local copies, waits for them, and re-layouts: 2.93 us -> none
    all_to_all x1, blocking collectives: 33.3 us -> 31.4 us  [body(): piece = jnp.sum(lax.all_to_all(tiles, ('x', 'y'), 0, 0, tiled=True), axis=0)]
    add x1, other arithmetic: 1.92 us -> 0.21 us  [body(): half = keep + lax.ppermute(send, 'c', swap)]
where the time goes in v2:
time: 148 us
  blocking collectives  91.7 us (62%)
  Pallas kernels  39.2 us (26%)
  starting transfers between devices  8.58 us (6%)
  waiting for transfers between devices  7.39 us (5%)
    all_to_all x1, blocking collectives, body(): piece = jnp.sum(lax.all_to_all(copies, 'z', 0, 0, tiled=True), axis=0)  33.2 us
    all_to_all x1, blocking collectives, body(): piece = jnp.sum(lax.all_to_all(tiles, ('x', 'y'), 0, 0, tiled=True), axis=0)  31.4 us
    all_to_all x1, blocking collectives, body(): lax.all_to_all(copies, ('x', 'y'), 0, 0, tiled=True)  27 us
    pallas_call x1, Pallas kernels, body(): return refine(pack, width, k, strip, total_tokens)(half, other)  25.3 us
    pallas_call x1, Pallas kernels, body(): keep, send = local_products(pack, width, tokens_dev, k)(*held)  13.9 us
    ppermute x1, starting transfers between devices, body(): other = lax.ppermute(half, 'c', swap)  5.23 us
    ppermute x1, waiting for transfers between devices, body(): other = lax.ppermute(half, 'c', swap)  3.69 us
    ppermute x1, waiting for transfers between devices, body(): half = keep + lax.ppermute(send, 'c', swap)  3.69 us
  transfers between devices with their start and end apart: 2, of which 2 were waited for; matrix products, arithmetic and copies ran while one was open for 0% of the time, Pallas kernels for 0%

profile of v2, /device:TPU:1, one launch (start us, length us, event | category | flops | bytes accessed | tf_op | source)
XLA Modules:
  0.0 148.2 jit_solution(1061126024584638606)
XLA Ops:
  0.6 13.9 %local_products.1 = (f32[3968,128]{1,0:T(8,128)S(1)}, f32[3968,128]{1,0:T(8,128)S(1)}) custom-call(bf16[2048,1280]{1,0:T(8,128)(2,1)} %tok_hbm.1, bf16[2048,128]{1,0:T(8,128)(2,1)} %smap_hbm.1, bf16[1,8192,128]{2,1,0:T(8,128)(2,1)} %test_hbm.1), custom_call_target="tpu_custom_call" | custom-call | tf_op jit(solution)/shard_map/products/local_products/pallas_call | solution.py:322
  14.5 3.4 %collective-permute-start = (f32[3968,128]{1,0:T(8,128)S(1)}, f32[3968,128]{1,0:T(8,128)S(1)}, u32[]{:S(2)}, u32[]{:S(2)}) collective-permute-start(f32[3968,128]{1,0:T(8,128)S(1)} %get-tuple-element.5), channel_id=1, source_target_pairs={{0,4},{4,0},{1,5},{5,1},{2,6},{6,2},{3,7},{7,3},{8,12},{12,8},{9,1... | collective-permute-start | bytes 6094856 | tf_op jit(solution)/shard_map/over_core/ppermute | solution.py:325
  17.8 3.7 %collective-permute-done = f32[3968,128]{1,0:T(8,128)S(1)} collective-permute-done((f32[3968,128]{1,0:T(8,128)S(1)}, f32[3968,128]{1,0:T(8,128)S(1)}, u32[]{:S(2)}, u32[]{:S(2)}) %collective-permute-start) | collective-permute-done | bytes 2031648 | tf_op jit(solution)/shard_map/over_core/ppermute | solution.py:325
  21.5 0.2 add.3
  21.7 31.4 %all_to_all.15 = f32[16,248,128]{2,1,0:T(8,128)S(1)} all-to-all(f32[16,248,128]{2,1,0:T(8,128)S(1)} %bitcast.4), channel_id=1, replica_groups=mesh['x'=4,'z'=8,'c'=2,'y'=4] {'x','y'}, dimensions={0} | all-to-all | bytes 4063232 | tf_op jit(solution)/shard_map/over_xy/all_to_all | solution.py:328
  53.2 0.1 reduce_sum.18
  53.3 0.1 broadcast_in_dim.6
  53.4 33.2 %all_to_all.16 = f32[8,248,128]{2,1,0:T(8,128)S(1)} all-to-all(f32[8,248,128]{2,1,0:T(8,128)S(1)} %broadcast_in_dim.6), channel_id=1, replica_groups=mesh['x'=4,'z'=8,'c'=2,'y'=4] {'z'}, dimensions={0} | all-to-all | bytes 2031616 | tf_op jit(solution)/shard_map/over_z/all_to_all | solution.py:331
  86.6 0.1 reduce_sum.19
  86.6 0.1 broadcast_in_dim.7
  86.7 27.0 %all_to_all.17 = f32[16,248,128]{2,1,0:T(8,128)S(1)} all-to-all(f32[16,248,128]{2,1,0:T(8,128)S(1)} %broadcast_in_dim.7), channel_id=1, replica_groups=mesh['x'=4,'z'=8,'c'=2,'y'=4] {'x','y'}, dimensions={0} | all-to-all | bytes 4063232 | tf_op jit(solution)/shard_map/back_xy/all_to_all | solution.py:334
  113.8 5.2 %collective-permute-start.1 = (f32[3968,128]{1,0:T(8,128)S(1)}, f32[3968,128]{1,0:T(8,128)S(1)}, u32[]{:S(2)}, u32[]{:S(2)}) collective-permute-start(f32[3968,128]{1,0:T(8,128)S(1)} %bitcast.2), channel_id=1, source_target_pairs={{0,4},{4,0},{1,5},{5,1},{2,6},{6,2},{3,7},{7,3},{8,12},{12,8},{9,1... | collective-permute-start | bytes 6094856 | tf_op jit(solution)/shard_map/back_core/ppermute | solution.py:336
  119.0 3.7 %collective-permute-done.1.other = f32[3968,128]{1,0:T(8,128)S(1)} collective-permute-done((f32[3968,128]{1,0:T(8,128)S(1)}, f32[3968,128]{1,0:T(8,128)S(1)}, u32[]{:S(2)}, u32[]{:S(2)}) %collective-permute-start.1) | collective-permute-done | bytes 2031648 | tf_op jit(solution)/shard_map/back_core/ppermute | solution.py:336
  122.7 25.3 %refine.1 = (f32[20,128]{1,0:T(8,128)}, f32[128,128]{1,0:T(8,128)}) custom-call(f32[3968,128]{1,0:T(8,128)S(1)} %bitcast.3, f32[3968,128]{1,0:T(8,128)S(1)} %collective-permute-done.1.other), custom_call_target="tpu_custom_call" | custom-call | tf_op jit(solution)/shard_map/refine/refine/pallas_call | solution.py:338
Async XLA Ops:
  14.5 7.0 %collective-permute-start = (f32[3968,128]{1,0:T(8,128)S(1)}, f32[3968,128]{1,0:T(8,128)S(1)}, u32[]{:S(2)}, u32[]{:S(2)}) collective-permute-start(f32[3968,128]{1,0:T(8,128)S(1)} %get-tuple-element.5), channel_id=1, source_target_pairs={{0,4},{4,0},{1,5},{5,1},{2,6},{6,2},{3,7},{7,3},{8,12},{12,8},{9,1... | collective-permute-start | bytes 6094856 | tf_op jit(solution)/shard_map/over_core/ppermute | solution.py:325
  113.8 8.9 %collective-permute-start.1 = (f32[3968,128]{1,0:T(8,128)S(1)}, f32[3968,128]{1,0:T(8,128)S(1)}, u32[]{:S(2)}, u32[]{:S(2)}) collective-permute-start(f32[3968,128]{1,0:T(8,128)S(1)} %bitcast.2), channel_id=1, source_target_pairs={{0,4},{4,0},{1,5},{5,1},{2,6},{6,2},{3,7},{7,3},{8,12},{12,8},{9,1... | collective-permute-start | bytes 6094856 | tf_op jit(solution)/shard_map/back_core/ppermute | solution.py:336

commit v3 on v2

v3 whole, which is shorter than its diff:
```python
import jax
import jax.numpy as jnp
from jax import lax
from jax.experimental import pallas as pl
from jax.experimental.pallas import tpu as pltpu
from jax.sharding import Mesh
from jax.sharding import PartitionSpec as P

ITERS = 2
ALL = ("x", "z", "c", "y")
LANES = 128
SUB = 8
MIB = 1024 * 1024
F32 = jnp.float32
BF16 = jnp.bfloat16
HI = lax.Precision.HIGHEST
NN = (((1,), (0,)), ((), ()))
NT = (((1,), (1,)), ((), ()))
TN = (((0,), (0,)), ((), ()))


class Packing:
    def __init__(self, width, pieces):
        self.n = width // LANES
        count = self.n // 2
        last = count - 1
        self.pairs = (list(range(last - 1, -1, -2)), list(range(last, -1, -2)))
        self.rows = []
        self.offset = {}
        for stream, pairs in enumerate(self.pairs):
            used = sum(4 * pair + 2 for pair in pairs) * LANES
            head = 0 if stream else -(-count // SUB) * SUB + self.n * LANES
            total = -(-(head + used) // (pieces * SUB)) * (pieces * SUB)
            at = total - used
            if not stream:
                self.start = at - self.n * LANES
                self.start_end = at
            for pair in pairs:
                left, right = 2 * pair, 2 * pair + 1
                for j in (left, right):
                    for i in range(j):
                        self.offset[i, j] = (stream, at)
                        at += LANES
                self.offset[left, left] = (stream, at)
                at += LANES
            self.rows.append(total)


def split_out(acc, keep, send, sem, rows, core):
    def copy(home, side):
        to = keep if side == home else send
        return pltpu.make_async_copy(
            acc.at[side * rows // 2 : (side + 1) * rows // 2], to, sem.at[side]
        )

    for home in range(2):

        @pl.when(core == home)
        def _():
            for side in (1 - home, home):
                copy(home, side).start()
            for side in (1 - home, home):
                copy(home, side).wait()


def local_products(pack, stream, width, tokens_dev, k):
    chunks = 4
    part = tokens_dev // chunks
    rows_out = pack.rows[stream]

    def pair_products(pack, tok, acc):
        row = lax.broadcasted_iota(jnp.int32, (LANES, LANES), 0)
        col = lax.broadcasted_iota(jnp.int32, (LANES, LANES), 1)
        for pair in pack.pairs[stream]:
            base = 2 * pair * LANES
            high = base + 2 * LANES
            out = lax.dot_general(tok[:, :high], tok[:, base:high], TN, preferred_element_type=F32)
            for j in range(2):
                for i in range(2 * pair + j):
                    at = pack.offset[i, 2 * pair + j][1]
                    acc[at : at + LANES, :] = out[
                        i * LANES : (i + 1) * LANES, j * LANES : (j + 1) * LANES
                    ]
            upper = out[base : base + LANES, :LANES]
            lower = out[base + LANES : high, LANES:]
            at = pack.offset[2 * pair, 2 * pair][1]
            acc[at : at + LANES, :] = jnp.where(row <= col, upper, lower)

    def with_start(tok_hbm, smap_hbm, test_hbm, keep, send, tok, smap, test, acc, sem, out_sem):
        core = lax.axis_index("c")
        slab = lax.axis_index(("x", "z", "c"))
        load_map = pltpu.make_async_copy(smap_hbm, smap, sem.at[chunks])
        load_test = pltpu.make_async_copy(
            test_hbm.at[0, pl.ds(pl.multiple_of(slab * k, k), k)], test, sem.at[chunks + 1]
        )
        loads = []
        for s in range(chunks):
            rows = pl.ds(s * part, part)
            loads.append(pltpu.make_async_copy(tok_hbm.at[rows], tok.at[rows], sem.at[s]))
        load_map.start()
        for load in loads:
            load.start()
        load_test.start()
        load_map.wait()
        sketch = jnp.zeros((k, width), F32)
        for s in range(chunks):
            loads[s].wait()
            rows = slice(s * part, (s + 1) * part)
            sketch = sketch + lax.dot_general(
                smap[rows, :], tok[rows, :], TN, preferred_element_type=F32
            )
        load_test.wait()
        start = lax.dot_general(test[...], sketch.astype(BF16), TN, preferred_element_type=F32)
        acc[: pack.start, :] = jnp.zeros((pack.start, LANES), F32)
        for i in range(pack.n):
            at = pack.start + i * LANES
            acc[at : at + LANES, :] = start[:, i * LANES : (i + 1) * LANES]
        pair_products(pack, tok, acc)
        row = lax.broadcasted_iota(jnp.int32, (LANES, LANES), 0)
        col = lax.broadcasted_iota(jnp.int32, (LANES, LANES), 1)
        for pair in range(pack.n // 2):
            odd = tok[:, (2 * pair + 1) * LANES : (2 * pair + 2) * LANES]
            own = lax.dot_general(odd, odd, TN, preferred_element_type=F32)
            acc[pair : pair + 1, :] = jnp.sum(jnp.where(row == col, own, 0.0), axis=0)[None, :]
        split_out(acc, keep, send, out_sem, rows_out, core)

    def without_start(tok_hbm, keep, send, tok, acc, sem, out_sem):
        core = lax.axis_index("c")
        load = pltpu.make_async_copy(tok_hbm, tok, sem.at[0])
        load.start()
        load.wait()
        pair_products(pack, tok, acc)
        split_out(acc, keep, send, out_sem, rows_out, core)

    half = jax.ShapeDtypeStruct((rows_out // 2, LANES), F32)
    small = [] if stream else [pltpu.VMEM((tokens_dev, k), BF16), pltpu.VMEM((k, k), BF16)]
    return pl.pallas_call(
        without_start if stream else with_start,
        out_shape=(half, half),
        in_specs=[pl.BlockSpec(memory_space=pl.ANY)] * (1 if stream else 3),
        out_specs=[pl.BlockSpec(memory_space=pl.ANY)] * 2,
        scratch_shapes=[
            pltpu.VMEM((tokens_dev, width), BF16),
            *small,
            pltpu.VMEM((rows_out, LANES), F32),
            pltpu.SemaphoreType.DMA((chunks + 2,)),
            pltpu.SemaphoreType.DMA((2,)),
        ],
        compiler_params=pltpu.CompilerParams(vmem_limit_bytes=24 * MIB),
        cost_estimate=pl.CostEstimate(
            flops=2 * tokens_dev * rows_out * LANES,
            bytes_accessed=2 * tokens_dev * width + 4 * rows_out * LANES,
            transcendentals=0,
        ),
        name="products_stream_%d" % stream,
    )


def eliminate(gram):
    k = gram.shape[0]
    blocks = k // SUB
    lane = lax.broadcasted_iota(jnp.int32, (SUB, k), 1)
    row = lax.broadcasted_iota(jnp.int32, (SUB, k), 0)
    work, trace = [], []
    for b in range(blocks):
        work.append(gram[b * SUB : (b + 1) * SUB, :])
        trace.append(jnp.where(lane == row + b * SUB, 1.0, 0.0).astype(F32))
    factor, inverse = [], []
    for b in range(blocks):
        at = b * SUB
        spread = {}
        for o in range(b, blocks):
            for q in range(SUB):
                spread[o, q] = jnp.broadcast_to(work[o][:, at + q : at + q + 1], (SUB, k))
        d = {(p, q): spread[b, q][p : p + 1, :] for p in range(SUB) for q in range(p, SUB)}
        scale = []
        for p in range(SUB):
            scale.append(lax.rsqrt(d[p, p]))
            for q in range(p + 1, SUB):
                d[p, q] = d[p, q] * scale[p]
            for q in range(p + 1, SUB):
                for s in range(q, SUB):
                    d[q, s] = d[q, s] - d[p, q] * d[p, s]
        ra = [work[b][p : p + 1, :] for p in range(SUB)]
        re = [trace[b][p : p + 1, :] for p in range(SUB)]
        for p in range(SUB):
            ra[p] = ra[p] * scale[p]
            re[p] = re[p] * scale[p]
            for q in range(p + 1, SUB):
                ra[q] = ra[q] - d[p, q] * ra[p]
                re[q] = re[q] - d[p, q] * re[p]
        for o in range(b + 1, blocks):
            column = [spread[o, q] for q in range(SUB)]
            for p in range(SUB):
                column[p] = column[p] * scale[p]
                for q in range(p + 1, SUB):
                    column[q] = column[q] - d[p, q] * column[p]
                work[o] = work[o] - column[p] * ra[p]
                trace[o] = trace[o] - column[p] * re[p]
        factor.append(jnp.where(lane >= row + at, jnp.concatenate(ra, axis=0), 0.0))
        inverse.append(jnp.concatenate(re, axis=0))
    return jnp.concatenate(factor, axis=0), jnp.concatenate(inverse, axis=0)


def orthonormal(pt):
    gram = lax.dot_general(pt, pt, NT, precision=HI, preferred_element_type=F32)
    factor, inverse = eliminate(gram)
    return jnp.dot(inverse, pt, precision=HI, preferred_element_type=F32), factor


def merged(mine, other, acc, sem, home, run):
    from_half = mine if home == run else other
    rows = acc.shape[0] // 2
    return pltpu.make_async_copy(from_half, acc.at[run * rows : (run + 1) * rows], sem)


def first_basis(pack, width, k):
    def kernel(mine, other, vt_out, held, sem):
        core = lax.axis_index("c")
        for home in range(2):

            @pl.when(core == home)
            def _():
                half = mine if home == 0 else other
                load = pltpu.make_async_copy(
                    half.at[pack.start : pack.start_end], held, sem
                )
                load.start()
                load.wait()

        pt = jnp.concatenate(
            [held[i * LANES : (i + 1) * LANES, :] for i in range(pack.n)], axis=1
        )
        vt_out[...] = orthonormal(pt)[0]

    return pl.pallas_call(
        kernel,
        out_shape=jax.ShapeDtypeStruct((k, width), F32),
        in_specs=[pl.BlockSpec(memory_space=pl.ANY)] * 2,
        out_specs=pl.BlockSpec(memory_space=pltpu.VMEM),
        scratch_shapes=[pltpu.VMEM((width, LANES), F32), pltpu.SemaphoreType.DMA],
        compiler_params=pltpu.CompilerParams(vmem_limit_bytes=8 * MIB),
        cost_estimate=pl.CostEstimate(
            flops=k * k * width * 400, bytes_accessed=8 * width * k, transcendentals=k
        ),
        name="first_basis",
    )


def refine(pack, width, k, strip, total_tokens):
    n = pack.n

    def kernel(mine_0, other_0, mine_1, other_1, first, basis, factor_out, acc_0, acc_1, parts, zt, turned, sem):
        core = lax.axis_index("c")
        slab = lax.axis_index(("x", "z", "c"))
        accs = (acc_0, acc_1)
        halves = ((mine_0, other_0), (mine_1, other_1))

        def each(action):
            for home in range(2):

                @pl.when(core == home)
                def _():
                    for stream in range(2):
                        for run in range(2):
                            copy = merged(
                                *halves[stream], accs[stream], sem.at[stream, run], home, run
                            )
                            action(copy)

        each(lambda copy: copy.start())
        each(lambda copy: copy.wait())

        def put(i, j, v):
            hi = v.astype(BF16)
            rest = v - hi.astype(F32)
            mid = rest.astype(BF16)
            low = (rest - mid.astype(F32)).astype(BF16)
            ri = slice(i * LANES, (i + 1) * LANES)
            rj = slice(j * LANES, (j + 1) * LANES)
            parts[0, ri, rj] = hi
            parts[1, ri, rj] = mid
            parts[2, ri, rj] = low

        row = lax.broadcasted_iota(jnp.int32, (LANES, LANES), 0)
        col = lax.broadcasted_iota(jnp.int32, (LANES, LANES), 1)
        for (i, j), (stream, at) in pack.offset.items():
            v = accs[stream][at : at + LANES, :]
            if i < j:
                put(i, j, v)
            else:
                flipped = v.T
                put(i, i, jnp.where(row <= col, v, flipped))
                pair = i // 2
                whole = jnp.where(row > col, v, flipped)
                put(i + 1, i + 1, jnp.where(row == col, acc_0[pair : pair + 1, :], whole))
        vt = first[...]
        for _ in range(ITERS):
            vb = vt.astype(BF16)
            for j in range(n):
                high = (j + 1) * LANES
                rj = slice(j * LANES, high)
                z = jnp.zeros((k, LANES), F32)
                for s in (2, 1, 0):
                    z = z + lax.dot_general(
                        vb[:, :high], parts[s, :high, rj], NN, preferred_element_type=F32
                    )
                    if j + 1 < n:
                        z = z + lax.dot_general(
                            vb[:, high:], parts[s, rj, high:], NT, preferred_element_type=F32
                        )
                zt[:, rj] = z * (1.0 / total_tokens)
            vt, factor = orthonormal(zt[...])
        factor_out[...] = factor
        for i in range(n):
            cols = slice(i * LANES, (i + 1) * LANES)
            turned[cols, :] = vt[:, cols].T
        basis[...] = turned[pl.ds(slab * strip, strip), :]

    return pl.pallas_call(
        kernel,
        out_shape=(
            jax.ShapeDtypeStruct((strip, k), F32),
            jax.ShapeDtypeStruct((k, k), F32),
        ),
        in_specs=[pl.BlockSpec(memory_space=pl.ANY)] * 4 + [pl.BlockSpec(memory_space=pltpu.VMEM)],
        out_specs=[pl.BlockSpec(memory_space=pltpu.VMEM)] * 2,
        scratch_shapes=[
            pltpu.VMEM((pack.rows[0], LANES), F32),
            pltpu.VMEM((pack.rows[1], LANES), F32),
            pltpu.VMEM((3, width, width), BF16),
            pltpu.VMEM((k, width), F32),
            pltpu.VMEM((width, k), F32),
            pltpu.SemaphoreType.DMA((2, 2)),
        ],
        compiler_params=pltpu.CompilerParams(vmem_limit_bytes=28 * MIB),
        name="refine",
    )


def to_all(piece, axes):
    copies = jnp.broadcast_to(piece, (lax.axis_size(axes), *piece.shape))
    return lax.all_to_all(copies, axes, 0, 0, tiled=True)


def body(tokens, sketch_map, test_matrix):
    tokens_dev, width = tokens.shape
    k = sketch_map.shape[1]
    strip = width // lax.axis_size(("x", "z", "c"))
    total_tokens = tokens_dev * lax.axis_size(ALL)
    plane = lax.axis_size(("x", "y"))
    pack = Packing(width, 2 * plane)
    swap = [(0, 1), (1, 0)]
    held = [
        pltpu.with_memory_space_constraint(array, pltpu.HBM)
        for array in (tokens, sketch_map, test_matrix)
    ]
    tokens, pieces = held[0], []
    for stream in range(2):
        operands = (tokens, *held[1:]) if not stream else (tokens,)
        with jax.named_scope("products_%d" % stream):
            keep, send = local_products(pack, stream, width, tokens_dev, k)(*operands)
            if stream:
                send, arrived = lax.optimization_barrier((send, arrived))
                pieces.append(jnp.sum(arrived, axis=0))
        with jax.named_scope("over_core_%d" % stream):
            half = keep + lax.ppermute(send, "c", swap)
            if not stream:
                tokens, half = lax.optimization_barrier((tokens, half))
        with jax.named_scope("over_xy_%d" % stream):
            tiles = half.reshape(plane, pack.rows[stream] // 2 // plane, LANES)
            arrived = lax.all_to_all(tiles, ("x", "y"), 0, 0, tiled=True)
    pieces.append(jnp.sum(arrived, axis=0))
    with jax.named_scope("over_z"):
        piece = jnp.sum(to_all(jnp.concatenate(pieces, axis=0), "z"), axis=0)
    cut = pieces[0].shape[0]
    with jax.named_scope("back_0"):
        mine_0 = to_all(piece[:cut], ("x", "y"))
        mine_0, later = lax.optimization_barrier((mine_0, piece[cut:]))
        mine_0 = mine_0.reshape(-1, LANES)
    with jax.named_scope("back_1"):
        mine_1 = to_all(later, ("x", "y")).reshape(-1, LANES)
    with jax.named_scope("first_basis"):
        other_0 = lax.ppermute(mine_0, "c", swap)
        first = first_basis(pack, width, k)(mine_0, other_0)
    with jax.named_scope("refine"):
        mine_1, first = lax.optimization_barrier((mine_1, first))
        other_1 = lax.ppermute(mine_1, "c", swap)
        return refine(pack, width, k, strip, total_tokens)(
            mine_0, other_0, mine_1, other_1, first
        )


def solution(mesh):
    finer = Mesh(mesh.devices.reshape(4, 8, 2, mesh.shape["rep"]), ALL)
    return jax.shard_map(
        body,
        mesh=finer,
        in_specs=(P(ALL, None), P(ALL, None), P("y", None, None)),
        out_specs=(P(("x", "z", "c"), None), P()),
        check_vma=False,
    )
```

time: 148 us -> 163 us (1.10)
  blocking collectives: 91.7 us -> 33.2 us
  waiting for transfers between devices: 7.39 us -> 53.2 us
  starting transfers between devices: 8.58 us -> 31.1 us
  local copies, waits for them, and re-layouts: 0.2 us -> 4.11 us
  other arithmetic: 0.36 us -> 2.3 us
  Pallas kernels: 39.2 us -> 37.5 us
    all_to_all x3 -> x1, blocking collectives: 91.7 us -> 33.2 us  [to_all(): return lax.all_to_all(copies, axes, 0, 0, tiled=True)]
    all_to_all x0 -> x4, waiting for transfers between devices: none -> 46.5 us  [the longest x2 24.8 us: body(): arrived = lax.all_to_all(tiles, ('x', 'y'), 0, 0, tiled=True)]
    all_to_all x0 -> x4, starting transfers between devices: none -> 16.8 us  [the longest x2 8.66 us: body(): arrived = lax.all_to_all(tiles, ('x', 'y'), 0, 0, tiled=True)]
    ppermute x1 -> x2, starting transfers between devices: 3.35 us -> 7.09 us  [body(): half = keep + lax.ppermute(send, 'c', swap)]
    ppermute x1 -> x2, starting transfers between devices: 5.23 us -> 7.2 us  [the longest x1 6.12 us: body(): other_0 = lax.ppermute(mine_0, 'c', swap)]
    unnamed x0 -> x4, local copies, waits for them, and re-layouts: none -> 1.95 us
    broadcast_in_dim x2 -> x3, local copies, waits for them, and re-layouts: 0.2 us -> 2.15 us  [to_all(): copies = jnp.broadcast_to(piece, (lax.axis_size(axes), *piece.shape))]
    add x1 -> x2, other arithmetic: 0.21 us -> 2.12 us  [body(): half = keep + lax.ppermute(send, 'c', swap)]
  transfers between devices with their start and end apart: 2 -> 8, of which waited for: 2 -> 7; matrix products, arithmetic and copies ran while one was open for 0% -> 1% of each run, Pallas kernels for 0% -> 8%
where the time goes in v3:
time: 163 us; the launch traced here: 162 us
  waiting for transfers between devices  53.2 us (33%)
  Pallas kernels  37.5 us (23%)
  blocking collectives  33.2 us (20%)
  starting transfers between devices  31.1 us (19%)
  local copies, waits for them, and re-layouts  4.11 us (3%)
  other arithmetic  2.3 us (1%)
    all_to_all x1, blocking collectives, to_all(): return lax.all_to_all(copies, axes, 0, 0, tiled=True)  33.2 us
    all_to_all x2, waiting for transfers between devices, body(): arrived = lax.all_to_all(tiles, ('x', 'y'), 0, 0, tiled=True)  24.8 us
    all_to_all x2, waiting for transfers between devices, to_all(): return lax.all_to_all(copies, axes, 0, 0, tiled=True)  21.7 us
    pallas_call x1, Pallas kernels, body(): refine(pack, width, k, strip, total_tokens)  19.3 us
    pallas_call x2, Pallas kernels, body(): keep, send = local_products(pack, stream, width, tokens_dev, k)(*operands)  11.8 us
    all_to_all x2, starting transfers between devices, body(): arrived = lax.all_to_all(tiles, ('x', 'y'), 0, 0, tiled=True)  8.66 us
    all_to_all x2, starting transfers between devices, to_all(): return lax.all_to_all(copies, axes, 0, 0, tiled=True)  8.16 us
    ppermute x2, starting transfers between devices, body(): half = keep + lax.ppermute(send, 'c', swap)  7.09 us
  transfers between devices with their start and end apart: 8, of which 7 were waited for; matrix products, arithmetic and copies ran while one was open for 1% of the time, Pallas kernels for 8%

profile of v3, /device:TPU:1, one launch (start us, length us, event | category | flops | bytes accessed | tf_op | source)
XLA Modules:
  0.0 162.3 jit_solution(7977379657571668601)
XLA Ops:
  0.6 6.0 %products_stream_0.1 = (f32[2048,128]{1,0:T(8,128)S(1)}, f32[2048,128]{1,0:T(8,128)S(1)}) custom-call(bf16[2048,1280]{1,0:T(8,128)(2,1)} %tok_hbm.2, bf16[2048,128]{1,0:T(8,128)(2,1)} %smap_hbm.1, bf16[1,8192,128]{2,1,0:T(8,128)(2,1)} %test_hbm.1), custom_call_target="tpu_custom_call" | custom-call | flops 2147483648 | bytes 7340032 | tf_op jit(solution)/shard_map/products_0/products_stream_0/pallas_call | solution.py:362
  6.6 3.3 %collective-permute-start = (f32[2048,128]{1,0:T(8,128)S(1)}, f32[2048,128]{1,0:T(8,128)S(1)}, u32[]{:S(2)}, u32[]{:S(2)}) collective-permute-start(f32[2048,128]{1,0:T(8,128)S(1)} %get-tuple-element.15), channel_id=1, source_target_pairs={{0,4},{4,0},{1,5},{5,1},{2,6},{6,2},{3,7},{7,3},{8,12},{12,8},{9,1... | collective-permute-start | bytes 3145736 | tf_op jit(solution)/shard_map/over_core_0/ppermute | solution.py:367
  10.0 2.3 %collective-permute-done = f32[2048,128]{1,0:T(8,128)S(1)} collective-permute-done((f32[2048,128]{1,0:T(8,128)S(1)}, f32[2048,128]{1,0:T(8,128)S(1)}, u32[]{:S(2)}, u32[]{:S(2)}) %collective-permute-start) | collective-permute-done | bytes 1048608 | tf_op jit(solution)/shard_map/over_core_0/ppermute | solution.py:367
  12.3 1.1 add.6
  13.3 5.0 %all-to-all-start = ((f32[16,128,128]{2,1,0:T(8,128)}), f32[16,128,128]{2,1,0:T(8,128)S(1)}, u32[]{:S(2)}, u32[]{:S(2)}) async-start(f32[16,128,128]{2,1,0:T(8,128)} %bitcast), calls=%async_computation | async-start | bytes 2097152 | tf_op jit(solution)/shard_map/over_xy_0/all_to_all | solution.py:372
  18.4 5.8 %products_stream_1.1 = (f32[1920,128]{1,0:T(8,128)S(1)}, f32[1920,128]{1,0:T(8,128)S(1)}) custom-call(bf16[2048,1280]{1,0:T(8,128)(2,1)} %tok_hbm.2), custom_call_target="tpu_custom_call" | custom-call | flops 2013265920 | bytes 7208960 | tf_op jit(solution)/shard_map/products_1/products_stream_1/pallas_call | solution.py:362
  24.2 9.2 %all-to-all-done = f32[16,128,128]{2,1,0:T(8,128)S(1)} async-done(((f32[16,128,128]{2,1,0:T(8,128)}), f32[16,128,128]{2,1,0:T(8,128)S(1)}, u32[]{:S(2)}, u32[]{:S(2)}) %all-to-all-start) | async-done | bytes 1048608 | tf_op jit(solution)/shard_map/over_xy_0/all_to_all | solution.py:372
  33.4 3.8 %collective-permute-start.1 = (f32[1920,128]{1,0:T(8,128)S(1)}, f32[1920,128]{1,0:T(8,128)S(1)}, u32[]{:S(2)}, u32[]{:S(2)}) collective-permute-start(f32[1920,128]{1,0:T(8,128)S(1)} %get-tuple-element.21), channel_id=1, source_target_pairs={{0,4},{4,0},{1,5},{5,1},{2,6},{6,2},{3,7},{7,3},{8,12},{12,8},{9,1... | collective-permute-start | bytes 2949128 | tf_op jit(solution)/shard_map/over_core_1/ppermute | solution.py:367
  37.1 2.2 %collective-permute-done.1 = f32[1920,128]{1,0:T(8,128)S(1)} collective-permute-done((f32[1920,128]{1,0:T(8,128)S(1)}, f32[1920,128]{1,0:T(8,128)S(1)}, u32[]{:S(2)}, u32[]{:S(2)}) %collective-permute-start.1) | collective-permute-done | bytes 983072 | tf_op jit(solution)/shard_map/over_core_1/ppermute | solution.py:367
  39.3 1.0 add.7
  40.4 3.6 %all-to-all-start.1 = ((f32[16,120,128]{2,1,0:T(8,128)}), f32[16,120,128]{2,1,0:T(8,128)S(1)}, u32[]{:S(2)}, u32[]{:S(2)}) async-start(f32[16,120,128]{2,1,0:T(8,128)} %bitcast.1), calls=%async_computation.1 | async-start | bytes 1966080 | tf_op jit(solution)/shard_map/over_xy_1/all_to_all | solution.py:372
  44.0 0.1 reduce_sum.27
  44.1 15.6 %all-to-all-done.1 = f32[16,120,128]{2,1,0:T(8,128)S(1)} async-done(((f32[16,120,128]{2,1,0:T(8,128)}), f32[16,120,128]{2,1,0:T(8,128)S(1)}, u32[]{:S(2)}, u32[]{:S(2)}) %all-to-all-start.1) | async-done | bytes 983072 | tf_op jit(solution)/shard_map/over_xy_1/all_to_all | solution.py:372
  59.7 0.1 reduce_sum.28
  59.8 0.1 broadcast_in_dim.9
  59.9 33.2 %all_to_all.25 = f32[8,248,128]{2,1,0:T(8,128)S(1)} all-to-all(f32[8,248,128]{2,1,0:T(8,128)S(1)} %broadcast_in_dim.9), channel_id=1, replica_groups=mesh['x'=4,'z'=8,'c'=2,'y'=4] {'z'}, dimensions={0} | all-to-all | bytes 2031616 | tf_op jit(solution)/shard_map/over_z/all_to_all | solution.py:343
  93.0 0.1 reduce_sum.29
  93.1 1.1 broadcast_in_dim.10
  94.2 4.5 %all-to-all-start.3 = ((f32[16,128,128]{2,1,0:T(8,128)}), f32[16,128,128]{2,1,0:T(8,128)S(1)}, u32[]{:S(2)}, u32[]{:S(2)}) async-start(f32[16,128,128]{2,1,0:T(8,128)} %broadcast_in_dim.10), calls=%async_computation.3 | async-start | bytes 2097152 | tf_op jit(solution)/shard_map/back_0/all_to_all | solution.py:343
  98.7 11.9 %all-to-all-done.3 = f32[16,128,128]{2,1,0:T(8,128)S(1)} async-done(((f32[16,128,128]{2,1,0:T(8,128)}), f32[16,128,128]{2,1,0:T(8,128)S(1)}, u32[]{:S(2)}, u32[]{:S(2)}) %all-to-all-start.3) | async-done | bytes 1048608 | tf_op jit(solution)/shard_map/back_0/all_to_all | solution.py:343
  110.6 6.1 %collective-permute-start.2 = (f32[2048,128]{1,0:T(8,128)S(1)}, f32[2048,128]{1,0:T(8,128)S(1)}, u32[]{:S(2)}, u32[]{:S(2)}) collective-permute-start(f32[2048,128]{1,0:T(8,128)S(1)} %bitcast.4), channel_id=1, source_target_pairs={{0,4},{4,0},{1,5},{5,1},{2,6},{6,2},{3,7},{7,3},{8,12},{12,8},{9,1... | collective-permute-start | bytes 3145736 | tf_op jit(solution)/shard_map/first_basis/ppermute | solution.py:384
  116.8 1.0 broadcast_in_dim.11
  117.8 3.6 %all-to-all-start.4 = ((f32[16,120,128]{2,1,0:T(8,128)}), f32[16,120,128]{2,1,0:T(8,128)S(1)}, u32[]{:S(2)}, u32[]{:S(2)}) async-start(f32[16,120,128]{2,1,0:T(8,128)} %broadcast_in_dim.11), calls=%async_computation.4 | async-start | bytes 1966080 | tf_op jit(solution)/shard_map/back_1/all_to_all | solution.py:343
  121.4 0.0 collective-permute-done.2.other.other_0
  121.4 6.4 %first_basis.1.first = f32[128,1280]{1,0:T(8,128)S(1)} custom-call(f32[2048,128]{1,0:T(8,128)S(1)} %bitcast.5, f32[2048,128]{1,0:T(8,128)S(1)} %collective-permute-done.2.other.other_0), custom_call_target="tpu_custom_call" | custom-call | flops 8388608000 | bytes 1310720 | tf_op jit(solution)/shard_map/first_basis/first_basis/pallas_call | solution.py:385
  127.8 0.0 copy-start
  127.8 0.9 copy-done
  128.7 9.8 %all-to-all-done.4 = f32[16,120,128]{2,1,0:T(8,128)S(1)} async-done(((f32[16,120,128]{2,1,0:T(8,128)}), f32[16,120,128]{2,1,0:T(8,128)S(1)}, u32[]{:S(2)}, u32[]{:S(2)}) %all-to-all-start.4) | async-done | bytes 983072 | tf_op jit(solution)/shard_map/back_1/all_to_all | solution.py:343
  138.5 1.1 collective-permute-start.3
  139.5 2.2 %collective-permute-done.3.other_1 = f32[1920,128]{1,0:T(8,128)S(1)} collective-permute-done((f32[1920,128]{1,0:T(8,128)S(1)}, f32[1920,128]{1,0:T(8,128)S(1)}, u32[]{:S(2)}, u32[]{:S(2)}) %collective-permute-start.3) | collective-permute-done | bytes 983072 | tf_op jit(solution)/shard_map/refine/ppermute | solution.py:388
  141.7 0.0 copy-start.1
  141.7 1.1 copy-done.1
  142.8 19.3 %refine.1 = (f32[20,128]{1,0:T(8,128)}, f32[128,128]{1,0:T(8,128)}) custom-call(f32[2048,128]{1,0:T(8,128)S(1)} %bitcast.6, f32[2048,128]{1,0:T(8,128)S(1)} %collective-permute-done.2.other.other_0, f32[1920,128]{1,0:T(8,128)S(1)} %bitcast.8, f32[1920,128]{1,0:T(8,128)S(1)} %collective-permute-done.3.other_1, f32[128,1280]{1,0:T(8,128)S(1)} %copy-done.1), custom_call_target="tpu_custom_call" | custom-call | tf_op jit(solution)/shard_map/refine/refine/pallas_call | solution.py:389
  (3 shorter events, 0.0 us)
Async XLA Ops:
  6.6 5.6 %collective-permute-start = (f32[2048,128]{1,0:T(8,128)S(1)}, f32[2048,128]{1,0:T(8,128)S(1)}, u32[]{:S(2)}, u32[]{:S(2)}) collective-permute-start(f32[2048,128]{1,0:T(8,128)S(1)} %get-tuple-element.15), channel_id=1, source_target_pairs={{0,4},{4,0},{1,5},{5,1},{2,6},{6,2},{3,7},{7,3},{8,12},{12,8},{9,1... | collective-permute-start | bytes 3145736 | tf_op jit(solution)/shard_map/over_core_0/ppermute | solution.py:367
  13.3 20.0 %all-to-all-start = ((f32[16,128,128]{2,1,0:T(8,128)}), f32[16,128,128]{2,1,0:T(8,128)S(1)}, u32[]{:S(2)}, u32[]{:S(2)}) async-start(f32[16,128,128]{2,1,0:T(8,128)} %bitcast), calls=%async_computation | async-start | bytes 2097152 | tf_op jit(solution)/shard_map/over_xy_0/all_to_all | solution.py:372
  33.4 5.9 %collective-permute-start.1 = (f32[1920,128]{1,0:T(8,128)S(1)}, f32[1920,128]{1,0:T(8,128)S(1)}, u32[]{:S(2)}, u32[]{:S(2)}) collective-permute-start(f32[1920,128]{1,0:T(8,128)S(1)} %get-tuple-element.21), channel_id=1, source_target_pairs={{0,4},{4,0},{1,5},{5,1},{2,6},{6,2},{3,7},{7,3},{8,12},{12,8},{9,1... | collective-permute-start | bytes 2949128 | tf_op jit(solution)/shard_map/over_core_1/ppermute | solution.py:367
  40.4 19.3 %all-to-all-start.1 = ((f32[16,120,128]{2,1,0:T(8,128)}), f32[16,120,128]{2,1,0:T(8,128)S(1)}, u32[]{:S(2)}, u32[]{:S(2)}) async-start(f32[16,120,128]{2,1,0:T(8,128)} %bitcast.1), calls=%async_computation.1 | async-start | bytes 1966080 | tf_op jit(solution)/shard_map/over_xy_1/all_to_all | solution.py:372
  94.2 16.5 %all-to-all-start.3 = ((f32[16,128,128]{2,1,0:T(8,128)}), f32[16,128,128]{2,1,0:T(8,128)S(1)}, u32[]{:S(2)}, u32[]{:S(2)}) async-start(f32[16,128,128]{2,1,0:T(8,128)} %broadcast_in_dim.10), calls=%async_computation.3 | async-start | bytes 2097152 | tf_op jit(solution)/shard_map/back_0/all_to_all | solution.py:343
  110.6 10.8 %collective-permute-start.2 = (f32[2048,128]{1,0:T(8,128)S(1)}, f32[2048,128]{1,0:T(8,128)S(1)}, u32[]{:S(2)}, u32[]{:S(2)}) collective-permute-start(f32[2048,128]{1,0:T(8,128)S(1)} %bitcast.4), channel_id=1, source_target_pairs={{0,4},{4,0},{1,5},{5,1},{2,6},{6,2},{3,7},{7,3},{8,12},{12,8},{9,1... | collective-permute-start | bytes 3145736 | tf_op jit(solution)/shard_map/first_basis/ppermute | solution.py:384
  117.8 20.7 %all-to-all-start.4 = ((f32[16,120,128]{2,1,0:T(8,128)}), f32[16,120,128]{2,1,0:T(8,128)S(1)}, u32[]{:S(2)}, u32[]{:S(2)}) async-start(f32[16,120,128]{2,1,0:T(8,128)} %broadcast_in_dim.11), calls=%async_computation.4 | async-start | bytes 1966080 | tf_op jit(solution)/shard_map/back_1/all_to_all | solution.py:343
  127.8 0.9 copy-start
  138.5 3.3 %collective-permute-start.3 = (f32[1920,128]{1,0:T(8,128)S(1)}, f32[1920,128]{1,0:T(8,128)S(1)}, u32[]{:S(2)}, u32[]{:S(2)}) collective-permute-start(f32[1920,128]{1,0:T(8,128)S(1)} %bitcast.7), channel_id=1, source_target_pairs={{0,4},{4,0},{1,5},{5,1},{2,6},{6,2},{3,7},{7,3},{8,12},{12,8},{9,1... | collective-permute-start | bytes 2949128 | tf_op jit(solution)/shard_map/refine/ppermute | solution.py:388
  141.7 1.1 copy-start.1

commit v4 on v2

v4 whole, which is shorter than its diff:
```python
import jax
import jax.numpy as jnp
from jax import lax
from jax.experimental import pallas as pl
from jax.experimental.pallas import tpu as pltpu
from jax.sharding import Mesh
from jax.sharding import PartitionSpec as P

ITERS = 2
ALL = ("x", "z", "c", "y")
LANES = 128
SUB = 8
PACKED = 16
MIB = 1024 * 1024
F32 = jnp.float32
BF16 = jnp.bfloat16
HI = lax.Precision.HIGHEST
NN = (((1,), (0,)), ((), ()))
NT = (((1,), (1,)), ((), ()))
TN = (((0,), (0,)), ((), ()))
ROUNDING = 2.0**-9
ALLOWED = 1.0e-3


class Packing:
    def __init__(self, width, pieces):
        self.n = width // LANES
        self.pieces = pieces
        count = self.n // 2
        self.pairs = list(range(count - 1, -1, -1))
        self.diagonal = self.n * LANES
        step = pieces * PACKED
        self.exact_rows = -(-(self.diagonal + self.n) // step) * step
        self.offset = {}
        at = 0
        for pair in self.pairs:
            left, right = 2 * pair, 2 * pair + 1
            for j in (left, right):
                for i in range(j):
                    self.offset[i, j] = at
                    at += LANES
            self.offset[left, left] = at
            at += LANES
        self.used = at
        self.cov_rows = -(-at // step) * step
        self.exact = self.exact_rows // pieces
        self.cov = self.cov_rows // pieces
        self.piece = 2 * self.exact + self.cov


def local_products(pack, width, tokens_dev, k):
    chunks = 4
    part = tokens_dev // chunks
    exact_half = pack.exact_rows // 2
    cov_half = pack.cov_rows // 2

    def kernel(
        tok_hbm, smap_hbm, test_hbm, keep_exact, keep_cov, send_exact, send_cov,
        tok, smap, test, exact, cov, rounded, sem, out_sem,
    ):
        core = lax.axis_index("c")
        slab = lax.axis_index(("x", "z", "c"))
        load_map = pltpu.make_async_copy(smap_hbm, smap, sem.at[chunks])
        load_test = pltpu.make_async_copy(
            test_hbm.at[0, pl.ds(pl.multiple_of(slab * k, k), k)], test, sem.at[chunks + 1]
        )
        loads = []
        for s in range(chunks):
            rows = pl.ds(s * part, part)
            loads.append(pltpu.make_async_copy(tok_hbm.at[rows], tok.at[rows], sem.at[s]))
        load_map.start()
        for load in loads:
            load.start()
        load_test.start()
        load_map.wait()
        sketch = jnp.zeros((k, width), F32)
        for s in range(chunks):
            loads[s].wait()
            rows = slice(s * part, (s + 1) * part)
            sketch = sketch + lax.dot_general(
                smap[rows, :], tok[rows, :], TN, preferred_element_type=F32
            )
        load_test.wait()
        start = lax.dot_general(test[...], sketch.astype(BF16), TN, preferred_element_type=F32)
        for i in range(pack.n):
            at = i * LANES
            exact[at : at + LANES, :] = start[:, at : at + LANES]
        exact[pack.diagonal :, :] = jnp.zeros((pack.exact_rows - pack.diagonal, LANES), F32)
        if pack.used < pack.cov_rows:
            cov[pack.used :, :] = jnp.zeros((pack.cov_rows - pack.used, LANES), F32)
        row = lax.broadcasted_iota(jnp.int32, (LANES, LANES), 0)
        col = lax.broadcasted_iota(jnp.int32, (LANES, LANES), 1)
        for pair in pack.pairs:
            base = 2 * pair * LANES
            high = base + 2 * LANES
            out = lax.dot_general(tok[:, :high], tok[:, base:high], TN, preferred_element_type=F32)
            for j in range(2):
                for i in range(2 * pair + j):
                    at = pack.offset[i, 2 * pair + j]
                    cov[at : at + LANES, :] = out[
                        i * LANES : (i + 1) * LANES, j * LANES : (j + 1) * LANES
                    ]
            upper = out[base : base + LANES, :LANES]
            lower = out[base + LANES : high, LANES:]
            at = pack.offset[2 * pair, 2 * pair]
            both = jnp.where(row < col, upper, lower)
            cov[at : at + LANES, :] = jnp.where(row == col, 0.0, both)
            for b, own in ((2 * pair, upper), (2 * pair + 1, lower)):
                line = jnp.sum(jnp.where(row == col, own, 0.0), axis=0)[None, :]
                exact[pack.diagonal + b : pack.diagonal + b + 1, :] = line
        away = 1 - core
        rounded[...] = cov[pl.ds(pl.multiple_of(away * cov_half, LANES), cov_half), :].astype(BF16)
        outs = []
        for from_ref, to in (
            (rounded, send_cov),
            (exact.at[pl.ds(pl.multiple_of(away * exact_half, LANES), exact_half)], send_exact),
            (exact.at[pl.ds(pl.multiple_of(core * exact_half, LANES), exact_half)], keep_exact),
            (cov.at[pl.ds(pl.multiple_of(core * cov_half, LANES), cov_half)], keep_cov),
        ):
            outs.append(pltpu.make_async_copy(from_ref, to, out_sem.at[len(outs)]))
        for copy in outs:
            copy.start()
        for copy in outs:
            copy.wait()

    return pl.pallas_call(
        kernel,
        out_shape=(
            jax.ShapeDtypeStruct((exact_half, LANES), F32),
            jax.ShapeDtypeStruct((cov_half, LANES), F32),
            jax.ShapeDtypeStruct((exact_half, LANES), F32),
            jax.ShapeDtypeStruct((cov_half, LANES), BF16),
        ),
        in_specs=[pl.BlockSpec(memory_space=pl.ANY)] * 3,
        out_specs=[pl.BlockSpec(memory_space=pl.ANY)] * 4,
        scratch_shapes=[
            pltpu.VMEM((tokens_dev, width), BF16),
            pltpu.VMEM((tokens_dev, k), BF16),
            pltpu.VMEM((k, k), BF16),
            pltpu.VMEM((pack.exact_rows, LANES), F32),
            pltpu.VMEM((pack.cov_rows, LANES), F32),
            pltpu.VMEM((cov_half, LANES), BF16),
            pltpu.SemaphoreType.DMA((chunks + 2,)),
            pltpu.SemaphoreType.DMA((4,)),
        ],
        compiler_params=pltpu.CompilerParams(vmem_limit_bytes=24 * MIB),
        name="local_products",
    )


def eliminate(gram):
    k = gram.shape[0]
    blocks = k // SUB
    lane = lax.broadcasted_iota(jnp.int32, (SUB, k), 1)
    row = lax.broadcasted_iota(jnp.int32, (SUB, k), 0)
    work, trace = [], []
    for b in range(blocks):
        work.append(gram[b * SUB : (b + 1) * SUB, :])
        trace.append(jnp.where(lane == row + b * SUB, 1.0, 0.0).astype(F32))
    factor, inverse = [], []
    for b in range(blocks):
        at = b * SUB
        spread = {}
        for o in range(b, blocks):
            for q in range(SUB):
                spread[o, q] = jnp.broadcast_to(work[o][:, at + q : at + q + 1], (SUB, k))
        d = {(p, q): spread[b, q][p : p + 1, :] for p in range(SUB) for q in range(p, SUB)}
        scale = []
        for p in range(SUB):
            scale.append(lax.rsqrt(d[p, p]))
            for q in range(p + 1, SUB):
                d[p, q] = d[p, q] * scale[p]
            for q in range(p + 1, SUB):
                for s in range(q, SUB):
                    d[q, s] = d[q, s] - d[p, q] * d[p, s]
        ra = [work[b][p : p + 1, :] for p in range(SUB)]
        re = [trace[b][p : p + 1, :] for p in range(SUB)]
        for p in range(SUB):
            ra[p] = ra[p] * scale[p]
            re[p] = re[p] * scale[p]
            for q in range(p + 1, SUB):
                ra[q] = ra[q] - d[p, q] * ra[p]
                re[q] = re[q] - d[p, q] * re[p]
        for o in range(b + 1, blocks):
            column = [spread[o, q] for q in range(SUB)]
            for p in range(SUB):
                column[p] = column[p] * scale[p]
                for q in range(p + 1, SUB):
                    column[q] = column[q] - d[p, q] * column[p]
                work[o] = work[o] - column[p] * ra[p]
                trace[o] = trace[o] - column[p] * re[p]
        factor.append(jnp.where(lane >= row + at, jnp.concatenate(ra, axis=0), 0.0))
        inverse.append(jnp.concatenate(re, axis=0))
    return jnp.concatenate(factor, axis=0), jnp.concatenate(inverse, axis=0)


def orthonormal(pt):
    gram = lax.dot_general(pt, pt, NT, precision=HI, preferred_element_type=F32)
    factor, inverse = eliminate(gram)
    return jnp.dot(inverse, pt, precision=HI, preferred_element_type=F32), factor, inverse


def packed_rows(ref, begin, count, length):
    found = []
    at = begin
    while at < begin + count:
        piece, row = at // length, at % length
        take = min(length - row, begin + count - at)
        found.append(ref[piece, row : row + take, :])
        at += take
    return found[0] if len(found) == 1 else jnp.concatenate(found, axis=0)


def refine(pack, width, k, strip, total_tokens):
    n = pack.n
    half = pack.pieces // 2

    def kernel(
        mine, other, basis, factor_out, first_out, error_out,
        value, rest, cov, dense, squares, zt, vt, turned, sem,
    ):
        core = lax.axis_index("c")
        slab = lax.axis_index(("x", "z", "c"))
        exact_at = pl.ds(0, pack.exact)
        rest_at = pl.ds(pack.exact, pack.exact)
        cov_at = pl.ds(2 * pack.exact, pack.cov)
        loads = []
        for side, home in ((mine, core), (other, 1 - core)):
            place = pl.ds(home * half, half)
            for rows, to in ((exact_at, value), (rest_at, rest), (cov_at, cov)):
                loads.append(
                    pltpu.make_async_copy(side.at[:, rows], to.at[place], sem.at[len(loads)])
                )
        for load in loads:
            load.start()
        for at in (0, 1, 3, 4):
            loads[at].wait()

        def exact_rows(begin, count):
            return packed_rows(value, begin, count, pack.exact).astype(F32) + packed_rows(
                rest, begin, count, pack.exact
            ).astype(F32)

        for i in range(n):
            zt[:, i * LANES : (i + 1) * LANES] = exact_rows(i * LANES, LANES)
        lines = exact_rows(pack.diagonal, PACKED)
        diagonal = jnp.concatenate([lines[i : i + 1, :] for i in range(n)], axis=1)

        def unpack():
            row = lax.broadcasted_iota(jnp.int32, (LANES, LANES), 0)
            col = lax.broadcasted_iota(jnp.int32, (LANES, LANES), 1)
            sums = [jnp.zeros((1, LANES), F32) for _ in range(n)]

            def put(i, j, v):
                dense[i * LANES : (i + 1) * LANES, j * LANES : (j + 1) * LANES] = v.astype(BF16)
                square = v * v
                sums[j] = sums[j] + jnp.sum(square, axis=0)[None, :]
                if i != j:
                    across = jnp.sum(square, axis=1, keepdims=True)
                    sums[i] = sums[i] + across.T

            for (i, j), at in pack.offset.items():
                v = packed_rows(cov, at, LANES, pack.cov).astype(F32)
                if i < j:
                    put(i, j, v)
                else:
                    flipped = v.T
                    put(i, i, jnp.where(row < col, v, flipped))
                    put(i + 1, i + 1, jnp.where(row > col, v, flipped))
            squares[...] = jnp.concatenate(sums, axis=1)

        error_out[...] = jnp.zeros(error_out.shape, F32)

        @pl.loop(0, ITERS + 1)
        def _(step):
            fresh, factor, inverse = orthonormal(zt[...])
            factor_out[...] = factor

            @pl.when(step == 0)
            def _():
                first_out[...] = fresh
                for at in (2, 5):
                    loads[at].wait()
                unpack()

            @pl.when(step > 0)
            def _():
                back = jnp.dot(inverse, vt[...], precision=HI, preferred_element_type=F32)
                share = (squares[...] * (1.0 / total_tokens) ** 2) * (back * back)
                line = jnp.sum(share, axis=0)[None, :]
                total = jnp.sum(line, axis=1, keepdims=True) * (ROUNDING**2 / k)
                error_out[...] = error_out[...] + jnp.broadcast_to(total, error_out.shape)

            vt[...] = fresh

            @pl.when(step < ITERS)
            def _():
                vb = fresh.astype(BF16)
                for j in range(n):
                    high = (j + 1) * LANES
                    rj = slice(j * LANES, high)
                    z = vb[:, rj].astype(F32) * diagonal[:, rj]
                    z = z + lax.dot_general(
                        vb[:, :high], dense[:high, rj], NN, preferred_element_type=F32
                    )
                    if j + 1 < n:
                        z = z + lax.dot_general(
                            vb[:, high:], dense[rj, high:], NT, preferred_element_type=F32
                        )
                    zt[:, rj] = z * (1.0 / total_tokens)

        for i in range(n):
            cols = slice(i * LANES, (i + 1) * LANES)
            turned[cols, :] = vt[:, cols].T
        basis[...] = turned[pl.ds(slab * strip, strip), :]

    return pl.pallas_call(
        kernel,
        out_shape=(
            jax.ShapeDtypeStruct((strip, k), F32),
            jax.ShapeDtypeStruct((k, k), F32),
            jax.ShapeDtypeStruct((k, width), F32),
            jax.ShapeDtypeStruct((SUB, LANES), F32),
        ),
        in_specs=[pl.BlockSpec(memory_space=pl.ANY)] * 2,
        out_specs=[pl.BlockSpec(memory_space=pltpu.VMEM)] * 4,
        scratch_shapes=[
            pltpu.VMEM((pack.pieces, pack.exact, LANES), BF16),
            pltpu.VMEM((pack.pieces, pack.exact, LANES), BF16),
            pltpu.VMEM((pack.pieces, pack.cov, LANES), BF16),
            pltpu.VMEM((width, width), BF16),
            pltpu.VMEM((1, width), F32),
            pltpu.VMEM((k, width), F32),
            pltpu.VMEM((k, width), F32),
            pltpu.VMEM((width, k), F32),
            pltpu.SemaphoreType.DMA((6,)),
        ],
        compiler_params=pltpu.CompilerParams(vmem_limit_bytes=28 * MIB),
        name="refine",
    )


def orthonormal_rows(zt):
    def kernel(zt_ref, vt_ref, factor_ref):
        vt, factor, _ = orthonormal(zt_ref[...])
        vt_ref[...] = vt
        factor_ref[...] = factor

    k = zt.shape[0]
    return pl.pallas_call(
        kernel,
        out_shape=(jax.ShapeDtypeStruct(zt.shape, F32), jax.ShapeDtypeStruct((k, k), F32)),
        compiler_params=pltpu.CompilerParams(vmem_limit_bytes=8 * MIB),
        name="orthonormal_rows",
    )(zt)


def direct(tokens, first, strip, total_tokens):
    k = first.shape[0]

    def step(_, state):
        vb = state[0].astype(BF16)
        projected = lax.dot_general(tokens, vb, NT, preferred_element_type=F32).astype(BF16)
        local = lax.dot_general(projected, tokens, TN, preferred_element_type=F32)
        return orthonormal_rows(lax.psum(local, ALL) / total_tokens)

    vt, factor = lax.fori_loop(0, ITERS, step, (first, jnp.zeros((k, k), F32)))
    slab = lax.axis_index(("x", "z", "c"))
    return lax.dynamic_slice_in_dim(vt, slab * strip, strip, 1).T, factor


def to_all(piece, axes):
    copies = jnp.broadcast_to(piece, (lax.axis_size(axes), *piece.shape))
    return lax.all_to_all(copies, axes, 0, 0, tiled=True)


def sendable(exact, cov, pieces):
    value = lax.reduce_precision(exact, exponent_bits=8, mantissa_bits=7)
    parts = [value, exact - value, cov]
    tiles = [part.astype(BF16).reshape(pieces, -1, LANES) for part in parts]
    return jnp.concatenate(tiles, axis=1)


def summed(arrived, pack):
    total = jnp.sum(arrived.astype(F32), axis=0)
    exact = total[: pack.exact] + total[pack.exact : 2 * pack.exact]
    return sendable(exact, total[2 * pack.exact :], 1)[0]


def body(tokens, sketch_map, test_matrix):
    tokens_dev, width = tokens.shape
    k = sketch_map.shape[1]
    strip = width // lax.axis_size(("x", "z", "c"))
    total_tokens = tokens_dev * lax.axis_size(ALL)
    plane = lax.axis_size(("x", "y"))
    pack = Packing(width, 2 * plane)
    swap = [(0, 1), (1, 0)]
    with jax.named_scope("products"):
        held = [
            pltpu.with_memory_space_constraint(array, pltpu.HBM)
            for array in (tokens, sketch_map, test_matrix)
        ]
        keep_exact, keep_cov, send_exact, send_cov = local_products(pack, width, tokens_dev, k)(
            *held
        )
    with jax.named_scope("over_core"):
        exact = keep_exact + lax.ppermute(send_exact, "c", swap)
        cov = keep_cov + lax.ppermute(send_cov, "c", swap).astype(F32)
        tiles = sendable(exact, cov, plane)
    with jax.named_scope("over_xy"):
        piece = summed(lax.all_to_all(tiles, ("x", "y"), 0, 0, tiled=True), pack)
    with jax.named_scope("over_z"):
        piece = summed(to_all(piece, "z"), pack)
    with jax.named_scope("back_xy"):
        mine = to_all(piece, ("x", "y"))
    with jax.named_scope("back_core"):
        other = lax.ppermute(mine, "c", swap)
    with jax.named_scope("refine"):
        basis, factor, first, error = refine(pack, width, k, strip, total_tokens)(mine, other)
    with jax.named_scope("check"):
        return lax.cond(
            error[0, 0] <= ALLOWED**2,
            lambda: (basis, factor),
            lambda: direct(tokens, first, strip, total_tokens),
        )


def solution(mesh):
    finer = Mesh(mesh.devices.reshape(4, 8, 2, mesh.shape["rep"]), ALL)
    return jax.shard_map(
        body,
        mesh=finer,
        in_specs=(P(ALL, None), P(ALL, None), P("y", None, None)),
        out_specs=(P(("x", "z", "c"), None), P()),
        check_vma=False,
    )
```

time: 148 us -> 658 us (4.45)
  waiting for transfers between devices: 7.39 us -> 502 us
  blocking collectives: 91.7 us -> 66.3 us
  matrix products: 0 us -> 16.3 us
  between operations: 0.85 us -> 14.8 us
    psum x0 -> x2, waiting for transfers between devices: none -> 497 us  [step(): return orthonormal_rows(lax.psum(local, ALL) / total_tokens)]
    all_to_all x3, blocking collectives: 91.7 us -> 66.3 us  [the longest x2 43.4 us: to_all(): return lax.all_to_all(copies, axes, 0, 0, tiled=True)]
    dot_general x0 -> x2, matrix products: none -> 16.3 us  [step(): local = lax.dot_general(projected, tokens, TN, preferred_element_type=F32)]
    pallas_call x2 -> x4, Pallas kernels: 39.2 us -> 45.1 us  [the longest x1 24.4 us: body(): refine(pack, width, k, strip, total_tokens)(mine, other)]
  transfers between devices with their start and end apart: 2 -> 5, of which waited for: 2 -> 4; matrix products, arithmetic and copies ran while one was open for 0% -> 0% of each run, Pallas kernels for 0% -> 0%
where the time goes in v4:
time: 658 us
  waiting for transfers between devices  502 us (76%)
  blocking collectives  66.3 us (10%)
  Pallas kernels  45.1 us (7%)
  matrix products  16.3 us (2%)
  between operations  14.8 us (2%)
  starting transfers between devices  8.72 us (1%)
    psum x2, waiting for transfers between devices, step(): return orthonormal_rows(lax.psum(local, ALL) / total_tokens)  497 us
    all_to_all x2, blocking collectives, to_all(): return lax.all_to_all(copies, axes, 0, 0, tiled=True)  43.4 us
    pallas_call x1, Pallas kernels, body(): refine(pack, width, k, strip, total_tokens)(mine, other)  24.4 us
    all_to_all x1, blocking collectives, body(): piece = summed(lax.all_to_all(tiles, ('x', 'y'), 0, 0, tiled=True), pack)  22.9 us
    dot_general x2, matrix products, step(): local = lax.dot_general(projected, tokens, TN, preferred_element_type=F32)  16.3 us
  transfers between devices with their start and end apart: 5, of which 4 were waited for; matrix products, arithmetic and copies ran while one was open for 0% of the time, Pallas kernels for 0%

profile of v4, /device:TPU:1, one launch (start us, length us, event | category | flops | bytes accessed | tf_op | source)
XLA Modules:
  0.0 657.8 jit_solution(9235332752165114347)
XLA Ops:
  7.2 8.8 %local_products.1 = (f32[768,128]{1,0:T(8,128)S(1)}, f32[3328,128]{1,0:T(8,128)S(1)}, f32[768,128]{1,0:T(8,128)S(1)}, bf16[3328,128]{1,0:T(8,128)(2,1)S(1)}) custom-call(bf16[2048,1280]{1,0:T(8,128)(2,1)} %tok_hbm.1, bf16[2048,128]{1,0:T(8,128)(2,1)} %smap_hbm.1, bf16[1,8192,128]{2,1,0:T(8,128)(2,1)} %test_hbm.1), custom_call_target="tpu_custom_call" | custom-call | tf_op jit(solution)/shard_map/products/local_products/pallas_call | solution.py:403
  16.0 3.4 collective-permute-start.1
  19.4 0.1 collective-permute-start
  19.5 2.5 collective-permute-done
  21.9 0.1 reduce-precision_convert_fusion
  22.0 0.0 collective-permute-done.1
  22.0 0.2 add_convert_fusion
  22.3 0.1 pad_maximum_fusion
  22.3 22.9 %all_to_all.15 = bf16[16,304,128]{2,1,0:T(8,128)(2,1)S(1)} all-to-all(bf16[16,304,128]{2,1,0:T(8,128)(2,1)S(1)} %pad_maximum_fusion), channel_id=1, replica_groups=mesh['x'=4,'z'=8,'c'=2,'y'=4] {'x','y'}, dimensions={0} | all-to-all | bytes 2490368 | tf_op jit(solution)/shard_map/over_xy/all_to_all | solution.py:411
  45.3 0.2 convert_reduce_fusion
  45.5 0.1 broadcast_in_dim.6
  45.6 24.7 %all_to_all.16 = bf16[8,304,128]{2,1,0:T(8,128)(2,1)S(1)} all-to-all(bf16[8,304,128]{2,1,0:T(8,128)(2,1)S(1)} %broadcast_in_dim.6), channel_id=1, replica_groups=mesh['x'=4,'z'=8,'c'=2,'y'=4] {'z'}, dimensions={0} | all-to-all | bytes 1245184 | tf_op jit(solution)/shard_map/over_z/all_to_all | solution.py:374
  70.3 0.1 convert_reduce_fusion.1
  70.5 0.2 broadcast_in_dim.7
  70.6 18.6 %all_to_all.17.mine = bf16[16,304,128]{2,1,0:T(8,128)(2,1)S(1)} all-to-all(bf16[16,304,128]{2,1,0:T(8,128)(2,1)S(1)} %broadcast_in_dim.7), channel_id=1, replica_groups=mesh['x'=4,'z'=8,'c'=2,'y'=4] {'x','y'}, dimensions={0} | all-to-all | bytes 2490368 | tf_op jit(solution)/shard_map/back_xy/all_to_all | solution.py:374
  89.3 5.1 collective-permute-start.2
  94.4 2.6 collective-permute-done.2.other
  96.9 24.4 %refine.1 = (f32[20,128]{1,0:T(8,128)S(1)}, f32[128,128]{1,0:T(8,128)}, f32[128,1280]{1,0:T(8,128)S(1)}, f32[8,128]{1,0:T(8,128)S(1)}) custom-call(bf16[16,304,128]{2,1,0:T(8,128)(2,1)S(1)} %all_to_all.17.mine, bf16[16,304,128]{2,1,0:T(8,128)(2,1)S(1)} %collective-permute-done.2.other), custom_call_target="tpu_custom_call" | custom-call | tf_op jit(solution)/shard_map/refine/refine/pallas_call | solution.py:419
  121.4 0.5 slice.29
  122.5 527.8 %conditional.1 = (f32[128,128]{1,0:T(8,128)}, f32[20,128]{1,0:T(8,128)S(1)}) conditional(s32[]{:T(128)} %bitcast.12, (bf16[2048,1280]{1,0:T(8,128)(2,1)}, f32[128,1280]{1,0:T(8,128)S(1)}) %tuple.18, (f32[20,128]{1,0:T(8,128)S(1)}, f32[128,128]{1,0:T(8,128)}) %tuple.19), branch_computations={%region_2.0_spmd, %region_6.0_spmd} | conditional | flops 1342930944 | bytes 11837799 | solution.py:421
  122.8 527.4 %while.11 = (s32[]{:T(128)}, f32[128,1280]{1,0:T(8,128)S(1)}, f32[128,128]{1,0:T(8,128)}, bf16[2048,1280]{1,0:T(8,128)(2,1)}, s32[]{:T(128)}) while((s32[]{:T(128)}, f32[128,1280]{1,0:T(8,128)S(1)}, f32[128,128]{1,0:T(8,128)}, bf16[2048,1280]{1,0:T(8,128)(2,1)}, s32[]{:T(128)}) %tuple.39), condition=%wide.region_5.0_spmd, body=%wide.region_3.0_spmd.sunk | while | flops 1342930944 | bytes 11796581 | solution.py:367
  122.8 0.0 all-reduce.2.cloned.1.call-start
  122.8 8.1 %fusion.21 = f32[128,1280]{1,0:T(8,128)} fusion(bf16[2048,1280]{1,0:T(8,128)(2,1)} %get-tuple-element.118, f32[128,1280]{1,0:T(8,128)S(1)} %get-tuple-element.111), kind=kOutput, calls=%fused_computation.1.clone.1 | convolution fusion | flops 1342603264 | bytes 6553600 | tf_op jit(solution)/shard_map/check/cond/branch_0_fun/while/body/eval_jaxpr/dot_general | solution.py:364
  131.0 0.0 all-reduce.2.cloned.1.call-update
  131.0 246.5 %all-reduce.2.cloned.1.call-done = f32[128,1280]{1,0:T(8,128)} async-done(((f32[128,1280]{1,0:T(8,128)}), f32[128,1280]{1,0:T(8,128)}) %all-reduce.2.cloned.1.call-update) | async-done | bytes 655376 | tf_op jit(solution)/shard_map/check/cond/branch_0_fun/while/body/eval_jaxpr/psum | solution.py:365
  377.5 1.1 broadcast_multiply_fusion.2.zt_ref
  378.6 6.0 orthonormal_rows.1
  384.6 0.0 all-reduce.2.cloned.1.call-start
  384.7 8.1 %fusion.21 = f32[128,1280]{1,0:T(8,128)} fusion(bf16[2048,1280]{1,0:T(8,128)(2,1)} %get-tuple-element.118, f32[128,1280]{1,0:T(8,128)S(1)} %get-tuple-element.111), kind=kOutput, calls=%fused_computation.1.clone.1 | convolution fusion | flops 1342603264 | bytes 6553600 | tf_op jit(solution)/shard_map/check/cond/branch_0_fun/while/body/eval_jaxpr/dot_general | solution.py:364
  392.8 0.0 all-reduce.2.cloned.1.call-update
  392.8 250.2 %all-reduce.2.cloned.1.call-done = f32[128,1280]{1,0:T(8,128)} async-done(((f32[128,1280]{1,0:T(8,128)}), f32[128,1280]{1,0:T(8,128)}) %all-reduce.2.cloned.1.call-update) | async-done | bytes 655376 | tf_op jit(solution)/shard_map/check/cond/branch_0_fun/while/body/eval_jaxpr/psum | solution.py:365
  643.0 1.1 broadcast_multiply_fusion.2.zt_ref
  644.2 6.0 orthonormal_rows.1
  650.1 0.1 dynamic-slice_bitcast_fusion
  650.2 0.1 copy.11
  650.3 0.0 copy-start
  650.3 0.6 copy-done
  (7 shorter events, 0.1 us)
Async XLA Ops:
  16.0 6.1 collective-permute-start.1
  19.4 2.6 collective-permute-start
  89.3 7.7 %collective-permute-start.2 = (bf16[16,304,128]{2,1,0:T(8,128)(2,1)S(1)}, bf16[16,304,128]{2,1,0:T(8,128)(2,1)S(1)}, u32[]{:S(2)}, u32[]{:S(2)}) collective-permute-start(bf16[16,304,128]{2,1,0:T(8,128)(2,1)S(1)} %all_to_all.17.mine), channel_id=1, source_target_pairs={{0,4},{4,0},{1,5},{5,1},{2,6},{6,2},{3,7},{7,3},{8,12},{12,8},{9,1... | collective-permute-start | bytes 3735560 | tf_op jit(solution)/shard_map/back_core/ppermute | solution.py:417
  122.8 254.7 %all-reduce.2.cloned.1.call-start = ((), (), s32[]{:S(2)}) async-start(), calls=%async_computation.3 | async-start | bytes 1310720 | tf_op jit(solution)/shard_map/check/cond/branch_0_fun/while/body/eval_jaxpr/psum | solution.py:365
  384.6 258.4 %all-reduce.2.cloned.1.call-start = ((), (), s32[]{:S(2)}) async-start(), calls=%async_computation.3 | async-start | bytes 1310720 | tf_op jit(solution)/shard_map/check/cond/branch_0_fun/while/body/eval_jaxpr/psum | solution.py:365
  650.3 0.6 copy-start
Sparse Core Ops, SparseCore 0:
  131.1 246.3 all-reduce.1
  393.0 250.0 all-reduce.1

commit v5 on v4

--- a/solution.py
+++ b/solution.py
@@ -249,17 +249,17 @@
         def unpack():
             row = lax.broadcasted_iota(jnp.int32, (LANES, LANES), 0)
             col = lax.broadcasted_iota(jnp.int32, (LANES, LANES), 1)
-            sums = [jnp.zeros((1, LANES), F32) for _ in range(n)]
+            down = [jnp.zeros((1, LANES), F32) for _ in range(n)]
+            across = [None] * n
 
             def put(i, j, v):
                 dense[i * LANES : (i + 1) * LANES, j * LANES : (j + 1) * LANES] = v.astype(BF16)
                 square = v * v
-                sums[j] = sums[j] + jnp.sum(square, axis=0)[None, :]
+                down[j] = down[j] + jnp.sum(square, axis=0)[None, :]
                 if i != j:
-                    across = jnp.sum(square, axis=1, keepdims=True)
-                    sums[i] = sums[i] + across.T
-
-            for (i, j), at in pack.offset.items():
+                    across[i] = square if across[i] is None else across[i] + square
+
+            for (i, j), at in sorted(pack.offset.items()):
                 v = packed_rows(cov, at, LANES, pack.cov).astype(F32)
                 if i < j:
                     put(i, j, v)
@@ -267,7 +267,10 @@
                     flipped = v.T
                     put(i, i, jnp.where(row < col, v, flipped))
                     put(i + 1, i + 1, jnp.where(row > col, v, flipped))
-            squares[...] = jnp.concatenate(sums, axis=1)
+            for i in range(n):
+                if across[i] is not None:
+                    down[i] = down[i] + jnp.sum(across[i].T, axis=0)[None, :]
+            squares[...] = jnp.concatenate(down, axis=1)
 
         error_out[...] = jnp.zeros(error_out.shape, F32)
 
@@ -285,7 +288,9 @@
 
             @pl.when(step > 0)
             def _():
-                back = jnp.dot(inverse, vt[...], precision=HI, preferred_element_type=F32)
+                back = jnp.dot(
+                    inverse.astype(BF16), vt[...].astype(BF16), preferred_element_type=F32
+                )
                 share = (squares[...] * (1.0 / total_tokens) ** 2) * (back * back)
                 line = jnp.sum(share, axis=0)[None, :]
                 total = jnp.sum(line, axis=1, keepdims=True) * (ROUNDING**2 / k)
@@ -362,7 +367,9 @@
         vb = state[0].astype(BF16)
         projected = lax.dot_general(tokens, vb, NT, preferred_element_type=F32).astype(BF16)
         local = lax.dot_general(projected, tokens, TN, preferred_element_type=F32)
-        return orthonormal_rows(lax.psum(local, ALL) / total_tokens)
+        tiles = local.reshape(lax.axis_size(ALL), -1, LANES)
+        share = jnp.sum(lax.all_to_all(tiles, ALL, 0, 0, tiled=True), axis=0)
+        return orthonormal_rows(to_all(share, ALL).reshape(local.shape) / total_tokens)
 
     vt, factor = lax.fori_loop(0, ITERS, step, (first, jnp.zeros((k, k), F32)))
     slab = lax.axis_index(("x", "z", "c"))

time: 658 us -> 300 us (0.46)
  waiting for transfers between devices: 502 us -> 70.2 us
  blocking collectives: 66.3 us -> 143 us
  between operations: 14.8 us -> 1.39 us
  starting transfers between devices: 8.72 us -> 20.2 us
    psum x2 -> x0, waiting for transfers between devices: 497 us -> none  [step(): return orthonormal_rows(lax.psum(local, ALL) / total_tokens)]
    all_to_all x0 -> x2, blocking collectives: none -> 77 us  [step(): share = jnp.sum(lax.all_to_all(tiles, ALL, 0, 0, tiled=True), axis=0)]
    all_to_all x0 -> x2, waiting for transfers between devices: none -> 65.2 us  [to_all(): return lax.all_to_all(copies, axes, 0, 0, tiled=True)]
    all_to_all x0 -> x2, starting transfers between devices: none -> 11.6 us  [to_all(): return lax.all_to_all(copies, axes, 0, 0, tiled=True)]
where the time goes in v5:
time: 300 us; the launch traced here: 299 us
  blocking collectives  143 us (48%)
  waiting for transfers between devices  70.2 us (23%)
  Pallas kernels  43.3 us (14%)
  starting transfers between devices  20.2 us (7%)
  matrix products  14.8 us (5%)
  local copies, waits for them, and re-layouts  4.36 us (1%)
    all_to_all x2, blocking collectives, step(): share = jnp.sum(lax.all_to_all(tiles, ALL, 0, 0, tiled=True), axis=0)  77 us
    all_to_all x2, waiting for transfers between devices, to_all(): return lax.all_to_all(copies, axes, 0, 0, tiled=True)  65.2 us
    all_to_all x2, blocking collectives, to_all(): return lax.all_to_all(copies, axes, 0, 0, tiled=True)  43.3 us
    all_to_all x1, blocking collectives, body(): piece = summed(lax.all_to_all(tiles, ('x', 'y'), 0, 0, tiled=True), pack)  22.9 us
    pallas_call x1, Pallas kernels, body(): refine(pack, width, k, strip, total_tokens)(mine, other)  22.5 us
    dot_general x2, matrix products, step(): local = lax.dot_general(projected, tokens, TN, preferred_element_type=F32)  14.8 us
    pallas_call x2, Pallas kernels, orthonormal_rows(): pl.pallas_call(kernel, out_shape=(jax.ShapeDtypeStruct(zt.shape, F32), ja...  11.9 us
    all_to_all x2, starting transfers between devices, to_all(): return lax.all_to_all(copies, axes, 0, 0, tiled=True)  11.6 us
  transfers between devices with their start and end apart: 5, of which 4 were waited for; matrix products, arithmetic and copies ran while one was open for 0% of the time, Pallas kernels for 0%

profile of v5, /device:TPU:1, one launch (start us, length us, event | category | flops | bytes accessed | tf_op | source)
XLA Modules:
  0.0 299.3 jit_solution(786251009996290976)
XLA Ops:
  0.6 8.8 %local_products.1 = (f32[768,128]{1,0:T(8,128)S(1)}, f32[3328,128]{1,0:T(8,128)S(1)}, f32[768,128]{1,0:T(8,128)S(1)}, bf16[3328,128]{1,0:T(8,128)(2,1)S(1)}) custom-call(bf16[2048,1280]{1,0:T(8,128)(2,1)} %tok_hbm.1, bf16[2048,128]{1,0:T(8,128)(2,1)} %smap_hbm.1, bf16[1,8192,128]{2,1,0:T(8,128)(2,1)} %test_hbm.1), custom_call_target="tpu_custom_call" | custom-call | tf_op jit(solution)/shard_map/products/local_products/pallas_call | solution.py:410
  9.4 3.4 %collective-permute-start.1 = (bf16[3328,128]{1,0:T(8,128)(2,1)S(1)}, bf16[3328,128]{1,0:T(8,128)(2,1)S(1)}, u32[]{:S(2)}, u32[]{:S(2)}) collective-permute-start(bf16[3328,128]{1,0:T(8,128)(2,1)S(1)} %get-tuple-element.47), channel_id=1, source_target_pairs={{0,4},{4,0},{1,5},{5,1},{2,6},{6,2},{3,7},{7,3},{8,12},{12,8},{9,1... | collective-permute-start | bytes 2555912 | tf_op jit(solution)/shard_map/over_core/ppermute | solution.py:415
  12.8 0.1 collective-permute-start
  12.9 2.5 collective-permute-done
  15.4 0.1 reduce-precision_convert_fusion
  15.5 0.0 collective-permute-done.1
  15.5 0.2 add_convert_fusion
  15.7 0.1 pad_maximum_fusion
  15.8 22.9 %all_to_all.27 = bf16[16,304,128]{2,1,0:T(8,128)(2,1)S(1)} all-to-all(bf16[16,304,128]{2,1,0:T(8,128)(2,1)S(1)} %pad_maximum_fusion), channel_id=1, replica_groups=mesh['x'=4,'z'=8,'c'=2,'y'=4] {'x','y'}, dimensions={0} | all-to-all | bytes 2490368 | tf_op jit(solution)/shard_map/over_xy/all_to_all | solution.py:418
  38.7 0.2 convert_reduce_fusion
  39.0 0.1 broadcast_in_dim.9
  39.1 24.7 %all_to_all.28 = bf16[8,304,128]{2,1,0:T(8,128)(2,1)S(1)} all-to-all(bf16[8,304,128]{2,1,0:T(8,128)(2,1)S(1)} %broadcast_in_dim.9), channel_id=1, replica_groups=mesh['x'=4,'z'=8,'c'=2,'y'=4] {'z'}, dimensions={0} | all-to-all | bytes 1245184 | tf_op jit(solution)/shard_map/over_z/all_to_all | solution.py:381
  63.8 0.1 convert_reduce_fusion.1
  63.9 0.2 broadcast_in_dim.10
  64.1 18.6 %all_to_all.29.mine = bf16[16,304,128]{2,1,0:T(8,128)(2,1)S(1)} all-to-all(bf16[16,304,128]{2,1,0:T(8,128)(2,1)S(1)} %broadcast_in_dim.10), channel_id=1, replica_groups=mesh['x'=4,'z'=8,'c'=2,'y'=4] {'x','y'}, dimensions={0} | all-to-all | bytes 2490368 | tf_op jit(solution)/shard_map/back_xy/all_to_all | solution.py:381
  82.7 5.1 %collective-permute-start.2 = (bf16[16,304,128]{2,1,0:T(8,128)(2,1)S(1)}, bf16[16,304,128]{2,1,0:T(8,128)(2,1)S(1)}, u32[]{:S(2)}, u32[]{:S(2)}) collective-permute-start(bf16[16,304,128]{2,1,0:T(8,128)(2,1)S(1)} %all_to_all.29.mine), channel_id=1, source_target_pairs={{0,4},{4,0},{1,5},{5,1},{2,6},{6,2},{3,7},{7,3},{8,12},{12,8},{9,1... | collective-permute-start | bytes 3735560 | tf_op jit(solution)/shard_map/back_core/ppermute | solution.py:424
  87.8 2.6 collective-permute-done.2.other
  90.4 22.5 %refine.1 = (f32[20,128]{1,0:T(8,128)S(1)}, f32[128,128]{1,0:T(8,128)}, f32[128,1280]{1,0:T(8,128)S(1)}, f32[8,128]{1,0:T(8,128)S(1)}) custom-call(bf16[16,304,128]{2,1,0:T(8,128)(2,1)S(1)} %all_to_all.29.mine, bf16[16,304,128]{2,1,0:T(8,128)(2,1)S(1)} %collective-permute-done.2.other), custom_call_target="tpu_custom_call" | custom-call | tf_op jit(solution)/shard_map/refine/refine/pallas_call | solution.py:426
  113.0 0.5 slice.29
  114.1 184.5 %conditional.1 = (f32[128,128]{1,0:T(8,128)}, f32[20,128]{1,0:T(8,128)S(1)}) conditional(s32[]{:T(128)} %bitcast.12, (bf16[2048,1280]{1,0:T(8,128)(2,1)}, f32[128,1280]{1,0:T(8,128)S(1)}) %tuple.18, (f32[20,128]{1,0:T(8,128)S(1)}, f32[128,128]{1,0:T(8,128)}) %tuple.19), branch_computations={%region_2.0_spmd, %region_6.0_spmd} | conditional | flops 1342930304 | bytes 15906163 | solution.py:428
  114.4 184.1 %while.11 = (s32[]{:T(128)}, f32[128,1280]{1,0:T(8,128)S(1)}, f32[128,128]{1,0:T(8,128)}, bf16[2048,1280]{1,0:T(8,128)(2,1)}, s32[]{:T(128)}, /*index=5*/f32[]{:T(128)}) while((s32[]{:T(128)}, f32[128,1280]{1,0:T(8,128)S(1)}, f32[128,128]{1,0:T(8,128)}, bf16[2048,1280]{1,0:T(8,128)(2,1)}, s32[]{:T(128)}, /*index=5*/f32[]{:T(128)}) %tuple.41), condition=%wide.region_5.0_spmd, body=%wide.region_3.0_spmd.sunk | while | flops 1342930304 | bytes 15864937 | solution.py:374
  114.4 7.4 %fusion.21 = f32[128,1280]{1,0:T(8,128)S(1)} fusion(bf16[2048,1280]{1,0:T(8,128)(2,1)} %get-tuple-element.124, f32[128,1280]{1,0:T(8,128)S(1)} %get-tuple-element.116), kind=kOutput, calls=%fused_computation.1.clone.1 | convolution fusion | flops 1342603264 | bytes 6553600 | tf_op jit(solution)/shard_map/check/cond/branch_0_fun/while/body/eval_jaxpr/dot_general | solution.py:369
  121.8 0.2 reshape.52
  122.0 38.9 %all_to_all.30 = f32[256,5,128]{2,1,0:T(8,128)S(1)} all-to-all(f32[256,5,128]{2,1,0:T(8,128)S(1)} %reshape.52), channel_id=1, replica_groups=mesh['x'=4,'z'=8,'c'=2,'y'=4] {'x','z','c','y'}, dimensions={0} | all-to-all | bytes 1310720 | tf_op jit(solution)/shard_map/check/cond/branch_0_fun/while/body/eval_jaxpr/all_to_all | solution.py:371
  160.9 0.3 reduce_sum.32
  161.1 1.0 broadcast_in_dim.12
  162.2 5.8 %all-to-all-start.1 = ((f32[256,5,128]{2,1,0:T(8,128)}), f32[256,5,128]{2,1,0:T(8,128)S(1)}, u32[]{:S(2)}, u32[]{:S(2)}) async-start(f32[256,5,128]{2,1,0:T(8,128)} %broadcast_in_dim.12), calls=%async_computation.1 | async-start | bytes 2097152 | tf_op jit(solution)/shard_map/check/cond/branch_0_fun/while/body/eval_jaxpr/all_to_all | solution.py:381
  168.0 32.6 %all-to-all-done.1 = f32[256,5,128]{2,1,0:T(8,128)S(1)} async-done(((f32[256,5,128]{2,1,0:T(8,128)}), f32[256,5,128]{2,1,0:T(8,128)S(1)}, u32[]{:S(2)}, u32[]{:S(2)}) %all-to-all-start.1) | async-done | bytes 655392 | tf_op jit(solution)/shard_map/check/cond/branch_0_fun/while/body/eval_jaxpr/all_to_all | solution.py:381
  200.6 0.1 broadcast_multiply_fusion.2
  200.7 0.2 div.9.zt_ref
  200.9 6.0 %orthonormal_rows.1 = (f32[128,1280]{1,0:T(8,128)S(1)}, f32[128,128]{1,0:T(8,128)}) custom-call(f32[128,1280]{1,0:T(8,128)S(1)} %div.9.zt_ref), custom_call_target="tpu_custom_call" | custom-call | tf_op jit(solution)/shard_map/check/cond/branch_0_fun/while/body/eval_jaxpr/orthonormal_rows/pallas_call | solution.py:355
  206.8 7.4 %fusion.21 = f32[128,1280]{1,0:T(8,128)S(1)} fusion(bf16[2048,1280]{1,0:T(8,128)(2,1)} %get-tuple-element.124, f32[128,1280]{1,0:T(8,128)S(1)} %get-tuple-element.116), kind=kOutput, calls=%fused_computation.1.clone.1 | convolution fusion | flops 1342603264 | bytes 6553600 | tf_op jit(solution)/shard_map/check/cond/branch_0_fun/while/body/eval_jaxpr/dot_general | solution.py:369
  214.2 0.2 reshape.52
  214.4 38.1 %all_to_all.30 = f32[256,5,128]{2,1,0:T(8,128)S(1)} all-to-all(f32[256,5,128]{2,1,0:T(8,128)S(1)} %reshape.52), channel_id=1, replica_groups=mesh['x'=4,'z'=8,'c'=2,'y'=4] {'x','z','c','y'}, dimensions={0} | all-to-all | bytes 1310720 | tf_op jit(solution)/shard_map/check/cond/branch_0_fun/while/body/eval_jaxpr/all_to_all | solution.py:371
  252.5 0.3 reduce_sum.32
  252.8 1.0 broadcast_in_dim.12
  253.8 5.8 %all-to-all-start.1 = ((f32[256,5,128]{2,1,0:T(8,128)}), f32[256,5,128]{2,1,0:T(8,128)S(1)}, u32[]{:S(2)}, u32[]{:S(2)}) async-start(f32[256,5,128]{2,1,0:T(8,128)} %broadcast_in_dim.12), calls=%async_computation.1 | async-start | bytes 2097152 | tf_op jit(solution)/shard_map/check/cond/branch_0_fun/while/body/eval_jaxpr/all_to_all | solution.py:381
  259.6 32.6 %all-to-all-done.1 = f32[256,5,128]{2,1,0:T(8,128)S(1)} async-done(((f32[256,5,128]{2,1,0:T(8,128)}), f32[256,5,128]{2,1,0:T(8,128)S(1)}, u32[]{:S(2)}, u32[]{:S(2)}) %all-to-all-start.1) | async-done | bytes 655392 | tf_op jit(solution)/shard_map/check/cond/branch_0_fun/while/body/eval_jaxpr/all_to_all | solution.py:381
  292.2 0.1 broadcast_multiply_fusion.2
  292.3 0.2 div.9.zt_ref
  292.5 6.0 %orthonormal_rows.1 = (f32[128,1280]{1,0:T(8,128)S(1)}, f32[128,128]{1,0:T(8,128)}) custom-call(f32[128,1280]{1,0:T(8,128)S(1)} %div.9.zt_ref), custom_call_target="tpu_custom_call" | custom-call | tf_op jit(solution)/shard_map/check/cond/branch_0_fun/while/body/eval_jaxpr/orthonormal_rows/pallas_call | solution.py:355
  298.5 0.1 dynamic-slice_bitcast_fusion
  298.6 0.1 copy.13
  298.6 0.0 copy-start
  298.7 0.6 copy-done
  (7 shorter events, 0.1 us)
Async XLA Ops:
  9.4 6.1 %collective-permute-start.1 = (bf16[3328,128]{1,0:T(8,128)(2,1)S(1)}, bf16[3328,128]{1,0:T(8,128)(2,1)S(1)}, u32[]{:S(2)}, u32[]{:S(2)}) collective-permute-start(bf16[3328,128]{1,0:T(8,128)(2,1)S(1)} %get-tuple-element.47), channel_id=1, source_target_pairs={{0,4},{4,0},{1,5},{5,1},{2,6},{6,2},{3,7},{7,3},{8,12},{12,8},{9,1... | collective-permute-start | bytes 2555912 | tf_op jit(solution)/shard_map/over_core/ppermute | solution.py:415
  12.8 2.6 collective-permute-start
  82.7 7.7 %collective-permute-start.2 = (bf16[16,304,128]{2,1,0:T(8,128)(2,1)S(1)}, bf16[16,304,128]{2,1,0:T(8,128)(2,1)S(1)}, u32[]{:S(2)}, u32[]{:S(2)}) collective-permute-start(bf16[16,304,128]{2,1,0:T(8,128)(2,1)S(1)} %all_to_all.29.mine), channel_id=1, source_target_pairs={{0,4},{4,0},{1,5},{5,1},{2,6},{6,2},{3,7},{7,3},{8,12},{12,8},{9,1... | collective-permute-start | bytes 3735560 | tf_op jit(solution)/shard_map/back_core/ppermute | solution.py:424
  162.2 38.4 %all-to-all-start.1 = ((f32[256,5,128]{2,1,0:T(8,128)}), f32[256,5,128]{2,1,0:T(8,128)S(1)}, u32[]{:S(2)}, u32[]{:S(2)}) async-start(f32[256,5,128]{2,1,0:T(8,128)} %broadcast_in_dim.12), calls=%async_computation.1 | async-start | bytes 2097152 | tf_op jit(solution)/shard_map/check/cond/branch_0_fun/while/body/eval_jaxpr/all_to_all | solution.py:381
  253.8 38.4 %all-to-all-start.1 = ((f32[256,5,128]{2,1,0:T(8,128)}), f32[256,5,128]{2,1,0:T(8,128)S(1)}, u32[]{:S(2)}, u32[]{:S(2)}) async-start(f32[256,5,128]{2,1,0:T(8,128)} %broadcast_in_dim.12), calls=%async_computation.1 | async-start | bytes 2097152 | tf_op jit(solution)/shard_map/check/cond/branch_0_fun/while/body/eval_jaxpr/all_to_all | solution.py:381
  298.6 0.6 copy-start

commit v6 on v5

--- a/solution.py
+++ b/solution.py
@@ -151,6 +151,7 @@
 def eliminate(gram):
     k = gram.shape[0]
     blocks = k // SUB
+    segment = blocks // 2
     lane = lax.broadcasted_iota(jnp.int32, (SUB, k), 1)
     row = lax.broadcasted_iota(jnp.int32, (SUB, k), 0)
     work, trace = [], []
@@ -160,8 +161,9 @@
     factor, inverse = [], []
     for b in range(blocks):
         at = b * SUB
+        stop = (b // segment + 1) * segment
         spread = {}
-        for o in range(b, blocks):
+        for o in range(b, stop):
             for q in range(SUB):
                 spread[o, q] = jnp.broadcast_to(work[o][:, at + q : at + q + 1], (SUB, k))
         d = {(p, q): spread[b, q][p : p + 1, :] for p in range(SUB) for q in range(p, SUB)}
@@ -181,7 +183,7 @@
             for q in range(p + 1, SUB):
                 ra[q] = ra[q] - d[p, q] * ra[p]
                 re[q] = re[q] - d[p, q] * re[p]
-        for o in range(b + 1, blocks):
+        for o in range(b + 1, stop):
             column = [spread[o, q] for q in range(SUB)]
             for p in range(SUB):
                 column[p] = column[p] * scale[p]
@@ -189,8 +191,18 @@
                     column[q] = column[q] - d[p, q] * column[p]
                 work[o] = work[o] - column[p] * ra[p]
                 trace[o] = trace[o] - column[p] * re[p]
-        factor.append(jnp.where(lane >= row + at, jnp.concatenate(ra, axis=0), 0.0))
+        factor.append(jnp.concatenate(ra, axis=0))
         inverse.append(jnp.concatenate(re, axis=0))
+        if b + 1 == stop and stop < blocks:
+            above = jnp.concatenate(factor[-segment:], axis=0)
+            beside = jnp.concatenate([above, jnp.concatenate(inverse[-segment:], axis=0)], axis=1)
+            update = lax.dot_general(above, beside, TN, precision=HI, preferred_element_type=F32)
+            for o in range(stop, blocks):
+                rows = slice(o * SUB, (o + 1) * SUB)
+                work[o] = work[o] - update[rows, :k]
+                trace[o] = trace[o] - update[rows, k:]
+    for b in range(blocks):
+        factor[b] = jnp.where(lane >= row + b * SUB, factor[b], 0.0)
     return jnp.concatenate(factor, axis=0), jnp.concatenate(inverse, axis=0)
 
 
@@ -216,8 +228,8 @@
     half = pack.pieces // 2
 
     def kernel(
-        mine, other, basis, factor_out, first_out, error_out,
-        value, rest, cov, dense, squares, zt, vt, turned, sem,
+        mine, other, basis, factor_out, first_out, fine_out,
+        value, rest, cov, dense, squares, error, zt, vt, turned, sem,
     ):
         core = lax.axis_index("c")
         slab = lax.axis_index(("x", "z", "c"))
@@ -272,7 +284,7 @@
                     down[i] = down[i] + jnp.sum(across[i].T, axis=0)[None, :]
             squares[...] = jnp.concatenate(down, axis=1)
 
-        error_out[...] = jnp.zeros(error_out.shape, F32)
+        error[...] = jnp.zeros(error.shape, F32)
 
         @pl.loop(0, ITERS + 1)
         def _(step):
@@ -294,7 +306,7 @@
                 share = (squares[...] * (1.0 / total_tokens) ** 2) * (back * back)
                 line = jnp.sum(share, axis=0)[None, :]
                 total = jnp.sum(line, axis=1, keepdims=True) * (ROUNDING**2 / k)
-                error_out[...] = error_out[...] + jnp.broadcast_to(total, error_out.shape)
+                error[...] = error[...] + jnp.broadcast_to(total, error.shape)
 
             vt[...] = fresh
 
@@ -318,6 +330,7 @@
             cols = slice(i * LANES, (i + 1) * LANES)
             turned[cols, :] = vt[:, cols].T
         basis[...] = turned[pl.ds(slab * strip, strip), :]
+        fine_out[0] = (jnp.sum(error[:1, :1]) <= ALLOWED**2).astype(jnp.int32)
 
     return pl.pallas_call(
         kernel,
@@ -325,16 +338,18 @@
             jax.ShapeDtypeStruct((strip, k), F32),
             jax.ShapeDtypeStruct((k, k), F32),
             jax.ShapeDtypeStruct((k, width), F32),
-            jax.ShapeDtypeStruct((SUB, LANES), F32),
+            jax.ShapeDtypeStruct((1,), jnp.int32),
         ),
         in_specs=[pl.BlockSpec(memory_space=pl.ANY)] * 2,
-        out_specs=[pl.BlockSpec(memory_space=pltpu.VMEM)] * 4,
+        out_specs=[pl.BlockSpec(memory_space=pltpu.VMEM)] * 3
+        + [pl.BlockSpec(memory_space=pltpu.SMEM)],
         scratch_shapes=[
             pltpu.VMEM((pack.pieces, pack.exact, LANES), BF16),
             pltpu.VMEM((pack.pieces, pack.exact, LANES), BF16),
             pltpu.VMEM((pack.pieces, pack.cov, LANES), BF16),
             pltpu.VMEM((width, width), BF16),
             pltpu.VMEM((1, width), F32),
+            pltpu.VMEM((SUB, LANES), F32),
             pltpu.VMEM((k, width), F32),
             pltpu.VMEM((k, width), F32),
             pltpu.VMEM((width, k), F32),
@@ -423,10 +438,10 @@
     with jax.named_scope("back_core"):
         other = lax.ppermute(mine, "c", swap)
     with jax.named_scope("refine"):
-        basis, factor, first, error = refine(pack, width, k, strip, total_tokens)(mine, other)
+        basis, factor, first, fine = refine(pack, width, k, strip, total_tokens)(mine, other)
     with jax.named_scope("check"):
         return lax.cond(
-            error[0, 0] <= ALLOWED**2,
+            fine[0] > 0,
             lambda: (basis, factor),
             lambda: direct(tokens, first, strip, total_tokens),
         )

time: 300 us -> 297 us (0.990)
  no operation moved by 1% of the time
where the time goes in v6:
time: 297 us
  blocking collectives  143 us (48%)
  waiting for transfers between devices  70.2 us (24%)
  Pallas kernels  41.3 us (14%)
  starting transfers between devices  20.2 us (7%)
  matrix products  14.8 us (5%)
  local copies, waits for them, and re-layouts  3.84 us (1%)
    all_to_all x2, blocking collectives, step(): share = jnp.sum(lax.all_to_all(tiles, ALL, 0, 0, tiled=True), axis=0)  77 us
    all_to_all x2, waiting for transfers between devices, to_all(): return lax.all_to_all(copies, axes, 0, 0, tiled=True)  65.2 us
    all_to_all x2, blocking collectives, to_all(): return lax.all_to_all(copies, axes, 0, 0, tiled=True)  43.3 us
    all_to_all x1, blocking collectives, body(): piece = summed(lax.all_to_all(tiles, ('x', 'y'), 0, 0, tiled=True), pack)  22.9 us
    pallas_call x1, Pallas kernels, body(): refine(pack, width, k, strip, total_tokens)(mine, other)  21.4 us
    dot_general x2, matrix products, step(): local = lax.dot_general(projected, tokens, TN, preferred_element_type=F32)  14.8 us
    all_to_all x2, starting transfers between devices, to_all(): return lax.all_to_all(copies, axes, 0, 0, tiled=True)  11.6 us
    pallas_call x2, Pallas kernels, orthonormal_rows(): pl.pallas_call(kernel, out_shape=(jax.ShapeDtypeStruct(zt.shape, F32), ja...  11.1 us
  transfers between devices with their start and end apart: 5, of which 4 were waited for; matrix products, arithmetic and copies ran while one was open for 0% of the time, Pallas kernels for 0%

profile of v6, /device:TPU:1, one launch (start us, length us, event | category | flops | bytes accessed | tf_op | source)
XLA Modules:
  0.0 296.8 jit_solution(5995261383658366597)
XLA Ops:
  0.6 8.8 %local_products.1 = (f32[768,128]{1,0:T(8,128)S(1)}, f32[3328,128]{1,0:T(8,128)S(1)}, f32[768,128]{1,0:T(8,128)S(1)}, bf16[3328,128]{1,0:T(8,128)(2,1)S(1)}) custom-call(bf16[2048,1280]{1,0:T(8,128)(2,1)} %tok_hbm.1, bf16[2048,128]{1,0:T(8,128)(2,1)} %smap_hbm.1, bf16[1,8192,128]{2,1,0:T(8,128)(2,1)} %test_hbm.1), custom_call_target="tpu_custom_call" | custom-call | tf_op jit(solution)/shard_map/products/local_products/pallas_call | solution.py:425
  9.4 3.4 %collective-permute-start.1 = (bf16[3328,128]{1,0:T(8,128)(2,1)S(1)}, bf16[3328,128]{1,0:T(8,128)(2,1)S(1)}, u32[]{:S(2)}, u32[]{:S(2)}) collective-permute-start(bf16[3328,128]{1,0:T(8,128)(2,1)S(1)} %get-tuple-element.47), channel_id=1, source_target_pairs={{0,4},{4,0},{1,5},{5,1},{2,6},{6,2},{3,7},{7,3},{8,12},{12,8},{9,1... | collective-permute-start | bytes 2555912 | tf_op jit(solution)/shard_map/over_core/ppermute | solution.py:430
  12.8 0.1 collective-permute-start
  12.9 2.5 collective-permute-done
  15.4 0.1 reduce-precision_convert_fusion
  15.5 0.0 collective-permute-done.1
  15.5 0.2 add_convert_fusion
  15.7 0.1 pad_maximum_fusion
  15.8 22.9 %all_to_all.27 = bf16[16,304,128]{2,1,0:T(8,128)(2,1)S(1)} all-to-all(bf16[16,304,128]{2,1,0:T(8,128)(2,1)S(1)} %pad_maximum_fusion), channel_id=1, replica_groups=mesh['x'=4,'z'=8,'c'=2,'y'=4] {'x','y'}, dimensions={0} | all-to-all | bytes 2490368 | tf_op jit(solution)/shard_map/over_xy/all_to_all | solution.py:433
  38.7 0.2 convert_reduce_fusion
  39.0 0.1 broadcast_in_dim.9
  39.1 24.7 %all_to_all.28 = bf16[8,304,128]{2,1,0:T(8,128)(2,1)S(1)} all-to-all(bf16[8,304,128]{2,1,0:T(8,128)(2,1)S(1)} %broadcast_in_dim.9), channel_id=1, replica_groups=mesh['x'=4,'z'=8,'c'=2,'y'=4] {'z'}, dimensions={0} | all-to-all | bytes 1245184 | tf_op jit(solution)/shard_map/over_z/all_to_all | solution.py:396
  63.8 0.1 convert_reduce_fusion.1
  63.9 0.2 broadcast_in_dim.10
  64.1 18.6 %all_to_all.29.mine = bf16[16,304,128]{2,1,0:T(8,128)(2,1)S(1)} all-to-all(bf16[16,304,128]{2,1,0:T(8,128)(2,1)S(1)} %broadcast_in_dim.10), channel_id=1, replica_groups=mesh['x'=4,'z'=8,'c'=2,'y'=4] {'x','y'}, dimensions={0} | all-to-all | bytes 2490368 | tf_op jit(solution)/shard_map/back_xy/all_to_all | solution.py:396
  82.7 5.1 %collective-permute-start.2 = (bf16[16,304,128]{2,1,0:T(8,128)(2,1)S(1)}, bf16[16,304,128]{2,1,0:T(8,128)(2,1)S(1)}, u32[]{:S(2)}, u32[]{:S(2)}) collective-permute-start(bf16[16,304,128]{2,1,0:T(8,128)(2,1)S(1)} %all_to_all.29.mine), channel_id=1, source_target_pairs={{0,4},{4,0},{1,5},{5,1},{2,6},{6,2},{3,7},{7,3},{8,12},{12,8},{9,1... | collective-permute-start | bytes 3735560 | tf_op jit(solution)/shard_map/back_core/ppermute | solution.py:439
  87.8 2.6 collective-permute-done.2.other
  90.4 21.4 %refine.1 = (f32[20,128]{1,0:T(8,128)S(1)}, f32[128,128]{1,0:T(8,128)}, f32[128,1280]{1,0:T(8,128)S(1)}, s32[1]{0:T(128)}) custom-call(bf16[16,304,128]{2,1,0:T(8,128)(2,1)S(1)} %all_to_all.29.mine, bf16[16,304,128]{2,1,0:T(8,128)(2,1)S(1)} %collective-permute-done.2.other), custom_call_target="tpu_custom_call" | custom-call | tf_op jit(solution)/shard_map/refine/refine/pallas_call | solution.py:441
  112.5 183.7 %conditional.1 = (f32[128,128]{1,0:T(8,128)}, f32[20,128]{1,0:T(8,128)S(1)}) conditional(s32[]{:T(128)} %bitcast.12, (bf16[2048,1280]{1,0:T(8,128)(2,1)}, f32[128,1280]{1,0:T(8,128)S(1)}) %tuple.18, (f32[20,128]{1,0:T(8,128)S(1)}, f32[128,128]{1,0:T(8,128)}) %tuple.19), branch_computations={%region_2.0_spmd, %region_6.0_spmd} | conditional | flops 1342930304 | bytes 15906163 | solution.py:443
  112.7 183.3 %while.11 = (s32[]{:T(128)}, f32[128,1280]{1,0:T(8,128)S(1)}, f32[128,128]{1,0:T(8,128)}, bf16[2048,1280]{1,0:T(8,128)(2,1)}, s32[]{:T(128)}, /*index=5*/f32[]{:T(128)}) while((s32[]{:T(128)}, f32[128,1280]{1,0:T(8,128)S(1)}, f32[128,128]{1,0:T(8,128)}, bf16[2048,1280]{1,0:T(8,128)(2,1)}, s32[]{:T(128)}, /*index=5*/f32[]{:T(128)}) %tuple.41), condition=%wide.region_5.0_spmd, body=%wide.region_3.0_spmd.sunk | while | flops 1342930304 | bytes 15864937 | solution.py:389
  112.7 7.4 %fusion.21 = f32[128,1280]{1,0:T(8,128)S(1)} fusion(bf16[2048,1280]{1,0:T(8,128)(2,1)} %get-tuple-element.124, f32[128,1280]{1,0:T(8,128)S(1)} %get-tuple-element.116), kind=kOutput, calls=%fused_computation.1.clone.1 | convolution fusion | flops 1342603264 | bytes 6553600 | tf_op jit(solution)/shard_map/check/cond/branch_0_fun/while/body/eval_jaxpr/dot_general | solution.py:384
  120.1 0.2 reshape.52
  120.3 38.9 %all_to_all.30 = f32[256,5,128]{2,1,0:T(8,128)S(1)} all-to-all(f32[256,5,128]{2,1,0:T(8,128)S(1)} %reshape.52), channel_id=1, replica_groups=mesh['x'=4,'z'=8,'c'=2,'y'=4] {'x','z','c','y'}, dimensions={0} | all-to-all | bytes 1310720 | tf_op jit(solution)/shard_map/check/cond/branch_0_fun/while/body/eval_jaxpr/all_to_all | solution.py:386
  159.2 0.3 reduce_sum.32
  159.5 1.0 broadcast_in_dim.12
  160.5 5.8 %all-to-all-start.1 = ((f32[256,5,128]{2,1,0:T(8,128)}), f32[256,5,128]{2,1,0:T(8,128)S(1)}, u32[]{:S(2)}, u32[]{:S(2)}) async-start(f32[256,5,128]{2,1,0:T(8,128)} %broadcast_in_dim.12), calls=%async_computation.1 | async-start | bytes 2097152 | tf_op jit(solution)/shard_map/check/cond/branch_0_fun/while/body/eval_jaxpr/all_to_all | solution.py:396
  166.3 32.6 %all-to-all-done.1 = f32[256,5,128]{2,1,0:T(8,128)S(1)} async-done(((f32[256,5,128]{2,1,0:T(8,128)}), f32[256,5,128]{2,1,0:T(8,128)S(1)}, u32[]{:S(2)}, u32[]{:S(2)}) %all-to-all-start.1) | async-done | bytes 655392 | tf_op jit(solution)/shard_map/check/cond/branch_0_fun/while/body/eval_jaxpr/all_to_all | solution.py:396
  198.9 0.1 broadcast_multiply_fusion.2
  199.0 0.2 div.9.zt_ref
  199.2 5.6 %orthonormal_rows.1 = (f32[128,1280]{1,0:T(8,128)S(1)}, f32[128,128]{1,0:T(8,128)}) custom-call(f32[128,1280]{1,0:T(8,128)S(1)} %div.9.zt_ref), custom_call_target="tpu_custom_call" | custom-call | tf_op jit(solution)/shard_map/check/cond/branch_0_fun/while/body/eval_jaxpr/orthonormal_rows/pallas_call | solution.py:370
  204.8 7.4 %fusion.21 = f32[128,1280]{1,0:T(8,128)S(1)} fusion(bf16[2048,1280]{1,0:T(8,128)(2,1)} %get-tuple-element.124, f32[128,1280]{1,0:T(8,128)S(1)} %get-tuple-element.116), kind=kOutput, calls=%fused_computation.1.clone.1 | convolution fusion | flops 1342603264 | bytes 6553600 | tf_op jit(solution)/shard_map/check/cond/branch_0_fun/while/body/eval_jaxpr/dot_general | solution.py:384
  212.2 0.2 reshape.52
  212.4 38.1 %all_to_all.30 = f32[256,5,128]{2,1,0:T(8,128)S(1)} all-to-all(f32[256,5,128]{2,1,0:T(8,128)S(1)} %reshape.52), channel_id=1, replica_groups=mesh['x'=4,'z'=8,'c'=2,'y'=4] {'x','z','c','y'}, dimensions={0} | all-to-all | bytes 1310720 | tf_op jit(solution)/shard_map/check/cond/branch_0_fun/while/body/eval_jaxpr/all_to_all | solution.py:386
  250.5 0.3 reduce_sum.32
  250.7 1.0 broadcast_in_dim.12
  251.8 5.8 %all-to-all-start.1 = ((f32[256,5,128]{2,1,0:T(8,128)}), f32[256,5,128]{2,1,0:T(8,128)S(1)}, u32[]{:S(2)}, u32[]{:S(2)}) async-start(f32[256,5,128]{2,1,0:T(8,128)} %broadcast_in_dim.12), calls=%async_computation.1 | async-start | bytes 2097152 | tf_op jit(solution)/shard_map/check/cond/branch_0_fun/while/body/eval_jaxpr/all_to_all | solution.py:396
  257.6 32.6 %all-to-all-done.1 = f32[256,5,128]{2,1,0:T(8,128)S(1)} async-done(((f32[256,5,128]{2,1,0:T(8,128)}), f32[256,5,128]{2,1,0:T(8,128)S(1)}, u32[]{:S(2)}, u32[]{:S(2)}) %all-to-all-start.1) | async-done | bytes 655392 | tf_op jit(solution)/shard_map/check/cond/branch_0_fun/while/body/eval_jaxpr/all_to_all | solution.py:396
  290.2 0.1 broadcast_multiply_fusion.2
  290.3 0.2 div.9.zt_ref
  290.4 5.6 %orthonormal_rows.1 = (f32[128,1280]{1,0:T(8,128)S(1)}, f32[128,128]{1,0:T(8,128)}) custom-call(f32[128,1280]{1,0:T(8,128)S(1)} %div.9.zt_ref), custom_call_target="tpu_custom_call" | custom-call | tf_op jit(solution)/shard_map/check/cond/branch_0_fun/while/body/eval_jaxpr/orthonormal_rows/pallas_call | solution.py:370
  296.0 0.1 dynamic-slice_bitcast_fusion
  296.1 0.1 copy.13
  296.2 0.0 copy-start
  296.2 0.6 copy-done
  (7 shorter events, 0.1 us)
Async XLA Ops:
  9.4 6.1 %collective-permute-start.1 = (bf16[3328,128]{1,0:T(8,128)(2,1)S(1)}, bf16[3328,128]{1,0:T(8,128)(2,1)S(1)}, u32[]{:S(2)}, u32[]{:S(2)}) collective-permute-start(bf16[3328,128]{1,0:T(8,128)(2,1)S(1)} %get-tuple-element.47), channel_id=1, source_target_pairs={{0,4},{4,0},{1,5},{5,1},{2,6},{6,2},{3,7},{7,3},{8,12},{12,8},{9,1... | collective-permute-start | bytes 2555912 | tf_op jit(solution)/shard_map/over_core/ppermute | solution.py:430
  12.8 2.6 collective-permute-start
  82.7 7.7 %collective-permute-start.2 = (bf16[16,304,128]{2,1,0:T(8,128)(2,1)S(1)}, bf16[16,304,128]{2,1,0:T(8,128)(2,1)S(1)}, u32[]{:S(2)}, u32[]{:S(2)}) collective-permute-start(bf16[16,304,128]{2,1,0:T(8,128)(2,1)S(1)} %all_to_all.29.mine), channel_id=1, source_target_pairs={{0,4},{4,0},{1,5},{5,1},{2,6},{6,2},{3,7},{7,3},{8,12},{12,8},{9,1... | collective-permute-start | bytes 3735560 | tf_op jit(solution)/shard_map/back_core/ppermute | solution.py:439
  160.5 38.4 %all-to-all-start.1 = ((f32[256,5,128]{2,1,0:T(8,128)}), f32[256,5,128]{2,1,0:T(8,128)S(1)}, u32[]{:S(2)}, u32[]{:S(2)}) async-start(f32[256,5,128]{2,1,0:T(8,128)} %broadcast_in_dim.12), calls=%async_computation.1 | async-start | bytes 2097152 | tf_op jit(solution)/shard_map/check/cond/branch_0_fun/while/body/eval_jaxpr/all_to_all | solution.py:396
  251.8 38.4 %all-to-all-start.1 = ((f32[256,5,128]{2,1,0:T(8,128)}), f32[256,5,128]{2,1,0:T(8,128)S(1)}, u32[]{:S(2)}, u32[]{:S(2)}) async-start(f32[256,5,128]{2,1,0:T(8,128)} %broadcast_in_dim.12), calls=%async_computation.1 | async-start | bytes 2097152 | tf_op jit(solution)/shard_map/check/cond/branch_0_fun/while/body/eval_jaxpr/all_to_all | solution.py:396
  296.2 0.6 copy-start

commit v7 on v6

--- a/solution.py
+++ b/solution.py
@@ -56,7 +56,7 @@
 
     def kernel(
         tok_hbm, smap_hbm, test_hbm, keep_exact, keep_cov, send_exact, send_cov,
-        tok, smap, test, exact, cov, rounded, sem, out_sem,
+        tok, smap, test, exact, cov, own, rounded, sem, out_sem,
     ):
         core = lax.axis_index("c")
         slab = lax.axis_index(("x", "z", "c"))
@@ -80,6 +80,23 @@
             sketch = sketch + lax.dot_general(
                 smap[rows, :], tok[rows, :], TN, preferred_element_type=F32
             )
+            if (s + 1) % (chunks // 2) == 0:
+                rows = slice((s + 1 - chunks // 2) * part, (s + 1) * part)
+                opening = s < chunks // 2
+                for pair in pack.pairs:
+                    base = 2 * pair * LANES
+                    high = base + 2 * LANES
+                    out = lax.dot_general(
+                        tok[rows, :high], tok[rows, base:high], TN, preferred_element_type=F32
+                    )
+                    for j in range(2):
+                        col = 2 * pair + j
+                        for i in range(col + 1):
+                            tile = out[i * LANES : (i + 1) * LANES, j * LANES : (j + 1) * LANES]
+                            to = own if i == col else cov
+                            at = col * LANES if i == col else pack.offset[i, col]
+                            place = slice(at, at + LANES)
+                            to[place, :] = tile if opening else to[place, :] + tile
         load_test.wait()
         start = lax.dot_general(test[...], sketch.astype(BF16), TN, preferred_element_type=F32)
         for i in range(pack.n):
@@ -92,21 +109,13 @@
         col = lax.broadcasted_iota(jnp.int32, (LANES, LANES), 1)
         for pair in pack.pairs:
             base = 2 * pair * LANES
-            high = base + 2 * LANES
-            out = lax.dot_general(tok[:, :high], tok[:, base:high], TN, preferred_element_type=F32)
-            for j in range(2):
-                for i in range(2 * pair + j):
-                    at = pack.offset[i, 2 * pair + j]
-                    cov[at : at + LANES, :] = out[
-                        i * LANES : (i + 1) * LANES, j * LANES : (j + 1) * LANES
-                    ]
-            upper = out[base : base + LANES, :LANES]
-            lower = out[base + LANES : high, LANES:]
+            upper = own[base : base + LANES, :]
+            lower = own[base + LANES : base + 2 * LANES, :]
             at = pack.offset[2 * pair, 2 * pair]
             both = jnp.where(row < col, upper, lower)
             cov[at : at + LANES, :] = jnp.where(row == col, 0.0, both)
-            for b, own in ((2 * pair, upper), (2 * pair + 1, lower)):
-                line = jnp.sum(jnp.where(row == col, own, 0.0), axis=0)[None, :]
+            for b, block in ((2 * pair, upper), (2 * pair + 1, lower)):
+                line = jnp.sum(jnp.where(row == col, block, 0.0), axis=0)[None, :]
                 exact[pack.diagonal + b : pack.diagonal + b + 1, :] = line
         away = 1 - core
         rounded[...] = cov[pl.ds(pl.multiple_of(away * cov_half, LANES), cov_half), :].astype(BF16)
@@ -139,6 +148,7 @@
             pltpu.VMEM((k, k), BF16),
             pltpu.VMEM((pack.exact_rows, LANES), F32),
             pltpu.VMEM((pack.cov_rows, LANES), F32),
+            pltpu.VMEM((width, LANES), F32),
             pltpu.VMEM((cov_half, LANES), BF16),
             pltpu.SemaphoreType.DMA((chunks + 2,)),
             pltpu.SemaphoreType.DMA((4,)),

time: 297 us -> 297 us (level)
  no operation moved by 1% of the time
where the time goes in v7:
time: 297 us
  blocking collectives  143 us (48%)
  waiting for transfers between devices  70.2 us (24%)
  Pallas kernels  41.1 us (14%)
  starting transfers between devices  20.1 us (7%)
  matrix products  14.8 us (5%)
  local copies, waits for them, and re-layouts  3.84 us (1%)
    all_to_all x2, blocking collectives, step(): share = jnp.sum(lax.all_to_all(tiles, ALL, 0, 0, tiled=True), axis=0)  77 us
    all_to_all x2, waiting for transfers between devices, to_all(): return lax.all_to_all(copies, axes, 0, 0, tiled=True)  65.2 us
    all_to_all x2, blocking collectives, to_all(): return lax.all_to_all(copies, axes, 0, 0, tiled=True)  43.4 us
    all_to_all x1, blocking collectives, body(): piece = summed(lax.all_to_all(tiles, ('x', 'y'), 0, 0, tiled=True), pack)  22.9 us
    pallas_call x1, Pallas kernels, body(): refine(pack, width, k, strip, total_tokens)(mine, other)  21.4 us
    dot_general x2, matrix products, step(): local = lax.dot_general(projected, tokens, TN, preferred_element_type=F32)  14.8 us
    all_to_all x2, starting transfers between devices, to_all(): return lax.all_to_all(copies, axes, 0, 0, tiled=True)  11.6 us
    pallas_call x2, Pallas kernels, orthonormal_rows(): pl.pallas_call(kernel, out_shape=(jax.ShapeDtypeStruct(zt.shape, F32), ja...  11.1 us
  transfers between devices with their start and end apart: 5, of which 4 were waited for; matrix products, arithmetic and copies ran while one was open for 0% of the time, Pallas kernels for 0%

profile of v7, /device:TPU:1, one launch (start us, length us, event | category | flops | bytes accessed | tf_op | source)
XLA Modules:
  0.0 296.6 jit_solution(18051028887569364760)
XLA Ops:
  0.6 8.6 %local_products.1 = (f32[768,128]{1,0:T(8,128)S(1)}, f32[3328,128]{1,0:T(8,128)S(1)}, f32[768,128]{1,0:T(8,128)S(1)}, bf16[3328,128]{1,0:T(8,128)(2,1)S(1)}) custom-call(bf16[2048,1280]{1,0:T(8,128)(2,1)} %tok_hbm.1, bf16[2048,128]{1,0:T(8,128)(2,1)} %smap_hbm.1, bf16[1,8192,128]{2,1,0:T(8,128)(2,1)} %test_hbm.1), custom_call_target="tpu_custom_call" | custom-call | tf_op jit(solution)/shard_map/products/local_products/pallas_call | solution.py:435
  9.3 3.3 %collective-permute-start.1 = (bf16[3328,128]{1,0:T(8,128)(2,1)S(1)}, bf16[3328,128]{1,0:T(8,128)(2,1)S(1)}, u32[]{:S(2)}, u32[]{:S(2)}) collective-permute-start(bf16[3328,128]{1,0:T(8,128)(2,1)S(1)} %get-tuple-element.47), channel_id=1, source_target_pairs={{0,4},{4,0},{1,5},{5,1},{2,6},{6,2},{3,7},{7,3},{8,12},{12,8},{9,1... | collective-permute-start | bytes 2555912 | tf_op jit(solution)/shard_map/over_core/ppermute | solution.py:440
  12.6 0.1 collective-permute-start
  12.7 2.5 collective-permute-done
  15.1 0.1 reduce-precision_convert_fusion
  15.2 0.0 collective-permute-done.1
  15.2 0.2 add_convert_fusion
  15.5 0.1 pad_maximum_fusion
  15.6 22.9 %all_to_all.27 = bf16[16,304,128]{2,1,0:T(8,128)(2,1)S(1)} all-to-all(bf16[16,304,128]{2,1,0:T(8,128)(2,1)S(1)} %pad_maximum_fusion), channel_id=1, replica_groups=mesh['x'=4,'z'=8,'c'=2,'y'=4] {'x','y'}, dimensions={0} | all-to-all | bytes 2490368 | tf_op jit(solution)/shard_map/over_xy/all_to_all | solution.py:443
  38.5 0.2 convert_reduce_fusion
  38.7 0.1 broadcast_in_dim.9
  38.8 24.7 %all_to_all.28 = bf16[8,304,128]{2,1,0:T(8,128)(2,1)S(1)} all-to-all(bf16[8,304,128]{2,1,0:T(8,128)(2,1)S(1)} %broadcast_in_dim.9), channel_id=1, replica_groups=mesh['x'=4,'z'=8,'c'=2,'y'=4] {'z'}, dimensions={0} | all-to-all | bytes 1245184 | tf_op jit(solution)/shard_map/over_z/all_to_all | solution.py:406
  63.5 0.1 convert_reduce_fusion.1
  63.7 0.2 broadcast_in_dim.10
  63.8 18.6 %all_to_all.29.mine = bf16[16,304,128]{2,1,0:T(8,128)(2,1)S(1)} all-to-all(bf16[16,304,128]{2,1,0:T(8,128)(2,1)S(1)} %broadcast_in_dim.10), channel_id=1, replica_groups=mesh['x'=4,'z'=8,'c'=2,'y'=4] {'x','y'}, dimensions={0} | all-to-all | bytes 2490368 | tf_op jit(solution)/shard_map/back_xy/all_to_all | solution.py:406
  82.5 5.1 %collective-permute-start.2 = (bf16[16,304,128]{2,1,0:T(8,128)(2,1)S(1)}, bf16[16,304,128]{2,1,0:T(8,128)(2,1)S(1)}, u32[]{:S(2)}, u32[]{:S(2)}) collective-permute-start(bf16[16,304,128]{2,1,0:T(8,128)(2,1)S(1)} %all_to_all.29.mine), channel_id=1, source_target_pairs={{0,4},{4,0},{1,5},{5,1},{2,6},{6,2},{3,7},{7,3},{8,12},{12,8},{9,1... | collective-permute-start | bytes 3735560 | tf_op jit(solution)/shard_map/back_core/ppermute | solution.py:449
  87.6 2.6 collective-permute-done.2.other
  90.2 21.4 %refine.1 = (f32[20,128]{1,0:T(8,128)S(1)}, f32[128,128]{1,0:T(8,128)}, f32[128,1280]{1,0:T(8,128)S(1)}, s32[1]{0:T(128)}) custom-call(bf16[16,304,128]{2,1,0:T(8,128)(2,1)S(1)} %all_to_all.29.mine, bf16[16,304,128]{2,1,0:T(8,128)(2,1)S(1)} %collective-permute-done.2.other), custom_call_target="tpu_custom_call" | custom-call | tf_op jit(solution)/shard_map/refine/refine/pallas_call | solution.py:451
  112.2 183.7 %conditional.1 = (f32[128,128]{1,0:T(8,128)}, f32[20,128]{1,0:T(8,128)S(1)}) conditional(s32[]{:T(128)} %bitcast.12, (bf16[2048,1280]{1,0:T(8,128)(2,1)}, f32[128,1280]{1,0:T(8,128)S(1)}) %tuple.18, (f32[20,128]{1,0:T(8,128)S(1)}, f32[128,128]{1,0:T(8,128)}) %tuple.19), branch_computations={%region_2.0_spmd, %region_6.0_spmd} | conditional | flops 1342930304 | bytes 15906163 | solution.py:453
  112.5 183.3 %while.11 = (s32[]{:T(128)}, f32[128,1280]{1,0:T(8,128)S(1)}, f32[128,128]{1,0:T(8,128)}, bf16[2048,1280]{1,0:T(8,128)(2,1)}, s32[]{:T(128)}, /*index=5*/f32[]{:T(128)}) while((s32[]{:T(128)}, f32[128,1280]{1,0:T(8,128)S(1)}, f32[128,128]{1,0:T(8,128)}, bf16[2048,1280]{1,0:T(8,128)(2,1)}, s32[]{:T(128)}, /*index=5*/f32[]{:T(128)}) %tuple.41), condition=%wide.region_5.0_spmd, body=%wide.region_3.0_spmd.sunk | while | flops 1342930304 | bytes 15864937 | solution.py:399
  112.5 7.4 %fusion.21 = f32[128,1280]{1,0:T(8,128)S(1)} fusion(bf16[2048,1280]{1,0:T(8,128)(2,1)} %get-tuple-element.124, f32[128,1280]{1,0:T(8,128)S(1)} %get-tuple-element.116), kind=kOutput, calls=%fused_computation.1.clone.1 | convolution fusion | flops 1342603264 | bytes 6553600 | tf_op jit(solution)/shard_map/check/cond/branch_0_fun/while/body/eval_jaxpr/dot_general | solution.py:394
  119.9 0.2 reshape.52
  120.1 38.9 %all_to_all.30 = f32[256,5,128]{2,1,0:T(8,128)S(1)} all-to-all(f32[256,5,128]{2,1,0:T(8,128)S(1)} %reshape.52), channel_id=1, replica_groups=mesh['x'=4,'z'=8,'c'=2,'y'=4] {'x','z','c','y'}, dimensions={0} | all-to-all | bytes 1310720 | tf_op jit(solution)/shard_map/check/cond/branch_0_fun/while/body/eval_jaxpr/all_to_all | solution.py:396
  159.0 0.3 reduce_sum.32
  159.2 1.0 broadcast_in_dim.12
  160.3 5.8 %all-to-all-start.1 = ((f32[256,5,128]{2,1,0:T(8,128)}), f32[256,5,128]{2,1,0:T(8,128)S(1)}, u32[]{:S(2)}, u32[]{:S(2)}) async-start(f32[256,5,128]{2,1,0:T(8,128)} %broadcast_in_dim.12), calls=%async_computation.1 | async-start | bytes 2097152 | tf_op jit(solution)/shard_map/check/cond/branch_0_fun/while/body/eval_jaxpr/all_to_all | solution.py:406
  166.1 32.6 %all-to-all-done.1 = f32[256,5,128]{2,1,0:T(8,128)S(1)} async-done(((f32[256,5,128]{2,1,0:T(8,128)}), f32[256,5,128]{2,1,0:T(8,128)S(1)}, u32[]{:S(2)}, u32[]{:S(2)}) %all-to-all-start.1) | async-done | bytes 655392 | tf_op jit(solution)/shard_map/check/cond/branch_0_fun/while/body/eval_jaxpr/all_to_all | solution.py:406
  198.7 0.1 broadcast_multiply_fusion.2
  198.8 0.2 div.9.zt_ref
  198.9 5.6 %orthonormal_rows.1 = (f32[128,1280]{1,0:T(8,128)S(1)}, f32[128,128]{1,0:T(8,128)}) custom-call(f32[128,1280]{1,0:T(8,128)S(1)} %div.9.zt_ref), custom_call_target="tpu_custom_call" | custom-call | tf_op jit(solution)/shard_map/check/cond/branch_0_fun/while/body/eval_jaxpr/orthonormal_rows/pallas_call | solution.py:380
  204.5 7.4 %fusion.21 = f32[128,1280]{1,0:T(8,128)S(1)} fusion(bf16[2048,1280]{1,0:T(8,128)(2,1)} %get-tuple-element.124, f32[128,1280]{1,0:T(8,128)S(1)} %get-tuple-element.116), kind=kOutput, calls=%fused_computation.1.clone.1 | convolution fusion | flops 1342603264 | bytes 6553600 | tf_op jit(solution)/shard_map/check/cond/branch_0_fun/while/body/eval_jaxpr/dot_general | solution.py:394
  211.9 0.2 reshape.52
  212.1 38.1 %all_to_all.30 = f32[256,5,128]{2,1,0:T(8,128)S(1)} all-to-all(f32[256,5,128]{2,1,0:T(8,128)S(1)} %reshape.52), channel_id=1, replica_groups=mesh['x'=4,'z'=8,'c'=2,'y'=4] {'x','z','c','y'}, dimensions={0} | all-to-all | bytes 1310720 | tf_op jit(solution)/shard_map/check/cond/branch_0_fun/while/body/eval_jaxpr/all_to_all | solution.py:396
  250.2 0.3 reduce_sum.32
  250.5 1.0 broadcast_in_dim.12
  251.5 5.8 %all-to-all-start.1 = ((f32[256,5,128]{2,1,0:T(8,128)}), f32[256,5,128]{2,1,0:T(8,128)S(1)}, u32[]{:S(2)}, u32[]{:S(2)}) async-start(f32[256,5,128]{2,1,0:T(8,128)} %broadcast_in_dim.12), calls=%async_computation.1 | async-start | bytes 2097152 | tf_op jit(solution)/shard_map/check/cond/branch_0_fun/while/body/eval_jaxpr/all_to_all | solution.py:406
  257.3 32.6 %all-to-all-done.1 = f32[256,5,128]{2,1,0:T(8,128)S(1)} async-done(((f32[256,5,128]{2,1,0:T(8,128)}), f32[256,5,128]{2,1,0:T(8,128)S(1)}, u32[]{:S(2)}, u32[]{:S(2)}) %all-to-all-start.1) | async-done | bytes 655392 | tf_op jit(solution)/shard_map/check/cond/branch_0_fun/while/body/eval_jaxpr/all_to_all | solution.py:406
  289.9 0.1 broadcast_multiply_fusion.2
  290.0 0.2 div.9.zt_ref
  290.2 5.6 %orthonormal_rows.1 = (f32[128,1280]{1,0:T(8,128)S(1)}, f32[128,128]{1,0:T(8,128)}) custom-call(f32[128,1280]{1,0:T(8,128)S(1)} %div.9.zt_ref), custom_call_target="tpu_custom_call" | custom-call | tf_op jit(solution)/shard_map/check/cond/branch_0_fun/while/body/eval_jaxpr/orthonormal_rows/pallas_call | solution.py:380
  295.8 0.1 dynamic-slice_bitcast_fusion
  295.9 0.1 copy.13
  296.0 0.0 copy-start
  296.0 0.6 copy-done
  (7 shorter events, 0.1 us)
Async XLA Ops:
  9.3 6.0 %collective-permute-start.1 = (bf16[3328,128]{1,0:T(8,128)(2,1)S(1)}, bf16[3328,128]{1,0:T(8,128)(2,1)S(1)}, u32[]{:S(2)}, u32[]{:S(2)}) collective-permute-start(bf16[3328,128]{1,0:T(8,128)(2,1)S(1)} %get-tuple-element.47), channel_id=1, source_target_pairs={{0,4},{4,0},{1,5},{5,1},{2,6},{6,2},{3,7},{7,3},{8,12},{12,8},{9,1... | collective-permute-start | bytes 2555912 | tf_op jit(solution)/shard_map/over_core/ppermute | solution.py:440
  12.6 2.6 collective-permute-start
  82.5 7.7 %collective-permute-start.2 = (bf16[16,304,128]{2,1,0:T(8,128)(2,1)S(1)}, bf16[16,304,128]{2,1,0:T(8,128)(2,1)S(1)}, u32[]{:S(2)}, u32[]{:S(2)}) collective-permute-start(bf16[16,304,128]{2,1,0:T(8,128)(2,1)S(1)} %all_to_all.29.mine), channel_id=1, source_target_pairs={{0,4},{4,0},{1,5},{5,1},{2,6},{6,2},{3,7},{7,3},{8,12},{12,8},{9,1... | collective-permute-start | bytes 3735560 | tf_op jit(solution)/shard_map/back_core/ppermute | solution.py:449
  160.3 38.4 %all-to-all-start.1 = ((f32[256,5,128]{2,1,0:T(8,128)}), f32[256,5,128]{2,1,0:T(8,128)S(1)}, u32[]{:S(2)}, u32[]{:S(2)}) async-start(f32[256,5,128]{2,1,0:T(8,128)} %broadcast_in_dim.12), calls=%async_computation.1 | async-start | bytes 2097152 | tf_op jit(solution)/shard_map/check/cond/branch_0_fun/while/body/eval_jaxpr/all_to_all | solution.py:406
  251.5 38.4 %all-to-all-start.1 = ((f32[256,5,128]{2,1,0:T(8,128)}), f32[256,5,128]{2,1,0:T(8,128)S(1)}, u32[]{:S(2)}, u32[]{:S(2)}) async-start(f32[256,5,128]{2,1,0:T(8,128)} %broadcast_in_dim.12), calls=%async_computation.1 | async-start | bytes 2097152 | tf_op jit(solution)/shard_map/check/cond/branch_0_fun/while/body/eval_jaxpr/all_to_all | solution.py:406
  296.0 0.6 copy-start

commit v8 on v6

--- a/solution.py
+++ b/solution.py
@@ -206,10 +206,29 @@
     return jnp.concatenate(factor, axis=0), jnp.concatenate(inverse, axis=0)
 
 
+def thirds(v):
+    high = v.astype(BF16)
+    rest = v - high.astype(F32)
+    mid = rest.astype(BF16)
+    return high, mid, (rest - mid.astype(F32)).astype(BF16)
+
+
 def orthonormal(pt):
-    gram = lax.dot_general(pt, pt, NT, precision=HI, preferred_element_type=F32)
+    k = pt.shape[0]
+    high, mid, low = thirds(pt)
+    three = jnp.concatenate([high, mid, low], axis=0)
+    wide = lax.dot_general(high, three, NT, preferred_element_type=F32)
+    middle = lax.dot_general(mid, mid, NT, preferred_element_type=F32)
+    cross = wide[:, 2 * k :] + wide[:, k : 2 * k]
+    gram = wide[:, :k] + (cross + cross.T + middle)
     factor, inverse = eliminate(gram)
-    return jnp.dot(inverse, pt, precision=HI, preferred_element_type=F32), factor, inverse
+    ih, im, il = thirds(inverse)
+    top = jnp.concatenate([high, mid], axis=0)
+    ends = jnp.concatenate([low, high], axis=0)
+    vt = jnp.dot(jnp.concatenate([ih, il], axis=1), ends, preferred_element_type=F32)
+    vt = vt + jnp.dot(jnp.concatenate([im, im], axis=1), top, preferred_element_type=F32)
+    vt = vt + jnp.dot(jnp.concatenate([ih, ih], axis=1), top, preferred_element_type=F32)
+    return vt, factor, inverse
 
 
 def packed_rows(ref, begin, count, length):

time: 297 us -> 293 us (0.987)
  Pallas kernels: 41.3 us -> 36.9 us
where the time goes in v8:
time: 293 us; the launch traced here: 292 us
  blocking collectives  143 us (49%)
  waiting for transfers between devices  70.2 us (24%)
  Pallas kernels  36.9 us (13%)
  starting transfers between devices  20.2 us (7%)
  matrix products  14.8 us (5%)
  local copies, waits for them, and re-layouts  3.84 us (1%)
    all_to_all x2, blocking collectives, step(): share = jnp.sum(lax.all_to_all(tiles, ALL, 0, 0, tiled=True), axis=0)  76.9 us
    all_to_all x2, waiting for transfers between devices, to_all(): return lax.all_to_all(copies, axes, 0, 0, tiled=True)  65.2 us
    all_to_all x2, blocking collectives, to_all(): return lax.all_to_all(copies, axes, 0, 0, tiled=True)  43.3 us
    all_to_all x1, blocking collectives, body(): piece = summed(lax.all_to_all(tiles, ('x', 'y'), 0, 0, tiled=True), pack)  22.9 us
    pallas_call x1, Pallas kernels, body(): refine(pack, width, k, strip, total_tokens)(mine, other)  18.7 us
    dot_general x2, matrix products, step(): local = lax.dot_general(projected, tokens, TN, preferred_element_type=F32)  14.8 us
    all_to_all x2, starting transfers between devices, to_all(): return lax.all_to_all(copies, axes, 0, 0, tiled=True)  11.6 us
    pallas_call x2, Pallas kernels, orthonormal_rows(): pl.pallas_call(kernel, out_shape=(jax.ShapeDtypeStruct(zt.shape, F32), ja...  9.44 us
  transfers between devices with their start and end apart: 5, of which 4 were waited for; matrix products, arithmetic and copies ran while one was open for 0% of the time, Pallas kernels for 0%

profile of v8, /device:TPU:1, one launch (start us, length us, event | category | flops | bytes accessed | tf_op | source)
XLA Modules:
  0.0 292.4 jit_solution(6918989164945355452)
XLA Ops:
  0.6 8.8 %local_products.1 = (f32[768,128]{1,0:T(8,128)S(1)}, f32[3328,128]{1,0:T(8,128)S(1)}, f32[768,128]{1,0:T(8,128)S(1)}, bf16[3328,128]{1,0:T(8,128)(2,1)S(1)}) custom-call(bf16[2048,1280]{1,0:T(8,128)(2,1)} %tok_hbm.1, bf16[2048,128]{1,0:T(8,128)(2,1)} %smap_hbm.1, bf16[1,8192,128]{2,1,0:T(8,128)(2,1)} %test_hbm.1), custom_call_target="tpu_custom_call" | custom-call | tf_op jit(solution)/shard_map/products/local_products/pallas_call | solution.py:444
  9.4 3.4 %collective-permute-start.1 = (bf16[3328,128]{1,0:T(8,128)(2,1)S(1)}, bf16[3328,128]{1,0:T(8,128)(2,1)S(1)}, u32[]{:S(2)}, u32[]{:S(2)}) collective-permute-start(bf16[3328,128]{1,0:T(8,128)(2,1)S(1)} %get-tuple-element.47), channel_id=1, source_target_pairs={{0,4},{4,0},{1,5},{5,1},{2,6},{6,2},{3,7},{7,3},{8,12},{12,8},{9,1... | collective-permute-start | bytes 2555912 | tf_op jit(solution)/shard_map/over_core/ppermute | solution.py:449
  12.8 0.1 collective-permute-start
  12.9 2.5 collective-permute-done
  15.4 0.1 reduce-precision_convert_fusion
  15.5 0.0 collective-permute-done.1
  15.5 0.2 add_convert_fusion
  15.7 0.1 pad_maximum_fusion
  15.8 22.9 %all_to_all.27 = bf16[16,304,128]{2,1,0:T(8,128)(2,1)S(1)} all-to-all(bf16[16,304,128]{2,1,0:T(8,128)(2,1)S(1)} %pad_maximum_fusion), channel_id=1, replica_groups=mesh['x'=4,'z'=8,'c'=2,'y'=4] {'x','y'}, dimensions={0} | all-to-all | bytes 2490368 | tf_op jit(solution)/shard_map/over_xy/all_to_all | solution.py:452
  38.7 0.2 convert_reduce_fusion
  39.0 0.1 broadcast_in_dim.9
  39.1 24.7 %all_to_all.28 = bf16[8,304,128]{2,1,0:T(8,128)(2,1)S(1)} all-to-all(bf16[8,304,128]{2,1,0:T(8,128)(2,1)S(1)} %broadcast_in_dim.9), channel_id=1, replica_groups=mesh['x'=4,'z'=8,'c'=2,'y'=4] {'z'}, dimensions={0} | all-to-all | bytes 1245184 | tf_op jit(solution)/shard_map/over_z/all_to_all | solution.py:415
  63.8 0.1 convert_reduce_fusion.1
  63.9 0.2 broadcast_in_dim.10
  64.1 18.6 %all_to_all.29.mine = bf16[16,304,128]{2,1,0:T(8,128)(2,1)S(1)} all-to-all(bf16[16,304,128]{2,1,0:T(8,128)(2,1)S(1)} %broadcast_in_dim.10), channel_id=1, replica_groups=mesh['x'=4,'z'=8,'c'=2,'y'=4] {'x','y'}, dimensions={0} | all-to-all | bytes 2490368 | tf_op jit(solution)/shard_map/back_xy/all_to_all | solution.py:415
  82.7 5.1 %collective-permute-start.2 = (bf16[16,304,128]{2,1,0:T(8,128)(2,1)S(1)}, bf16[16,304,128]{2,1,0:T(8,128)(2,1)S(1)}, u32[]{:S(2)}, u32[]{:S(2)}) collective-permute-start(bf16[16,304,128]{2,1,0:T(8,128)(2,1)S(1)} %all_to_all.29.mine), channel_id=1, source_target_pairs={{0,4},{4,0},{1,5},{5,1},{2,6},{6,2},{3,7},{7,3},{8,12},{12,8},{9,1... | collective-permute-start | bytes 3735560 | tf_op jit(solution)/shard_map/back_core/ppermute | solution.py:458
  87.8 2.6 collective-permute-done.2.other
  90.4 18.7 %refine.1 = (f32[20,128]{1,0:T(8,128)S(1)}, f32[128,128]{1,0:T(8,128)}, f32[128,1280]{1,0:T(8,128)S(1)}, s32[1]{0:T(128)}) custom-call(bf16[16,304,128]{2,1,0:T(8,128)(2,1)S(1)} %all_to_all.29.mine, bf16[16,304,128]{2,1,0:T(8,128)(2,1)S(1)} %collective-permute-done.2.other), custom_call_target="tpu_custom_call" | custom-call | tf_op jit(solution)/shard_map/refine/refine/pallas_call | solution.py:460
  109.8 182.0 %conditional.1 = (f32[128,128]{1,0:T(8,128)}, f32[20,128]{1,0:T(8,128)S(1)}) conditional(s32[]{:T(128)} %bitcast.12, (bf16[2048,1280]{1,0:T(8,128)(2,1)}, f32[128,1280]{1,0:T(8,128)S(1)}) %tuple.18, (f32[20,128]{1,0:T(8,128)S(1)}, f32[128,128]{1,0:T(8,128)}) %tuple.19), branch_computations={%region_2.0_spmd, %region_6.0_spmd} | conditional | flops 1342930304 | bytes 15906163 | solution.py:462
  110.0 181.6 %while.11 = (s32[]{:T(128)}, f32[128,1280]{1,0:T(8,128)S(1)}, f32[128,128]{1,0:T(8,128)}, bf16[2048,1280]{1,0:T(8,128)(2,1)}, s32[]{:T(128)}, /*index=5*/f32[]{:T(128)}) while((s32[]{:T(128)}, f32[128,1280]{1,0:T(8,128)S(1)}, f32[128,128]{1,0:T(8,128)}, bf16[2048,1280]{1,0:T(8,128)(2,1)}, s32[]{:T(128)}, /*index=5*/f32[]{:T(128)}) %tuple.41), condition=%wide.region_5.0_spmd, body=%wide.region_3.0_spmd.sunk | while | flops 1342930304 | bytes 15864937 | solution.py:408
  110.0 7.4 %fusion.21 = f32[128,1280]{1,0:T(8,128)S(1)} fusion(bf16[2048,1280]{1,0:T(8,128)(2,1)} %get-tuple-element.124, f32[128,1280]{1,0:T(8,128)S(1)} %get-tuple-element.116), kind=kOutput, calls=%fused_computation.1.clone.1 | convolution fusion | flops 1342603264 | bytes 6553600 | tf_op jit(solution)/shard_map/check/cond/branch_0_fun/while/body/eval_jaxpr/dot_general | solution.py:403
  117.4 0.2 reshape.52
  117.6 38.9 %all_to_all.30 = f32[256,5,128]{2,1,0:T(8,128)S(1)} all-to-all(f32[256,5,128]{2,1,0:T(8,128)S(1)} %reshape.52), channel_id=1, replica_groups=mesh['x'=4,'z'=8,'c'=2,'y'=4] {'x','z','c','y'}, dimensions={0} | all-to-all | bytes 1310720 | tf_op jit(solution)/shard_map/check/cond/branch_0_fun/while/body/eval_jaxpr/all_to_all | solution.py:405
  156.5 0.3 reduce_sum.32
  156.8 1.0 broadcast_in_dim.12
  157.8 5.8 %all-to-all-start.1 = ((f32[256,5,128]{2,1,0:T(8,128)}), f32[256,5,128]{2,1,0:T(8,128)S(1)}, u32[]{:S(2)}, u32[]{:S(2)}) async-start(f32[256,5,128]{2,1,0:T(8,128)} %broadcast_in_dim.12), calls=%async_computation.1 | async-start | bytes 2097152 | tf_op jit(solution)/shard_map/check/cond/branch_0_fun/while/body/eval_jaxpr/all_to_all | solution.py:415
  163.6 32.6 %all-to-all-done.1 = f32[256,5,128]{2,1,0:T(8,128)S(1)} async-done(((f32[256,5,128]{2,1,0:T(8,128)}), f32[256,5,128]{2,1,0:T(8,128)S(1)}, u32[]{:S(2)}, u32[]{:S(2)}) %all-to-all-start.1) | async-done | bytes 655392 | tf_op jit(solution)/shard_map/check/cond/branch_0_fun/while/body/eval_jaxpr/all_to_all | solution.py:415
  196.2 0.1 broadcast_multiply_fusion.2
  196.3 0.2 div.9.zt_ref
  196.5 4.7 %orthonormal_rows.1 = (f32[128,1280]{1,0:T(8,128)S(1)}, f32[128,128]{1,0:T(8,128)}) custom-call(f32[128,1280]{1,0:T(8,128)S(1)} %div.9.zt_ref), custom_call_target="tpu_custom_call" | custom-call | tf_op jit(solution)/shard_map/check/cond/branch_0_fun/while/body/eval_jaxpr/orthonormal_rows/pallas_call | solution.py:389
  201.2 7.4 %fusion.21 = f32[128,1280]{1,0:T(8,128)S(1)} fusion(bf16[2048,1280]{1,0:T(8,128)(2,1)} %get-tuple-element.124, f32[128,1280]{1,0:T(8,128)S(1)} %get-tuple-element.116), kind=kOutput, calls=%fused_computation.1.clone.1 | convolution fusion | flops 1342603264 | bytes 6553600 | tf_op jit(solution)/shard_map/check/cond/branch_0_fun/while/body/eval_jaxpr/dot_general | solution.py:403
  208.6 0.2 reshape.52
  208.8 38.1 %all_to_all.30 = f32[256,5,128]{2,1,0:T(8,128)S(1)} all-to-all(f32[256,5,128]{2,1,0:T(8,128)S(1)} %reshape.52), channel_id=1, replica_groups=mesh['x'=4,'z'=8,'c'=2,'y'=4] {'x','z','c','y'}, dimensions={0} | all-to-all | bytes 1310720 | tf_op jit(solution)/shard_map/check/cond/branch_0_fun/while/body/eval_jaxpr/all_to_all | solution.py:405
  246.9 0.3 reduce_sum.32
  247.2 1.0 broadcast_in_dim.12
  248.2 5.8 %all-to-all-start.1 = ((f32[256,5,128]{2,1,0:T(8,128)}), f32[256,5,128]{2,1,0:T(8,128)S(1)}, u32[]{:S(2)}, u32[]{:S(2)}) async-start(f32[256,5,128]{2,1,0:T(8,128)} %broadcast_in_dim.12), calls=%async_computation.1 | async-start | bytes 2097152 | tf_op jit(solution)/shard_map/check/cond/branch_0_fun/while/body/eval_jaxpr/all_to_all | solution.py:415
  254.0 32.6 %all-to-all-done.1 = f32[256,5,128]{2,1,0:T(8,128)S(1)} async-done(((f32[256,5,128]{2,1,0:T(8,128)}), f32[256,5,128]{2,1,0:T(8,128)S(1)}, u32[]{:S(2)}, u32[]{:S(2)}) %all-to-all-start.1) | async-done | bytes 655392 | tf_op jit(solution)/shard_map/check/cond/branch_0_fun/while/body/eval_jaxpr/all_to_all | solution.py:415
  286.6 0.1 broadcast_multiply_fusion.2
  286.7 0.2 div.9.zt_ref
  286.9 4.7 %orthonormal_rows.1 = (f32[128,1280]{1,0:T(8,128)S(1)}, f32[128,128]{1,0:T(8,128)}) custom-call(f32[128,1280]{1,0:T(8,128)S(1)} %div.9.zt_ref), custom_call_target="tpu_custom_call" | custom-call | tf_op jit(solution)/shard_map/check/cond/branch_0_fun/while/body/eval_jaxpr/orthonormal_rows/pallas_call | solution.py:389
  291.6 0.1 dynamic-slice_bitcast_fusion
  291.7 0.1 copy.13
  291.8 0.0 copy-start
  291.8 0.6 copy-done
  (7 shorter events, 0.1 us)
Async XLA Ops:
  9.4 6.1 %collective-permute-start.1 = (bf16[3328,128]{1,0:T(8,128)(2,1)S(1)}, bf16[3328,128]{1,0:T(8,128)(2,1)S(1)}, u32[]{:S(2)}, u32[]{:S(2)}) collective-permute-start(bf16[3328,128]{1,0:T(8,128)(2,1)S(1)} %get-tuple-element.47), channel_id=1, source_target_pairs={{0,4},{4,0},{1,5},{5,1},{2,6},{6,2},{3,7},{7,3},{8,12},{12,8},{9,1... | collective-permute-start | bytes 2555912 | tf_op jit(solution)/shard_map/over_core/ppermute | solution.py:449
  12.8 2.6 collective-permute-start
  82.7 7.7 %collective-permute-start.2 = (bf16[16,304,128]{2,1,0:T(8,128)(2,1)S(1)}, bf16[16,304,128]{2,1,0:T(8,128)(2,1)S(1)}, u32[]{:S(2)}, u32[]{:S(2)}) collective-permute-start(bf16[16,304,128]{2,1,0:T(8,128)(2,1)S(1)} %all_to_all.29.mine), channel_id=1, source_target_pairs={{0,4},{4,0},{1,5},{5,1},{2,6},{6,2},{3,7},{7,3},{8,12},{12,8},{9,1... | collective-permute-start | bytes 3735560 | tf_op jit(solution)/shard_map/back_core/ppermute | solution.py:458
  157.8 38.4 %all-to-all-start.1 = ((f32[256,5,128]{2,1,0:T(8,128)}), f32[256,5,128]{2,1,0:T(8,128)S(1)}, u32[]{:S(2)}, u32[]{:S(2)}) async-start(f32[256,5,128]{2,1,0:T(8,128)} %broadcast_in_dim.12), calls=%async_computation.1 | async-start | bytes 2097152 | tf_op jit(solution)/shard_map/check/cond/branch_0_fun/while/body/eval_jaxpr/all_to_all | solution.py:415
  248.2 38.4 %all-to-all-start.1 = ((f32[256,5,128]{2,1,0:T(8,128)}), f32[256,5,128]{2,1,0:T(8,128)S(1)}, u32[]{:S(2)}, u32[]{:S(2)}) async-start(f32[256,5,128]{2,1,0:T(8,128)} %broadcast_in_dim.12), calls=%async_computation.1 | async-start | bytes 2097152 | tf_op jit(solution)/shard_map/check/cond/branch_0_fun/while/body/eval_jaxpr/all_to_all | solution.py:415
  291.8 0.6 copy-start

commit v9 on v8

--- a/solution.py
+++ b/solution.py
@@ -294,6 +294,9 @@
                 v = packed_rows(cov, at, LANES, pack.cov).astype(F32)
                 if i < j:
                     put(i, j, v)
+                    if i + 1 == j and j % 2:
+                        rows = slice(j * LANES, (j + 1) * LANES)
+                        dense[rows, i * LANES : (i + 1) * LANES] = v.T.astype(BF16)
                 else:
                     flipped = v.T
                     put(i, i, jnp.where(row < col, v, flipped))
@@ -332,14 +335,14 @@
             @pl.when(step < ITERS)
             def _():
                 vb = fresh.astype(BF16)
-                for j in range(n):
-                    high = (j + 1) * LANES
-                    rj = slice(j * LANES, high)
+                for pair in range(n // 2):
+                    high = 2 * (pair + 1) * LANES
+                    rj = slice(2 * pair * LANES, high)
                     z = vb[:, rj].astype(F32) * diagonal[:, rj]
                     z = z + lax.dot_general(
                         vb[:, :high], dense[:high, rj], NN, preferred_element_type=F32
                     )
-                    if j + 1 < n:
+                    if high < width:
                         z = z + lax.dot_general(
                             vb[:, high:], dense[rj, high:], NT, preferred_element_type=F32
                         )

time: 293 us -> 292 us (level)
  no operation moved by 1% of the time
where the time goes in v9:
time: 292 us
  blocking collectives  143 us (49%)
  waiting for transfers between devices  70.2 us (24%)
  Pallas kernels  36.4 us (12%)
  starting transfers between devices  20.2 us (7%)
  matrix products  14.8 us (5%)
  local copies, waits for them, and re-layouts  3.84 us (1%)
    all_to_all x2, blocking collectives, step(): share = jnp.sum(lax.all_to_all(tiles, ALL, 0, 0, tiled=True), axis=0)  77 us
    all_to_all x2, waiting for transfers between devices, to_all(): return lax.all_to_all(copies, axes, 0, 0, tiled=True)  65.2 us
    all_to_all x2, blocking collectives, to_all(): return lax.all_to_all(copies, axes, 0, 0, tiled=True)  43.3 us
    all_to_all x1, blocking collectives, body(): piece = summed(lax.all_to_all(tiles, ('x', 'y'), 0, 0, tiled=True), pack)  22.9 us
    pallas_call x1, Pallas kernels, body(): refine(pack, width, k, strip, total_tokens)(mine, other)  18.1 us
    dot_general x2, matrix products, step(): local = lax.dot_general(projected, tokens, TN, preferred_element_type=F32)  14.8 us
    all_to_all x2, starting transfers between devices, to_all(): return lax.all_to_all(copies, axes, 0, 0, tiled=True)  11.6 us
    pallas_call x2, Pallas kernels, orthonormal_rows(): pl.pallas_call(kernel, out_shape=(jax.ShapeDtypeStruct(zt.shape, F32), ja...  9.44 us
  transfers between devices with their start and end apart: 5, of which 4 were waited for; matrix products, arithmetic and copies ran while one was open for 0% of the time, Pallas kernels for 0%

profile of v9, /device:TPU:1, one launch (start us, length us, event | category | flops | bytes accessed | tf_op | source)
XLA Modules:
  0.0 291.8 jit_solution(10622000132341663996)
XLA Ops:
  0.6 8.8 %local_products.1 = (f32[768,128]{1,0:T(8,128)S(1)}, f32[3328,128]{1,0:T(8,128)S(1)}, f32[768,128]{1,0:T(8,128)S(1)}, bf16[3328,128]{1,0:T(8,128)(2,1)S(1)}) custom-call(bf16[2048,1280]{1,0:T(8,128)(2,1)} %tok_hbm.1, bf16[2048,128]{1,0:T(8,128)(2,1)} %smap_hbm.1, bf16[1,8192,128]{2,1,0:T(8,128)(2,1)} %test_hbm.1), custom_call_target="tpu_custom_call" | custom-call | tf_op jit(solution)/shard_map/products/local_products/pallas_call | solution.py:447
  9.4 3.4 %collective-permute-start.1 = (bf16[3328,128]{1,0:T(8,128)(2,1)S(1)}, bf16[3328,128]{1,0:T(8,128)(2,1)S(1)}, u32[]{:S(2)}, u32[]{:S(2)}) collective-permute-start(bf16[3328,128]{1,0:T(8,128)(2,1)S(1)} %get-tuple-element.47), channel_id=1, source_target_pairs={{0,4},{4,0},{1,5},{5,1},{2,6},{6,2},{3,7},{7,3},{8,12},{12,8},{9,1... | collective-permute-start | bytes 2555912 | tf_op jit(solution)/shard_map/over_core/ppermute | solution.py:452
  12.8 0.1 collective-permute-start
  12.9 2.5 collective-permute-done
  15.4 0.1 reduce-precision_convert_fusion
  15.5 0.0 collective-permute-done.1
  15.5 0.2 add_convert_fusion
  15.7 0.1 pad_maximum_fusion
  15.8 22.9 %all_to_all.27 = bf16[16,304,128]{2,1,0:T(8,128)(2,1)S(1)} all-to-all(bf16[16,304,128]{2,1,0:T(8,128)(2,1)S(1)} %pad_maximum_fusion), channel_id=1, replica_groups=mesh['x'=4,'z'=8,'c'=2,'y'=4] {'x','y'}, dimensions={0} | all-to-all | bytes 2490368 | tf_op jit(solution)/shard_map/over_xy/all_to_all | solution.py:455
  38.7 0.2 convert_reduce_fusion
  39.0 0.1 broadcast_in_dim.9
  39.1 24.7 %all_to_all.28 = bf16[8,304,128]{2,1,0:T(8,128)(2,1)S(1)} all-to-all(bf16[8,304,128]{2,1,0:T(8,128)(2,1)S(1)} %broadcast_in_dim.9), channel_id=1, replica_groups=mesh['x'=4,'z'=8,'c'=2,'y'=4] {'z'}, dimensions={0} | all-to-all | bytes 1245184 | tf_op jit(solution)/shard_map/over_z/all_to_all | solution.py:418
  63.8 0.1 convert_reduce_fusion.1
  63.9 0.2 broadcast_in_dim.10
  64.1 18.6 %all_to_all.29.mine = bf16[16,304,128]{2,1,0:T(8,128)(2,1)S(1)} all-to-all(bf16[16,304,128]{2,1,0:T(8,128)(2,1)S(1)} %broadcast_in_dim.10), channel_id=1, replica_groups=mesh['x'=4,'z'=8,'c'=2,'y'=4] {'x','y'}, dimensions={0} | all-to-all | bytes 2490368 | tf_op jit(solution)/shard_map/back_xy/all_to_all | solution.py:418
  82.7 5.1 %collective-permute-start.2 = (bf16[16,304,128]{2,1,0:T(8,128)(2,1)S(1)}, bf16[16,304,128]{2,1,0:T(8,128)(2,1)S(1)}, u32[]{:S(2)}, u32[]{:S(2)}) collective-permute-start(bf16[16,304,128]{2,1,0:T(8,128)(2,1)S(1)} %all_to_all.29.mine), channel_id=1, source_target_pairs={{0,4},{4,0},{1,5},{5,1},{2,6},{6,2},{3,7},{7,3},{8,12},{12,8},{9,1... | collective-permute-start | bytes 3735560 | tf_op jit(solution)/shard_map/back_core/ppermute | solution.py:461
  87.8 2.6 collective-permute-done.2.other
  90.4 18.1 %refine.1 = (f32[20,128]{1,0:T(8,128)S(1)}, f32[128,128]{1,0:T(8,128)}, f32[128,1280]{1,0:T(8,128)S(1)}, s32[1]{0:T(128)}) custom-call(bf16[16,304,128]{2,1,0:T(8,128)(2,1)S(1)} %all_to_all.29.mine, bf16[16,304,128]{2,1,0:T(8,128)(2,1)S(1)} %collective-permute-done.2.other), custom_call_target="tpu_custom_call" | custom-call | tf_op jit(solution)/shard_map/refine/refine/pallas_call | solution.py:463
  109.2 182.0 %conditional.1 = (f32[128,128]{1,0:T(8,128)}, f32[20,128]{1,0:T(8,128)S(1)}) conditional(s32[]{:T(128)} %bitcast.12, (bf16[2048,1280]{1,0:T(8,128)(2,1)}, f32[128,1280]{1,0:T(8,128)S(1)}) %tuple.18, (f32[20,128]{1,0:T(8,128)S(1)}, f32[128,128]{1,0:T(8,128)}) %tuple.19), branch_computations={%region_2.0_spmd, %region_6.0_spmd} | conditional | flops 1342930304 | bytes 15906163 | solution.py:465
  109.5 181.6 %while.11 = (s32[]{:T(128)}, f32[128,1280]{1,0:T(8,128)S(1)}, f32[128,128]{1,0:T(8,128)}, bf16[2048,1280]{1,0:T(8,128)(2,1)}, s32[]{:T(128)}, /*index=5*/f32[]{:T(128)}) while((s32[]{:T(128)}, f32[128,1280]{1,0:T(8,128)S(1)}, f32[128,128]{1,0:T(8,128)}, bf16[2048,1280]{1,0:T(8,128)(2,1)}, s32[]{:T(128)}, /*index=5*/f32[]{:T(128)}) %tuple.41), condition=%wide.region_5.0_spmd, body=%wide.region_3.0_spmd.sunk | while | flops 1342930304 | bytes 15864937 | solution.py:411
  109.5 7.4 %fusion.21 = f32[128,1280]{1,0:T(8,128)S(1)} fusion(bf16[2048,1280]{1,0:T(8,128)(2,1)} %get-tuple-element.124, f32[128,1280]{1,0:T(8,128)S(1)} %get-tuple-element.116), kind=kOutput, calls=%fused_computation.1.clone.1 | convolution fusion | flops 1342603264 | bytes 6553600 | tf_op jit(solution)/shard_map/check/cond/branch_0_fun/while/body/eval_jaxpr/dot_general | solution.py:406
  116.9 0.2 reshape.52
  117.1 38.9 %all_to_all.30 = f32[256,5,128]{2,1,0:T(8,128)S(1)} all-to-all(f32[256,5,128]{2,1,0:T(8,128)S(1)} %reshape.52), channel_id=1, replica_groups=mesh['x'=4,'z'=8,'c'=2,'y'=4] {'x','z','c','y'}, dimensions={0} | all-to-all | bytes 1310720 | tf_op jit(solution)/shard_map/check/cond/branch_0_fun/while/body/eval_jaxpr/all_to_all | solution.py:408
  155.9 0.3 reduce_sum.32
  156.2 1.0 broadcast_in_dim.12
  157.3 5.8 %all-to-all-start.1 = ((f32[256,5,128]{2,1,0:T(8,128)}), f32[256,5,128]{2,1,0:T(8,128)S(1)}, u32[]{:S(2)}, u32[]{:S(2)}) async-start(f32[256,5,128]{2,1,0:T(8,128)} %broadcast_in_dim.12), calls=%async_computation.1 | async-start | bytes 2097152 | tf_op jit(solution)/shard_map/check/cond/branch_0_fun/while/body/eval_jaxpr/all_to_all | solution.py:418
  163.1 32.6 %all-to-all-done.1 = f32[256,5,128]{2,1,0:T(8,128)S(1)} async-done(((f32[256,5,128]{2,1,0:T(8,128)}), f32[256,5,128]{2,1,0:T(8,128)S(1)}, u32[]{:S(2)}, u32[]{:S(2)}) %all-to-all-start.1) | async-done | bytes 655392 | tf_op jit(solution)/shard_map/check/cond/branch_0_fun/while/body/eval_jaxpr/all_to_all | solution.py:418
  195.7 0.1 broadcast_multiply_fusion.2
  195.7 0.2 div.9.zt_ref
  195.9 4.7 %orthonormal_rows.1 = (f32[128,1280]{1,0:T(8,128)S(1)}, f32[128,128]{1,0:T(8,128)}) custom-call(f32[128,1280]{1,0:T(8,128)S(1)} %div.9.zt_ref), custom_call_target="tpu_custom_call" | custom-call | tf_op jit(solution)/shard_map/check/cond/branch_0_fun/while/body/eval_jaxpr/orthonormal_rows/pallas_call | solution.py:392
  200.7 7.4 %fusion.21 = f32[128,1280]{1,0:T(8,128)S(1)} fusion(bf16[2048,1280]{1,0:T(8,128)(2,1)} %get-tuple-element.124, f32[128,1280]{1,0:T(8,128)S(1)} %get-tuple-element.116), kind=kOutput, calls=%fused_computation.1.clone.1 | convolution fusion | flops 1342603264 | bytes 6553600 | tf_op jit(solution)/shard_map/check/cond/branch_0_fun/while/body/eval_jaxpr/dot_general | solution.py:406
  208.1 0.2 reshape.52
  208.3 38.1 %all_to_all.30 = f32[256,5,128]{2,1,0:T(8,128)S(1)} all-to-all(f32[256,5,128]{2,1,0:T(8,128)S(1)} %reshape.52), channel_id=1, replica_groups=mesh['x'=4,'z'=8,'c'=2,'y'=4] {'x','z','c','y'}, dimensions={0} | all-to-all | bytes 1310720 | tf_op jit(solution)/shard_map/check/cond/branch_0_fun/while/body/eval_jaxpr/all_to_all | solution.py:408
  246.3 0.3 reduce_sum.32
  246.6 1.0 broadcast_in_dim.12
  247.7 5.8 %all-to-all-start.1 = ((f32[256,5,128]{2,1,0:T(8,128)}), f32[256,5,128]{2,1,0:T(8,128)S(1)}, u32[]{:S(2)}, u32[]{:S(2)}) async-start(f32[256,5,128]{2,1,0:T(8,128)} %broadcast_in_dim.12), calls=%async_computation.1 | async-start | bytes 2097152 | tf_op jit(solution)/shard_map/check/cond/branch_0_fun/while/body/eval_jaxpr/all_to_all | solution.py:418
  253.5 32.6 %all-to-all-done.1 = f32[256,5,128]{2,1,0:T(8,128)S(1)} async-done(((f32[256,5,128]{2,1,0:T(8,128)}), f32[256,5,128]{2,1,0:T(8,128)S(1)}, u32[]{:S(2)}, u32[]{:S(2)}) %all-to-all-start.1) | async-done | bytes 655392 | tf_op jit(solution)/shard_map/check/cond/branch_0_fun/while/body/eval_jaxpr/all_to_all | solution.py:418
  286.0 0.1 broadcast_multiply_fusion.2
  286.1 0.2 div.9.zt_ref
  286.3 4.7 %orthonormal_rows.1 = (f32[128,1280]{1,0:T(8,128)S(1)}, f32[128,128]{1,0:T(8,128)}) custom-call(f32[128,1280]{1,0:T(8,128)S(1)} %div.9.zt_ref), custom_call_target="tpu_custom_call" | custom-call | tf_op jit(solution)/shard_map/check/cond/branch_0_fun/while/body/eval_jaxpr/orthonormal_rows/pallas_call | solution.py:392
  291.1 0.1 dynamic-slice_bitcast_fusion
  291.1 0.1 copy.13
  291.2 0.0 copy-start
  291.2 0.6 copy-done
  (7 shorter events, 0.1 us)
Async XLA Ops:
  9.4 6.1 %collective-permute-start.1 = (bf16[3328,128]{1,0:T(8,128)(2,1)S(1)}, bf16[3328,128]{1,0:T(8,128)(2,1)S(1)}, u32[]{:S(2)}, u32[]{:S(2)}) collective-permute-start(bf16[3328,128]{1,0:T(8,128)(2,1)S(1)} %get-tuple-element.47), channel_id=1, source_target_pairs={{0,4},{4,0},{1,5},{5,1},{2,6},{6,2},{3,7},{7,3},{8,12},{12,8},{9,1... | collective-permute-start | bytes 2555912 | tf_op jit(solution)/shard_map/over_core/ppermute | solution.py:452
  12.8 2.6 collective-permute-start
  82.7 7.7 %collective-permute-start.2 = (bf16[16,304,128]{2,1,0:T(8,128)(2,1)S(1)}, bf16[16,304,128]{2,1,0:T(8,128)(2,1)S(1)}, u32[]{:S(2)}, u32[]{:S(2)}) collective-permute-start(bf16[16,304,128]{2,1,0:T(8,128)(2,1)S(1)} %all_to_all.29.mine), channel_id=1, source_target_pairs={{0,4},{4,0},{1,5},{5,1},{2,6},{6,2},{3,7},{7,3},{8,12},{12,8},{9,1... | collective-permute-start | bytes 3735560 | tf_op jit(solution)/shard_map/back_core/ppermute | solution.py:461
  157.3 38.4 %all-to-all-start.1 = ((f32[256,5,128]{2,1,0:T(8,128)}), f32[256,5,128]{2,1,0:T(8,128)S(1)}, u32[]{:S(2)}, u32[]{:S(2)}) async-start(f32[256,5,128]{2,1,0:T(8,128)} %broadcast_in_dim.12), calls=%async_computation.1 | async-start | bytes 2097152 | tf_op jit(solution)/shard_map/check/cond/branch_0_fun/while/body/eval_jaxpr/all_to_all | solution.py:418
  247.7 38.4 %all-to-all-start.1 = ((f32[256,5,128]{2,1,0:T(8,128)}), f32[256,5,128]{2,1,0:T(8,128)S(1)}, u32[]{:S(2)}, u32[]{:S(2)}) async-start(f32[256,5,128]{2,1,0:T(8,128)} %broadcast_in_dim.12), calls=%async_computation.1 | async-start | bytes 2097152 | tf_op jit(solution)/shard_map/check/cond/branch_0_fun/while/body/eval_jaxpr/all_to_all | solution.py:418
  291.2 0.6 copy-start

commit v10 on v9

--- a/solution.py
+++ b/solution.py
@@ -14,7 +14,6 @@
 MIB = 1024 * 1024
 F32 = jnp.float32
 BF16 = jnp.bfloat16
-HI = lax.Precision.HIGHEST
 NN = (((1,), (0,)), ((), ()))
 NT = (((1,), (1,)), ((), ()))
 TN = (((0,), (0,)), ((), ()))
@@ -196,7 +195,11 @@
         if b + 1 == stop and stop < blocks:
             above = jnp.concatenate(factor[-segment:], axis=0)
             beside = jnp.concatenate([above, jnp.concatenate(inverse[-segment:], axis=0)], axis=1)
-            update = lax.dot_general(above, beside, TN, precision=HI, preferred_element_type=F32)
+            ah, am, al = thirds(above)
+            bh, bm, bl = thirds(beside)
+            left = jnp.concatenate([al, ah, am, am, ah, ah], axis=0)
+            right = jnp.concatenate([bh, bl, bm, bh, bm, bh], axis=0)
+            update = lax.dot_general(left, right, TN, preferred_element_type=F32)
             for o in range(stop, blocks):
                 rows = slice(o * SUB, (o + 1) * SUB)
                 work[o] = work[o] - update[rows, :k]
@@ -262,8 +265,8 @@
                 loads.append(
                     pltpu.make_async_copy(side.at[:, rows], to.at[place], sem.at[len(loads)])
                 )
-        for load in loads:
-            load.start()
+        for at in (0, 1, 3, 4, 2, 5):
+            loads[at].start()
         for at in (0, 1, 3, 4):
             loads[at].wait()
 

time: 292 us -> 291 us (level)
  no operation moved by 1% of the time
where the time goes in v10:
time: 291 us; the launch traced here: 290 us
  blocking collectives  143 us (49%)
  waiting for transfers between devices  70.2 us (24%)
  Pallas kernels  34.7 us (12%)
  starting transfers between devices  20.2 us (7%)
  matrix products  14.8 us (5%)
  local copies, waits for them, and re-layouts  3.84 us (1%)
    all_to_all x2, blocking collectives, step(): share = jnp.sum(lax.all_to_all(tiles, ALL, 0, 0, tiled=True), axis=0)  77 us
    all_to_all x2, waiting for transfers between devices, to_all(): return lax.all_to_all(copies, axes, 0, 0, tiled=True)  65.2 us
    all_to_all x2, blocking collectives, to_all(): return lax.all_to_all(copies, axes, 0, 0, tiled=True)  43.3 us
    all_to_all x1, blocking collectives, body(): piece = summed(lax.all_to_all(tiles, ('x', 'y'), 0, 0, tiled=True), pack)  22.9 us
    pallas_call x1, Pallas kernels, body(): refine(pack, width, k, strip, total_tokens)(mine, other)  17 us
    dot_general x2, matrix products, step(): local = lax.dot_general(projected, tokens, TN, preferred_element_type=F32)  14.8 us
    all_to_all x2, starting transfers between devices, to_all(): return lax.all_to_all(copies, axes, 0, 0, tiled=True)  11.6 us
    pallas_call x2, Pallas kernels, orthonormal_rows(): pl.pallas_call(kernel, out_shape=(jax.ShapeDtypeStruct(zt.shape, F32), ja...  8.98 us
  transfers between devices with their start and end apart: 5, of which 4 were waited for; matrix products, arithmetic and copies ran while one was open for 0% of the time, Pallas kernels for 0%

profile of v10, /device:TPU:1, one launch (start us, length us, event | category | flops | bytes accessed | tf_op | source)
XLA Modules:
  0.0 290.2 jit_solution(14527350055765074943)
XLA Ops:
  0.6 8.8 %local_products.1 = (f32[768,128]{1,0:T(8,128)S(1)}, f32[3328,128]{1,0:T(8,128)S(1)}, f32[768,128]{1,0:T(8,128)S(1)}, bf16[3328,128]{1,0:T(8,128)(2,1)S(1)}) custom-call(bf16[2048,1280]{1,0:T(8,128)(2,1)} %tok_hbm.1, bf16[2048,128]{1,0:T(8,128)(2,1)} %smap_hbm.1, bf16[1,8192,128]{2,1,0:T(8,128)(2,1)} %test_hbm.1), custom_call_target="tpu_custom_call" | custom-call | tf_op jit(solution)/shard_map/products/local_products/pallas_call | solution.py:450
  9.4 3.4 %collective-permute-start.1 = (bf16[3328,128]{1,0:T(8,128)(2,1)S(1)}, bf16[3328,128]{1,0:T(8,128)(2,1)S(1)}, u32[]{:S(2)}, u32[]{:S(2)}) collective-permute-start(bf16[3328,128]{1,0:T(8,128)(2,1)S(1)} %get-tuple-element.47), channel_id=1, source_target_pairs={{0,4},{4,0},{1,5},{5,1},{2,6},{6,2},{3,7},{7,3},{8,12},{12,8},{9,1... | collective-permute-start | bytes 2555912 | tf_op jit(solution)/shard_map/over_core/ppermute | solution.py:455
  12.8 0.1 collective-permute-start
  12.9 2.5 collective-permute-done
  15.4 0.1 reduce-precision_convert_fusion
  15.5 0.0 collective-permute-done.1
  15.5 0.2 add_convert_fusion
  15.7 0.1 pad_maximum_fusion
  15.8 22.9 %all_to_all.27 = bf16[16,304,128]{2,1,0:T(8,128)(2,1)S(1)} all-to-all(bf16[16,304,128]{2,1,0:T(8,128)(2,1)S(1)} %pad_maximum_fusion), channel_id=1, replica_groups=mesh['x'=4,'z'=8,'c'=2,'y'=4] {'x','y'}, dimensions={0} | all-to-all | bytes 2490368 | tf_op jit(solution)/shard_map/over_xy/all_to_all | solution.py:458
  38.7 0.2 convert_reduce_fusion
  39.0 0.1 broadcast_in_dim.9
  39.1 24.7 %all_to_all.28 = bf16[8,304,128]{2,1,0:T(8,128)(2,1)S(1)} all-to-all(bf16[8,304,128]{2,1,0:T(8,128)(2,1)S(1)} %broadcast_in_dim.9), channel_id=1, replica_groups=mesh['x'=4,'z'=8,'c'=2,'y'=4] {'z'}, dimensions={0} | all-to-all | bytes 1245184 | tf_op jit(solution)/shard_map/over_z/all_to_all | solution.py:421
  63.8 0.1 convert_reduce_fusion.1
  63.9 0.2 broadcast_in_dim.10
  64.1 18.6 %all_to_all.29.mine = bf16[16,304,128]{2,1,0:T(8,128)(2,1)S(1)} all-to-all(bf16[16,304,128]{2,1,0:T(8,128)(2,1)S(1)} %broadcast_in_dim.10), channel_id=1, replica_groups=mesh['x'=4,'z'=8,'c'=2,'y'=4] {'x','y'}, dimensions={0} | all-to-all | bytes 2490368 | tf_op jit(solution)/shard_map/back_xy/all_to_all | solution.py:421
  82.7 5.1 %collective-permute-start.2 = (bf16[16,304,128]{2,1,0:T(8,128)(2,1)S(1)}, bf16[16,304,128]{2,1,0:T(8,128)(2,1)S(1)}, u32[]{:S(2)}, u32[]{:S(2)}) collective-permute-start(bf16[16,304,128]{2,1,0:T(8,128)(2,1)S(1)} %all_to_all.29.mine), channel_id=1, source_target_pairs={{0,4},{4,0},{1,5},{5,1},{2,6},{6,2},{3,7},{7,3},{8,12},{12,8},{9,1... | collective-permute-start | bytes 3735560 | tf_op jit(solution)/shard_map/back_core/ppermute | solution.py:464
  87.8 2.6 collective-permute-done.2.other
  90.4 17.0 %refine.1 = (f32[20,128]{1,0:T(8,128)S(1)}, f32[128,128]{1,0:T(8,128)}, f32[128,1280]{1,0:T(8,128)S(1)}, s32[1]{0:T(128)}) custom-call(bf16[16,304,128]{2,1,0:T(8,128)(2,1)S(1)} %all_to_all.29.mine, bf16[16,304,128]{2,1,0:T(8,128)(2,1)S(1)} %collective-permute-done.2.other), custom_call_target="tpu_custom_call" | custom-call | tf_op jit(solution)/shard_map/refine/refine/pallas_call | solution.py:466
  108.0 181.5 %conditional.1 = (f32[128,128]{1,0:T(8,128)}, f32[20,128]{1,0:T(8,128)S(1)}) conditional(s32[]{:T(128)} %bitcast.12, (bf16[2048,1280]{1,0:T(8,128)(2,1)}, f32[128,1280]{1,0:T(8,128)S(1)}) %tuple.18, (f32[20,128]{1,0:T(8,128)S(1)}, f32[128,128]{1,0:T(8,128)}) %tuple.19), branch_computations={%region_2.0_spmd, %region_6.0_spmd} | conditional | flops 1342930304 | bytes 15906163 | solution.py:468
  108.3 181.1 %while.11 = (s32[]{:T(128)}, f32[128,1280]{1,0:T(8,128)S(1)}, f32[128,128]{1,0:T(8,128)}, bf16[2048,1280]{1,0:T(8,128)(2,1)}, s32[]{:T(128)}, /*index=5*/f32[]{:T(128)}) while((s32[]{:T(128)}, f32[128,1280]{1,0:T(8,128)S(1)}, f32[128,128]{1,0:T(8,128)}, bf16[2048,1280]{1,0:T(8,128)(2,1)}, s32[]{:T(128)}, /*index=5*/f32[]{:T(128)}) %tuple.41), condition=%wide.region_5.0_spmd, body=%wide.region_3.0_spmd.sunk | while | flops 1342930304 | bytes 15864937 | solution.py:414
  108.3 7.4 %fusion.21 = f32[128,1280]{1,0:T(8,128)S(1)} fusion(bf16[2048,1280]{1,0:T(8,128)(2,1)} %get-tuple-element.124, f32[128,1280]{1,0:T(8,128)S(1)} %get-tuple-element.116), kind=kOutput, calls=%fused_computation.1.clone.1 | convolution fusion | flops 1342603264 | bytes 6553600 | tf_op jit(solution)/shard_map/check/cond/branch_0_fun/while/body/eval_jaxpr/dot_general | solution.py:409
  115.7 0.2 reshape.52
  115.9 38.9 %all_to_all.30 = f32[256,5,128]{2,1,0:T(8,128)S(1)} all-to-all(f32[256,5,128]{2,1,0:T(8,128)S(1)} %reshape.52), channel_id=1, replica_groups=mesh['x'=4,'z'=8,'c'=2,'y'=4] {'x','z','c','y'}, dimensions={0} | all-to-all | bytes 1310720 | tf_op jit(solution)/shard_map/check/cond/branch_0_fun/while/body/eval_jaxpr/all_to_all | solution.py:411
  154.8 0.3 reduce_sum.32
  155.0 1.0 broadcast_in_dim.12
  156.1 5.8 %all-to-all-start.1 = ((f32[256,5,128]{2,1,0:T(8,128)}), f32[256,5,128]{2,1,0:T(8,128)S(1)}, u32[]{:S(2)}, u32[]{:S(2)}) async-start(f32[256,5,128]{2,1,0:T(8,128)} %broadcast_in_dim.12), calls=%async_computation.1 | async-start | bytes 2097152 | tf_op jit(solution)/shard_map/check/cond/branch_0_fun/while/body/eval_jaxpr/all_to_all | solution.py:421
  161.9 32.6 %all-to-all-done.1 = f32[256,5,128]{2,1,0:T(8,128)S(1)} async-done(((f32[256,5,128]{2,1,0:T(8,128)}), f32[256,5,128]{2,1,0:T(8,128)S(1)}, u32[]{:S(2)}, u32[]{:S(2)}) %all-to-all-start.1) | async-done | bytes 655392 | tf_op jit(solution)/shard_map/check/cond/branch_0_fun/while/body/eval_jaxpr/all_to_all | solution.py:421
  194.5 0.1 broadcast_multiply_fusion.2
  194.6 0.2 div.9.zt_ref
  194.8 4.5 %orthonormal_rows.1 = (f32[128,1280]{1,0:T(8,128)S(1)}, f32[128,128]{1,0:T(8,128)}) custom-call(f32[128,1280]{1,0:T(8,128)S(1)} %div.9.zt_ref), custom_call_target="tpu_custom_call" | custom-call | tf_op jit(solution)/shard_map/check/cond/branch_0_fun/while/body/eval_jaxpr/orthonormal_rows/pallas_call | solution.py:395
  199.2 7.4 %fusion.21 = f32[128,1280]{1,0:T(8,128)S(1)} fusion(bf16[2048,1280]{1,0:T(8,128)(2,1)} %get-tuple-element.124, f32[128,1280]{1,0:T(8,128)S(1)} %get-tuple-element.116), kind=kOutput, calls=%fused_computation.1.clone.1 | convolution fusion | flops 1342603264 | bytes 6553600 | tf_op jit(solution)/shard_map/check/cond/branch_0_fun/while/body/eval_jaxpr/dot_general | solution.py:409
  206.7 0.2 reshape.52
  206.8 38.1 %all_to_all.30 = f32[256,5,128]{2,1,0:T(8,128)S(1)} all-to-all(f32[256,5,128]{2,1,0:T(8,128)S(1)} %reshape.52), channel_id=1, replica_groups=mesh['x'=4,'z'=8,'c'=2,'y'=4] {'x','z','c','y'}, dimensions={0} | all-to-all | bytes 1310720 | tf_op jit(solution)/shard_map/check/cond/branch_0_fun/while/body/eval_jaxpr/all_to_all | solution.py:411
  244.9 0.3 reduce_sum.32
  245.2 1.0 broadcast_in_dim.12
  246.2 5.8 %all-to-all-start.1 = ((f32[256,5,128]{2,1,0:T(8,128)}), f32[256,5,128]{2,1,0:T(8,128)S(1)}, u32[]{:S(2)}, u32[]{:S(2)}) async-start(f32[256,5,128]{2,1,0:T(8,128)} %broadcast_in_dim.12), calls=%async_computation.1 | async-start | bytes 2097152 | tf_op jit(solution)/shard_map/check/cond/branch_0_fun/while/body/eval_jaxpr/all_to_all | solution.py:421
  252.0 32.6 %all-to-all-done.1 = f32[256,5,128]{2,1,0:T(8,128)S(1)} async-done(((f32[256,5,128]{2,1,0:T(8,128)}), f32[256,5,128]{2,1,0:T(8,128)S(1)}, u32[]{:S(2)}, u32[]{:S(2)}) %all-to-all-start.1) | async-done | bytes 655392 | tf_op jit(solution)/shard_map/check/cond/branch_0_fun/while/body/eval_jaxpr/all_to_all | solution.py:421
  284.6 0.1 broadcast_multiply_fusion.2
  284.7 0.2 div.9.zt_ref
  284.9 4.5 %orthonormal_rows.1 = (f32[128,1280]{1,0:T(8,128)S(1)}, f32[128,128]{1,0:T(8,128)}) custom-call(f32[128,1280]{1,0:T(8,128)S(1)} %div.9.zt_ref), custom_call_target="tpu_custom_call" | custom-call | tf_op jit(solution)/shard_map/check/cond/branch_0_fun/while/body/eval_jaxpr/orthonormal_rows/pallas_call | solution.py:395
  289.4 0.1 dynamic-slice_bitcast_fusion
  289.5 0.1 copy.13
  289.6 0.0 copy-start
  289.6 0.6 copy-done
  (7 shorter events, 0.1 us)
Async XLA Ops:
  9.4 6.1 %collective-permute-start.1 = (bf16[3328,128]{1,0:T(8,128)(2,1)S(1)}, bf16[3328,128]{1,0:T(8,128)(2,1)S(1)}, u32[]{:S(2)}, u32[]{:S(2)}) collective-permute-start(bf16[3328,128]{1,0:T(8,128)(2,1)S(1)} %get-tuple-element.47), channel_id=1, source_target_pairs={{0,4},{4,0},{1,5},{5,1},{2,6},{6,2},{3,7},{7,3},{8,12},{12,8},{9,1... | collective-permute-start | bytes 2555912 | tf_op jit(solution)/shard_map/over_core/ppermute | solution.py:455
  12.8 2.6 collective-permute-start
  82.7 7.7 %collective-permute-start.2 = (bf16[16,304,128]{2,1,0:T(8,128)(2,1)S(1)}, bf16[16,304,128]{2,1,0:T(8,128)(2,1)S(1)}, u32[]{:S(2)}, u32[]{:S(2)}) collective-permute-start(bf16[16,304,128]{2,1,0:T(8,128)(2,1)S(1)} %all_to_all.29.mine), channel_id=1, source_target_pairs={{0,4},{4,0},{1,5},{5,1},{2,6},{6,2},{3,7},{7,3},{8,12},{12,8},{9,1... | collective-permute-start | bytes 3735560 | tf_op jit(solution)/shard_map/back_core/ppermute | solution.py:464
  156.1 38.4 %all-to-all-start.1 = ((f32[256,5,128]{2,1,0:T(8,128)}), f32[256,5,128]{2,1,0:T(8,128)S(1)}, u32[]{:S(2)}, u32[]{:S(2)}) async-start(f32[256,5,128]{2,1,0:T(8,128)} %broadcast_in_dim.12), calls=%async_computation.1 | async-start | bytes 2097152 | tf_op jit(solution)/shard_map/check/cond/branch_0_fun/while/body/eval_jaxpr/all_to_all | solution.py:421
  246.2 38.4 %all-to-all-start.1 = ((f32[256,5,128]{2,1,0:T(8,128)}), f32[256,5,128]{2,1,0:T(8,128)S(1)}, u32[]{:S(2)}, u32[]{:S(2)}) async-start(f32[256,5,128]{2,1,0:T(8,128)} %broadcast_in_dim.12), calls=%async_computation.1 | async-start | bytes 2097152 | tf_op jit(solution)/shard_map/check/cond/branch_0_fun/while/body/eval_jaxpr/all_to_all | solution.py:421
  289.6 0.6 copy-start
